TPU v7x, 512 devices: a whole 4x4x16 slice. The times are simulated.
512 devices in a mesh: dp: 32 (over y, z_lo), seq: 16 (over z_hi, x, core).
Axes of the slice: x: 4, y: 4, z: 16 (z_hi: 2, z_lo: 8; z = z_hi * 8 + z_lo), core: 2. Of those that a mesh axis runs over, the one named last changes fastest.
Arguments:
- signal: bfloat16 [32, 2048, 768], P('dp', 'seq'), may hold values from -6 to 6
- norm_gain: float32 [768], replicated, may hold values from 0.1 to 1.9
- conv_taps: float32 [5, 768], replicated, may hold values from -3 to 3
- w_query: bfloat16 [768, 768], replicated, may hold values from -1 to 1
- w_key: bfloat16 [768, 768], replicated, may hold values from -8 to 8
- w_value: bfloat16 [768, 768], replicated, may hold values from -0.21875 to 0.21875
- cotangent: bfloat16 [32, 2048, 768], P('dp', 'seq'), may hold values from -6 to 6
Outputs:
- grad_signal: bfloat16 [32, 2048, 768], P('dp', 'seq')
- grad_taps: float32 [5, 768], replicated
- grad_gain: float32 [768], replicated
All inputs are finite; a program needn't handle non-finite values.
Results may differ from a plain program's by a relative error of at most 0.035.
Values may be sent and summed in bfloat16 or wider, within the bound.
No kernel may reach another device: no remote copies, remote signals or barrier semaphores. Data moves between devices by JAX's collectives and lax.ppermute only.
A program may use at most 128 MiB of HBM per device.

v0:
```python
import math

import jax
import jax.numpy as jnp
from jax import lax
from jax.sharding import PartitionSpec as P

HEADS = 6
HEAD_DIM = 128


EPSILON = 1e-06
GELU_ROOT = math.sqrt(2.0 / math.pi)


def padded(cells, sides, width):
    for axis, dim in sides:
        count = lax.axis_size(axis)
        ends = count - 1
        head = lax.slice_in_dim(cells, 0, width, axis=dim)
        tail = lax.slice_in_dim(cells, cells.shape[dim] - width, cells.shape[dim], axis=dim)
        cells = jnp.concatenate(
            [
                lax.ppermute(tail, axis, [(i, (i + 1) % count) for i in range(ends)]),
                cells,
                lax.ppermute(head, axis, [((i + 1) % count, i) for i in range(ends)]),
            ],
            axis=dim,
        )
    return cells


def gelu_pair(inputs):
    inner = GELU_ROOT * (inputs + 0.044715 * inputs * inputs * inputs)
    tangent = jnp.tanh(inner)
    output = 0.5 * inputs * (1.0 + tangent)
    derivative = 0.5 * (1.0 + tangent) + 0.5 * inputs * (1.0 - tangent * tangent) * GELU_ROOT * (
        1.0 + 3.0 * 0.044715 * inputs * inputs
    )
    return (output, derivative)


def back_project(grad_rows, weight):
    return lax.dot_general(
        grad_rows, weight, (((1,), (1,)), ((), ())), preferred_element_type=jnp.float32
    )


def shards(signal, norm_gain, conv_taps, w_query, w_key, w_value, cotangent):
    score_scale = 1.0 / math.sqrt(HEAD_DIM)
    tap_count = conv_taps.shape[0]
    margin = tap_count // 2
    local_bins = signal[0]
    shard_rows = local_bins.shape[0]
    head_count = HEADS
    head_size = HEAD_DIM
    extended = padded(local_bins, (("seq", 0),), margin)
    wide_ext = extended.astype(jnp.float32)
    inv_rms_ext = lax.rsqrt(jnp.mean(wide_ext * wide_ext, axis=-1, keepdims=True) + EPSILON)
    normed_ext = wide_ext * inv_rms_ext * norm_gain
    conv_out = jnp.zeros((shard_rows, normed_ext.shape[1]), jnp.float32)
    for offset in range(tap_count):
        conv_out = conv_out + conv_taps[offset] * normed_ext[offset : offset + shard_rows]
    active, gelu_slope = gelu_pair(conv_out)
    wide_in = wide_ext[margin : margin + shard_rows]
    inv_rms = inv_rms_ext[margin : margin + shard_rows]
    hidden = (wide_in + active).astype(jnp.bfloat16)
    queries = jnp.dot(hidden, w_query, preferred_element_type=jnp.float32).astype(jnp.bfloat16)
    keys_local = jnp.dot(hidden, w_key, preferred_element_type=jnp.float32).astype(jnp.bfloat16)
    values_local = jnp.dot(hidden, w_value, preferred_element_type=jnp.float32).astype(jnp.bfloat16)
    keys_all, values_all = (
        lax.all_gather(keys_local, "seq", axis=0, tiled=True),
        lax.all_gather(values_local, "seq", axis=0, tiled=True),
    )
    total_rows = keys_all.shape[0]
    query_heads = queries.reshape(shard_rows, head_count, head_size)
    key_heads = keys_all.reshape(total_rows, head_count, head_size)
    value_heads = values_all.reshape(total_rows, head_count, head_size)
    scores = (
        jnp.einsum("qhd,khd->hqk", query_heads, key_heads, preferred_element_type=jnp.float32)
        * score_scale
    )
    row_max = jnp.max(scores, axis=-1, keepdims=True)
    exp_scores = jnp.exp(scores - row_max)
    row_total = jnp.sum(exp_scores, axis=-1, keepdims=True)
    weights = (exp_scores / row_total).astype(jnp.bfloat16)
    attended = jnp.einsum(
        "hqk,khd->qhd", weights, value_heads, preferred_element_type=jnp.float32
    ).astype(jnp.bfloat16)
    log_total = (row_max + jnp.log(row_total))[..., 0]
    grad_rows = cotangent[0]
    grad_heads = grad_rows.reshape(shard_rows, head_count, head_size)
    row_delta = jnp.sum(grad_heads.astype(jnp.float32) * attended.astype(jnp.float32), axis=-1)
    probs = jnp.exp(scores - log_total[..., None])
    dprob = jnp.einsum("qhd,khd->hqk", grad_heads, value_heads, preferred_element_type=jnp.float32)
    dscore = (probs * (dprob - row_delta.T[:, :, None])).astype(jnp.bfloat16)
    grad_query = (
        jnp.einsum("hqk,khd->qhd", dscore, key_heads, preferred_element_type=jnp.float32)
        * score_scale
    ).astype(jnp.bfloat16)
    totals_all, deltas_all = (
        lax.all_gather(log_total.T, "seq", axis=0, tiled=True),
        lax.all_gather(row_delta, "seq", axis=0, tiled=True),
    )
    key_local_heads = keys_local.reshape(shard_rows, head_count, head_size)
    value_local_heads = values_local.reshape(shard_rows, head_count, head_size)
    query_piece = lax.all_gather(queries, "seq", axis=0, tiled=True)
    grad_piece = lax.all_gather(grad_rows, "seq", axis=0, tiled=True)
    piece_rows = query_piece.shape[0]
    block_count = piece_rows // shard_rows
    query_blocks = query_piece.reshape(block_count, shard_rows, head_count, head_size)
    grad_blocks = grad_piece.reshape(block_count, shard_rows, head_count, head_size)
    total_blocks = totals_all.reshape(block_count, shard_rows, head_count).transpose(0, 2, 1)
    delta_blocks = deltas_all.reshape(block_count, shard_rows, head_count).transpose(0, 2, 1)
    block_scores = (
        jnp.einsum(
            "bqhd,khd->bhqk", query_blocks, key_local_heads, preferred_element_type=jnp.float32
        )
        * score_scale
    )
    block_probs = jnp.exp(block_scores - total_blocks[..., None])
    value_parts = jnp.einsum(
        "bhqk,bqhd->bkhd",
        block_probs.astype(jnp.bfloat16),
        grad_blocks,
        preferred_element_type=jnp.float32,
    ).astype(jnp.bfloat16)
    block_dprob = jnp.einsum(
        "bqhd,khd->bhqk", grad_blocks, value_local_heads, preferred_element_type=jnp.float32
    )
    block_dscore = (block_probs * (block_dprob - delta_blocks[..., None])).astype(jnp.bfloat16)
    key_parts = (
        jnp.einsum(
            "bhqk,bqhd->bkhd", block_dscore, query_blocks, preferred_element_type=jnp.float32
        )
        * score_scale
    ).astype(jnp.bfloat16)
    key_sum = jnp.sum(key_parts.astype(jnp.float32), axis=0)
    value_sum = jnp.sum(value_parts.astype(jnp.float32), axis=0)
    grad_key = key_sum.astype(jnp.bfloat16).reshape(shard_rows, head_count * head_size)
    grad_value = value_sum.astype(jnp.bfloat16).reshape(shard_rows, head_count * head_size)
    grad_hidden = back_project(grad_query.reshape(shard_rows, head_count * head_size), w_query)
    grad_hidden = grad_hidden + back_project(grad_key, w_key)
    grad_hidden = grad_hidden + back_project(grad_value, w_value)
    grad_conv = grad_hidden * gelu_slope
    grad_ext = padded(grad_conv, (("seq", 0),), margin)
    tap_rows = []
    grad_normed = jnp.zeros_like(grad_conv)
    for offset in range(tap_count):
        tap_rows.append(jnp.sum(grad_conv * normed_ext[offset : offset + shard_rows], axis=0))
        start_at = 2 * margin - offset
        grad_normed = grad_normed + conv_taps[offset] * grad_ext[start_at : start_at + shard_rows]
    taps_local = jnp.stack(tap_rows)
    gain_local = jnp.sum(grad_normed * wide_in * inv_rms, axis=0)
    grad_taps, grad_gain = lax.psum((taps_local, gain_local), ("dp", "seq"))
    scaled = grad_normed * norm_gain
    grad_signal = (
        grad_hidden
        + inv_rms * scaled
        - wide_in * inv_rms * inv_rms * inv_rms * jnp.mean(scaled * wide_in, axis=-1, keepdims=True)
    )
    return (grad_signal.astype(jnp.bfloat16)[None], grad_taps, grad_gain)


def solution(mesh):
    in_specs = (P("dp", "seq", None), P(), P(), P(), P(), P(), P("dp", "seq", None))
    out_specs = (P("dp", "seq", None), P(), P())
    return jax.shard_map(shards, mesh=mesh, in_specs=in_specs, out_specs=out_specs, check_vma=False)
```

profile of v0, /device:TPU:7, one launch (start us, length us, event | category | flops | bytes accessed | tf_op | source)
XLA Modules:
  0.0 577.7 jit_solution(18349334429816625755)
XLA Ops:
  8.7 2.6 collective-permute-start.1
  11.3 15.3 %collective-permute-start = (bf16[2,768]{1,0:T(2,128)(2,1)S(1)}, bf16[2,768]{1,0:T(2,128)(2,1)S(1)}, u32[]{:S(2)}, u32[]{:S(2)}) collective-permute-start(bf16[2,768]{1,0:T(2,128)(2,1)S(1)} %get-tuple-element.23), channel_id=1, source_target_pairs={{0,1},{1,2},{2,3},{3,4},{4,5},{5,6},{6,7},{7,8},{8,9},{9,10},{10,1... | collective-permute-start | bytes 9224 | tf_op jit(solution)/shard_map/ppermute | solution.py:24
  32.9 2.3 convolution_convert_fusion
  42.6 79.9 %all-gather.12.cloned.1.call-done = bf16[1,2048,768]{2,1,0:T(8,128)(2,1)} async-done(((bf16[1,128,768]{2,1,0:T(8,128)(2,1)}), bf16[1,2048,768]{2,1,0:T(8,128)(2,1)}) %all-gather.12.cloned.1.call-update) | async-done | bytes 3145744 | tf_op jit(solution)/shard_map/all_gather | solution.py:108
  122.5 4.7 copy.50
  127.2 4.5 copy.73
  131.8 92.6 %all-gather.6.cloned.1.call-done = bf16[2048,768]{1,0:T(8,128)(2,1)} async-done(((bf16[128,768]{1,0:T(8,128)(2,1)}), bf16[2048,768]{1,0:T(8,128)(2,1)}) %all-gather.6.cloned.1.call-update) | async-done | bytes 3145744 | tf_op jit(solution)/shard_map/all_gather | solution.py:72
  224.4 4.7 copy.36
  229.1 3.1 multiply_reduce_fusion
  234.9 33.0 %all_gather.21 = f32[2048,6]{0,1:T(8,128)S(1)} all-gather(f32[128,6]{0,1:T(8,128)S(1)} %bitcast.137), channel_id=1, replica_groups=mesh['dp'=32,'seq'=16] {'seq'}, dimensions={0}, use_global_device_ids=true | all-gather | bytes 52224 | tf_op jit(solution)/shard_map/all_gather | solution.py:102
  268.0 58.1 %all-gather.8.cloned.1.call-done = bf16[2048,768]{1,0:T(8,128)(2,1)} async-done(((bf16[128,768]{1,0:T(8,128)(2,1)}), bf16[2048,768]{1,0:T(8,128)(2,1)}) %all-gather.8.cloned.1.call-update) | async-done | bytes 3145744 | tf_op jit(solution)/shard_map/all_gather | solution.py:73
  326.0 4.7 copy.40
  330.8 5.4 fusion.35
  336.2 33.3 %all_gather.23 = f32[2048,6]{0,1:T(8,128)S(1)} all-gather(f32[128,6]{0,1:T(8,128)S(1)} %fusion.35), channel_id=1, replica_groups=mesh['dp'=32,'seq'=16] {'seq'}, dimensions={0}, use_global_device_ids=true | all-gather | bytes 52224 | tf_op jit(solution)/shard_map/all_gather | solution.py:103
  369.4 8.5 %fusion.34 = bf16[6,128,128]{2,1,0:T(8,128)(2,1)} fusion(bf16[2048,6,128]{0,2,1:T(8,128)(2,1)} %bitcast.115, f32[6,128,2048]{2,1,0:T(8,128)} %copy-done.1, bf16[2048,6,128]{0,2,1:T(8,128)(2,1)} %bitcast.119, bf16[128,6,128]{0,2,1:T(8,128)(2,1)} %bitcast.135, f32[6,128]{1,0:T(8,128)S(1)} %bitcast.138, f32[6,128]{1,0:T(8,128)S(1)} %log_add_fusion), kind=kOutput, calls=%fused_computation.34 | convolution fusion | flops 813367296 | bytes 12982272 | tf_op jit(solution)/shard_map/hqk,khd->qhd/dot_general | solution.py:98
  380.1 47.4 %all-gather.10.cloned.1.call-done = bf16[2048,768]{1,0:T(8,128)(2,1)} async-done(((bf16[128,768]{1,0:T(8,128)(2,1)}), bf16[2048,768]{1,0:T(8,128)(2,1)}) %all-gather.10.cloned.1.call-update) | async-done | bytes 3145744 | tf_op jit(solution)/shard_map/all_gather | solution.py:107
  427.5 4.8 copy.45
  432.3 2.9 copy.71
  437.4 2.4 fusion.1
  439.8 3.4 fusion.6
  443.1 3.0 convert_reduce_fusion
  453.2 2.4 collective-permute-start.2
  455.8 13.2 %collective-permute-done.2 = f32[2,768]{1,0:T(2,128)S(1)} collective-permute-done((f32[2,768]{1,0:T(2,128)S(1)}, f32[2,768]{1,0:T(2,128)S(1)}, u32[]{:S(2)}, u32[]{:S(2)}) %collective-permute-start.2) | collective-permute-done | bytes 6176 | tf_op jit(solution)/shard_map/ppermute | solution.py:26
  470.3 100.9 %all-reduce = (f32[5,768]{1,0:T(8,128)}, f32[768]{0:T(1024)}) all-reduce(f32[5,768]{1,0:T(8,128)S(1)} %stack.23, f32[768]{0:T(1024)S(1)} %get-tuple-element.3), channel_id=1, replica_groups=mesh['dp'=32,'seq'=16] {'dp','seq'}, use_global_device_ids=true, to_apply=%region_12.0 | all-reduce | flops 4608 | bytes 36864 | tf_op jit(solution)/shard_map/psum | solution.py:155
  (60 shorter events, 30.6 us)
Async XLA Ops:
  7.2 28.1 %copy-start = (bf16[768,768]{1,0:T(8,128)(2,1)S(1)}, bf16[768,768]{1,0:T(8,128)(2,1)}, u32[]{:S(2)}) copy-start(bf16[768,768]{1,0:T(8,128)(2,1)} %param.10) | copy-start | bytes 3538948
  7.2 24.6 %copy-start.3 = (bf16[768,768]{1,0:T(8,128)(2,1)S(1)}, bf16[768,768]{1,0:T(8,128)(2,1)}, u32[]{:S(2)}) copy-start(bf16[768,768]{1,0:T(8,128)(2,1)} %param.11) | copy-start | bytes 3538948
  7.2 115.3 %all-gather.12.cloned.1.call-start = ((), (), s32[]{:S(2)}) async-start(), calls=%async_computation.3 | async-start | bytes 3342336 | tf_op jit(solution)/shard_map/all_gather | solution.py:108
  7.9 216.5 %all-gather.6.cloned.1.call-start = ((), (), s32[]{:S(2)}) async-start(), calls=%async_computation | async-start | bytes 3342336 | tf_op jit(solution)/shard_map/all_gather | solution.py:72
  8.7 18.8 %collective-permute-start.1 = (bf16[2,768]{1,0:T(2,128)(2,1)S(1)}, bf16[2,768]{1,0:T(2,128)(2,1)S(1)}, u32[]{:S(2)}, u32[]{:S(2)}) collective-permute-start(bf16[2,768]{1,0:T(2,128)(2,1)S(1)} %get-tuple-element.24), channel_id=1, source_target_pairs={{1,0},{2,1},{3,2},{4,3},{5,4},{6,5},{7,6},{8,7},{9,8},{10,9},{11,1... | collective-permute-start | bytes 9224 | tf_op jit(solution)/shard_map/ppermute | solution.py:26
  11.3 16.2 %collective-permute-start = (bf16[2,768]{1,0:T(2,128)(2,1)S(1)}, bf16[2,768]{1,0:T(2,128)(2,1)S(1)}, u32[]{:S(2)}, u32[]{:S(2)}) collective-permute-start(bf16[2,768]{1,0:T(2,128)(2,1)S(1)} %get-tuple-element.23), channel_id=1, source_target_pairs={{0,1},{1,2},{2,3},{3,4},{4,5},{5,6},{6,7},{7,8},{8,9},{9,10},{10,1... | collective-permute-start | bytes 9224 | tf_op jit(solution)/shard_map/ppermute | solution.py:24
  32.8 293.2 %all-gather.8.cloned.1.call-start = ((), (), s32[]{:S(2)}) async-start(), calls=%async_computation.1 | async-start | bytes 3342336 | tf_op jit(solution)/shard_map/all_gather | solution.py:73
  35.2 392.3 %all-gather.10.cloned.1.call-start = ((), (), s32[]{:S(2)}) async-start(), calls=%async_computation.2 | async-start | bytes 3342336 | tf_op jit(solution)/shard_map/all_gather | solution.py:107
  232.2 2.7 copy-start.1
  432.3 3.0 copy-start.5
  435.3 2.1 copy-start.2
  447.2 3.5 copy-start.4
  448.9 20.1 %copy-start.6 = (f32[768]{0:T(1024)S(1)}, f32[768]{0:T(1024)}, u32[]{:S(2)}) copy-start(f32[768]{0:T(1024)} %param.8) | copy-start | bytes 9220
  451.3 4.5 collective-permute-start.3
  453.2 15.8 %collective-permute-start.2 = (f32[2,768]{1,0:T(2,128)S(1)}, f32[2,768]{1,0:T(2,128)S(1)}, u32[]{:S(2)}, u32[]{:S(2)}) collective-permute-start(f32[2,768]{1,0:T(2,128)S(1)} %get-tuple-element.21), channel_id=1, source_target_pairs={{1,0},{2,1},{3,2},{4,3},{5,4},{6,5},{7,6},{8,7},{9,8},{10,9},{11,1... | collective-permute-start | bytes 18440 | tf_op jit(solution)/shard_map/ppermute | solution.py:26
Sparse Core Ops, SparseCore 0:
  11.3 111.1 all-gather.11
  126.4 97.9 all-gather.5
  227.7 98.2 all-gather.7
  329.2 98.2 all-gather.9
where the time goes:
time: 582 us; the launch traced here: 578 us
  waiting for transfers between devices  292 us (50%)
  blocking collectives  167 us (29%)
  matrix products  37.9 us (7%)
  local copies, waits for them, and re-layouts  37.2 us (6%)
  starting transfers between devices  22.3 us (4%)
  between operations  14 us (2%)
  other arithmetic  7.2 us (1%)
    psum x1, blocking collectives, shards(): grad_taps, grad_gain = lax.psum((taps_local, gain_local), ('dp', 'seq'))  101 us
    all_gather x1, waiting for transfers between devices, shards(): lax.all_gather(keys_local, 'seq', axis=0, tiled=True)  92.6 us
    all_gather x1, waiting for transfers between devices, shards(): grad_piece = lax.all_gather(grad_rows, 'seq', axis=0, tiled=True)  79.9 us
    all_gather x1, waiting for transfers between devices, shards(): lax.all_gather(values_local, 'seq', axis=0, tiled=True)  58.1 us
    all_gather x1, waiting for transfers between devices, shards(): query_piece = lax.all_gather(queries, 'seq', axis=0, tiled=True)  47.4 us
    all_gather x1, blocking collectives, shards(): lax.all_gather(row_delta, 'seq', axis=0, tiled=True)  33.3 us
    all_gather x1, blocking collectives, shards(): lax.all_gather(log_total.T, 'seq', axis=0, tiled=True)  33 us
    ppermute x2, starting transfers between devices, padded(): lax.ppermute(tail, axis, [(i, (i + 1) % count) for i in range(ends)])  17.2 us
  transfers between devices with their start and end apart: 8, of which 5 were waited for; matrix products, arithmetic and copies ran while one was open for 10% of the time, Pallas kernels for 0%

commit v1 on v0

v1 whole, which is shorter than its diff:
```python
import math

import jax
import jax.numpy as jnp
from jax import lax
from jax.experimental import pallas as pl
from jax.experimental.pallas import tpu as pltpu
from jax.sharding import Mesh
from jax.sharding import PartitionSpec as P

HEADS = 6
HEAD_DIM = 128
OWN_HEADS = 3
HALF = OWN_HEADS * HEAD_DIM
EPSILON = 1e-06
GELU_ROOT = math.sqrt(2.0 / math.pi)
SCALE = 1.0 / math.sqrt(HEAD_DIM)
BLOCK = 128
CHUNK = 256
CHUNKS = 8
BINS = 2048
C = 768
INTERPRET = False
F32 = jnp.float32
BF16 = jnp.bfloat16
VM = pltpu.VMEM


def vspec():
    return pl.BlockSpec(memory_space=pltpu.VMEM)


def sspec():
    return pl.BlockSpec(memory_space=pltpu.SMEM)


def call(body, out_shape, args, scratch=(), limit=40):
    specs = [sspec() if a.dtype == jnp.int32 else vspec() for a in args]
    outs = jax.tree.map(lambda _: vspec(), out_shape)
    return pl.pallas_call(
        body,
        out_shape=out_shape,
        in_specs=specs,
        out_specs=outs,
        scratch_shapes=list(scratch),
        compiler_params=pltpu.CompilerParams(vmem_limit_bytes=limit << 20),
        interpret=INTERPRET,
    )(*args)


def nt(a, b):
    return lax.dot_general(a, b, (((1,), (1,)), ((), ())), preferred_element_type=F32)


def nn(a, b):
    return lax.dot_general(a, b, (((1,), (0,)), ((), ())), preferred_element_type=F32)


def neighbours(pos, dz, dx):
    zh = pos[0]
    xa = lax.rem(pos[1] + dx, 4)
    za = lax.rem(zh + dz, 2)
    wrap_lo = (xa == 0).astype(jnp.int32)
    wrap_hi = (xa == 3).astype(jnp.int32)
    prev = lax.rem(dz + wrap_lo, 2) * 4 + lax.rem(dx + 3, 4)
    nxt = lax.rem(dz + wrap_hi, 2) * 4 + lax.rem(dx + 1, 4)
    prev_ok = 1 - wrap_lo * (1 - za)
    nxt_ok = 1 - wrap_hi * za
    return prev, nxt, prev_ok.astype(F32), nxt_ok.astype(F32)


def normalize(rows):
    return rows * lax.rsqrt(jnp.mean(rows * rows, axis=-1, keepdims=True) + EPSILON)


def hidden_body(
    pos, s0, s1, s2, s3, s4, s5, s6, s7, e0, e1, w, gain, taps, q, k, v, ext, xs, ns, hs
):
    core = pos[2]
    here = pl.multiple_of(core * BLOCK, BLOCK)
    there = pl.multiple_of((1 - core) * BLOCK, BLOCK)
    for c, s in enumerate((s0, s1, s2, s3, s4, s5, s6, s7)):
        other = e0 if c < 4 else e1
        xs[c, pl.ds(here, BLOCK), :] = s[0:BLOCK, :]
        xs[c, pl.ds(there, BLOCK), :] = other[(c % 4) * BLOCK : (c % 4 + 1) * BLOCK, :]
    prev, nxt, prev_ok, nxt_ok = neighbours(pos, jnp.int32(0), jnp.int32(0))
    first = core == 0
    ext[16:144, :] = s0[0:BLOCK, :]

    @pl.when(first)
    def _():
        ext[0:16, :] = (xs[prev, 240:256, :].astype(F32) * prev_ok).astype(BF16)
        ext[144:160, :] = xs[0, 128:144, :]

    @pl.when(jnp.logical_not(first))
    def _():
        ext[0:16, :] = xs[0, 112:128, :]
        ext[144:160, :] = (xs[nxt, 0:16, :].astype(F32) * nxt_ok).astype(BF16)

    def chunk(c, _):
        dz = lax.div(c, 4)
        dx = lax.rem(c, 4)
        prev, nxt, prev_ok, nxt_ok = neighbours(pos, dz, dx)
        g = gain[0:1, :]
        ns[0:16, :] = normalize(xs[prev, 240:256, :].astype(F32)) * g * prev_ok
        ns[272:288, :] = normalize(xs[nxt, 0:16, :].astype(F32)) * g * nxt_ok
        for r in range(0, CHUNK, 16):
            ns[16 + r : 32 + r, :] = normalize(xs[c, r : r + 16, :].astype(F32)) * g
        for j in range(0, C, 128):
            tap = [taps[t : t + 1, j : j + 128] for t in range(5)]
            for r in range(0, CHUNK, 64):
                u = tap[0] * ns[14 + r : 78 + r, j : j + 128]
                for t in range(1, 5):
                    u = u + tap[t] * ns[14 + r + t : 78 + r + t, j : j + 128]
                inner = GELU_ROOT * (u + 0.044715 * u * u * u)
                act = 0.5 * u * (1.0 + jnp.tanh(inner))
                x = xs[c, r : r + 64, j : j + 128].astype(F32)
                hs[r : r + 64, j : j + 128] = (x + act).astype(BF16)
        y = nn(hs[...], w[...]).astype(BF16)
        at = pl.multiple_of(c * CHUNK, CHUNK)
        for h in range(OWN_HEADS):
            q[h, pl.ds(at, CHUNK), :] = y[:, h * 128 : (h + 1) * 128]
            k[h, pl.ds(at, CHUNK), :] = y[:, HALF + h * 128 : HALF + (h + 1) * 128]
            v[h, pl.ds(at, CHUNK), :] = y[:, 2 * HALF + h * 128 : 2 * HALF + (h + 1) * 128]
        return 0

    lax.fori_loop(0, CHUNKS, chunk, 0)


KB = 512


def forward_body(q, k, v, d0, d4, dq, stats, ds, ss, sm):
    for g, d in enumerate((d0, d4)):
        for h in range(OWN_HEADS):
            ds[h, g * CHUNK : g * CHUNK + BLOCK, :] = d[0:BLOCK, h * 128 : (h + 1) * 128]
            ds[h, g * CHUNK + BLOCK : (g + 1) * CHUNK, :] = d[
                0:BLOCK, HALF + h * 128 : HALF + (h + 1) * 128
            ]
    sm[...] = jnp.zeros_like(sm)
    lane = lax.broadcasted_iota(jnp.int32, (CHUNK, 128), 1)

    def head(h, _):
        for g in range(2):
            qh = q[h, g * 1024 : g * 1024 + CHUNK, :]
            top = None
            for b in range(0, BINS, KB):
                s = nt(qh, k[h, b : b + KB, :])
                ss[:, b : b + KB] = s
                m = jnp.max(s, axis=1, keepdims=True)
                top = m if top is None else jnp.maximum(top, m)
            total = jnp.zeros((CHUNK, 1), F32)
            out = jnp.zeros((CHUNK, HEAD_DIM), F32)
            for b in range(0, BINS, KB):
                p = jnp.exp((ss[:, b : b + KB] - top) * SCALE)
                total = total + jnp.sum(p, axis=1, keepdims=True)
                out = out + nn(p.astype(BF16), v[h, b : b + KB, :])
                if g == 0:
                    ss[:, b : b + KB] = p
            inverse = 1.0 / total
            attended = (out * inverse).astype(BF16).astype(F32)
            do = ds[h, g * CHUNK : (g + 1) * CHUNK, :]
            delta = jnp.sum(do.astype(F32) * attended, axis=1, keepdims=True)
            log_total = top * SCALE + jnp.log(total)
            sl = slice(g * CHUNK, (g + 1) * CHUNK)
            sm[sl, :] = jnp.where(
                lane == h, log_total, jnp.where(lane == h + OWN_HEADS, delta, sm[sl, :])
            )
            if g == 0:
                acc = jnp.zeros((CHUNK, HEAD_DIM), F32)
                for b in range(0, BINS, KB):
                    dp = nt(do, v[h, b : b + KB, :])
                    dsc = (ss[:, b : b + KB] * inverse * (dp - delta)).astype(BF16)
                    acc = acc + nn(dsc, k[h, b : b + KB, :])
                dq[h, :, :] = (acc * SCALE).astype(BF16)
        return 0

    lax.fori_loop(0, OWN_HEADS, head, 0)
    stats[...] = jnp.transpose(sm[...])[0:8, :]


def backward_body(pos, q, k, v, d0, d1, d2, d3, d4, d5, d6, d7, stats, dk, dv, ds):
    for c, d in enumerate((d0, d1, d2, d3, d4, d5, d6, d7)):
        low = BLOCK if c in (1, 2, 3) else 0
        for h in range(OWN_HEADS):
            ds[h, c * CHUNK : c * CHUNK + BLOCK, :] = d[
                low : low + BLOCK, h * 128 : (h + 1) * 128
            ]
            ds[h, c * CHUNK + BLOCK : (c + 1) * CHUNK, :] = d[
                low : low + BLOCK, HALF + h * 128 : HALF + (h + 1) * 128
            ]
    for h in range(OWN_HEADS):
        kh = k[h, 0:CHUNK, :]
        vh = v[h, 0:CHUNK, :]

        def step(dx, carry):
            acc_k, acc_v = carry
            xa = lax.rem(pos[1] + dx, 4)
            for dz in range(2):
                at = pl.multiple_of(dz * 1024 + dx * CHUNK, CHUNK)
                qc = q[h, pl.ds(at, CHUNK), :]
                dc = ds[h, pl.ds(at, CHUNK), :]
                log_total = stats[xa, h : h + 1, dz * CHUNK : (dz + 1) * CHUNK]
                delta = stats[xa, h + OWN_HEADS : h + OWN_HEADS + 1, dz * CHUNK : (dz + 1) * CHUNK]
                p = jnp.exp(nt(kh, qc) * SCALE - log_total)
                acc_v = acc_v + nn(p.astype(BF16), dc)
                dsc = (p * (nt(vh, dc) - delta)).astype(BF16)
                acc_k = acc_k + nn(dsc, qc)
            return acc_k, acc_v

        zero = jnp.zeros((CHUNK, HEAD_DIM), F32)
        acc_k, acc_v = lax.fori_loop(0, 4, step, (zero, zero))
        dk[h, :, :] = (acc_k * SCALE).astype(BF16)
        dv[h, :, :] = acc_v.astype(BF16)


def conv_body(mine, recv, w_own, w_oth, ext, gain, taps, gh, gc, usum, ns):
    g = gain[0:1, :]
    for r in range(0, 160, 16):
        ns[r : r + 16, :] = normalize(ext[r : r + 16, :].astype(F32))
    gh[...] = nt(mine[...], w_own[...]) + nt(recv[...], w_oth[...])
    for j in range(0, C, 128):
        tap = [taps[t : t + 1, j : j + 128] for t in range(5)]
        sums = [jnp.zeros((8, 128), F32) for _ in range(5)]
        gj = g[:, j : j + 128]
        for r in range(0, BLOCK, 64):
            near = [ns[14 + r + t : 78 + r + t, j : j + 128] for t in range(5)]
            u = tap[0] * (near[0] * gj)
            for t in range(1, 5):
                u = u + tap[t] * (near[t] * gj)
            inner = GELU_ROOT * (u + 0.044715 * u * u * u)
            th = jnp.tanh(inner)
            slope = 0.5 * (1.0 + th) + 0.5 * u * (1.0 - th * th) * GELU_ROOT * (
                1.0 + 3.0 * 0.044715 * u * u
            )
            gcv = gh[r : r + 64, j : j + 128] * slope
            gc[r : r + 64, j : j + 128] = gcv
            for t in range(5):
                sums[t] = sums[t] + jnp.sum((gcv * near[t]).reshape(8, 8, 128), axis=0)
        for t in range(5):
            usum[t : t + 1, j : j + 128] = jnp.sum(sums[t], axis=0, keepdims=True)
        usum[5:8, j : j + 128] = jnp.zeros((3, 128), F32)


def final_body(gh, gc, before, after, ext, gain, taps, out, es):
    es[0:8, :] = before[...]
    es[8:136, :] = gc[...]
    es[136:144, :] = after[...]
    g = gain[0:1, :]
    tap = [taps[t : t + 1, :] for t in range(5)]
    for r in range(0, BLOCK, 16):
        gn = tap[0] * es[10 + r : 26 + r, :]
        for t in range(1, 5):
            gn = gn + tap[t] * es[10 + r - t : 26 + r - t, :]
        x = ext[16 + r : 32 + r, :].astype(F32)
        inv = lax.rsqrt(jnp.mean(x * x, axis=-1, keepdims=True) + EPSILON)
        scaled = gn * g
        inner = jnp.mean(scaled * x, axis=-1, keepdims=True)
        res = gh[r : r + 16, :] + inv * scaled - x * (inv * inv * inv * inner)
        out[r : r + 16, :] = res.astype(BF16)


AXES = ("y", "zm", "zl", "zh", "x", "core")


def swap(a, axis):
    return lax.ppermute(a, axis, [(0, 1), (1, 0)])


def from_x(a, step):
    return lax.ppermute(a, "x", [((i + step) % 4, i) for i in range(4)])


def share(a, axes, size):
    wide = jnp.broadcast_to(a[None], (size,) + a.shape)
    return lax.all_to_all(wide, axes, 0, 0)


def shards(signal, norm_gain, conv_taps, w_query, w_key, w_value, cotangent):
    zh = lax.axis_index("zh")
    xi = lax.axis_index("x")
    core = lax.axis_index("core")
    pos = jnp.stack([zh, xi, core]).astype(jnp.int32)
    first = core == 0
    sig = signal[0]
    cot = cotangent[0]
    gain = norm_gain.reshape(1, C)

    def halves(a):
        low, high = a[:, :HALF], a[:, HALF:]
        return jnp.where(first, low, high), jnp.where(first, high, low)

    sig_z = swap(sig, "zh")
    keep, give = halves(cot)
    got = swap(give, "core")
    cot_own = jnp.concatenate(
        [jnp.where(first, keep, got), jnp.where(first, got, keep)], axis=1
    )
    cot_z = swap(cot_own, "zh")
    both = jnp.concatenate([sig, cot_own], axis=0)
    near = [from_x(both, d) for d in (1, 2, 3)]
    far = [from_x(sig_z, d) for d in (1, 2, 3)]
    e0 = swap(jnp.concatenate([sig] + [n[:BLOCK] for n in near], axis=0), "core")
    e1 = swap(jnp.concatenate([sig_z] + far, axis=0), "core")
    cot_far = [from_x(cot_z, d) for d in (1, 2, 3)]

    parts = [halves(w) for w in (w_query, w_key, w_value)]
    w_own = jnp.concatenate([p[0] for p in parts], axis=1)
    w_oth = jnp.concatenate([p[1] for p in parts], axis=1)

    head_shape = jax.ShapeDtypeStruct((OWN_HEADS, BINS, HEAD_DIM), BF16)
    q, k, v, ext = call(
        hidden_body,
        (head_shape, head_shape, head_shape, jax.ShapeDtypeStruct((160, C), BF16)),
        (pos, sig, *near, sig_z, *far, e0, e1, w_own, gain, conv_taps),
        (VM((CHUNKS, CHUNK, C), BF16), VM((288, C), F32), VM((CHUNK, C), BF16)),
    )
    part = jax.ShapeDtypeStruct((OWN_HEADS, CHUNK, HEAD_DIM), BF16)
    dq, stats = call(
        forward_body,
        (part, jax.ShapeDtypeStruct((8, 2 * CHUNK), F32)),
        (q, k, v, cot_own, cot_z),
        (
            VM((OWN_HEADS, 2 * CHUNK, HEAD_DIM), BF16),
            VM((CHUNK, BINS), F32),
            VM((2 * CHUNK, 128), F32),
        ),
    )
    stats_all = share(stats, "x", 4)
    dk, dv = call(
        backward_body,
        (part, part),
        (pos, q, k, v, cot_own, *near, cot_z, *cot_far, stats_all),
        (VM((OWN_HEADS, BINS, HEAD_DIM), BF16),),
    )
    grads = jnp.concatenate([dq[h] for h in range(3)] + [dk[h] for h in range(3)] + [dv[h] for h in range(3)], axis=1)
    mine = jnp.where(first, grads[:BLOCK], grads[BLOCK:])
    give = jnp.where(first, grads[BLOCK:], grads[:BLOCK])
    recv = swap(give, "core")
    wide = jax.ShapeDtypeStruct((BLOCK, C), F32)
    gh, gc, usum = call(
        conv_body,
        (wide, wide, jax.ShapeDtypeStruct((8, C), F32)),
        (mine, recv, w_own, w_oth, ext, gain, conv_taps),
        (VM((160, C), F32),),
    )
    ring = ("zh", "x", "core")
    before = lax.ppermute(gc[BLOCK - 8 :], ring, [(i, i + 1) for i in range(15)])
    after = lax.ppermute(gc[:8], ring, [(i + 1, i) for i in range(15)])
    out = call(
        final_body,
        jax.ShapeDtypeStruct((BLOCK, C), BF16),
        (gh, gc, before, after, ext, gain, conv_taps),
        (VM((144, C), F32),),
    )
    usum = usum + swap(usum, "core")
    usum = jnp.sum(share(usum, ("y", "x"), 16), axis=0)
    usum = jnp.sum(share(usum, ("zl",), 4), axis=0)
    usum = jnp.sum(share(usum, ("zm", "zh"), 4), axis=0)[:5]
    grad_taps = usum * gain
    grad_gain = jnp.sum(usum * conv_taps, axis=0)
    return out[None], grad_taps, grad_gain


def solution(mesh):
    shape = (mesh.devices.size // 128, 2, 4, 2, 4, 2)
    fine = Mesh(mesh.devices.reshape(shape), AXES)
    rows = P(("y", "zm", "zl"), ("zh", "x", "core"), None)
    in_specs = (rows, P(), P(), P(), P(), P(), rows)
    out_specs = (rows, P(), P())
    return jax.shard_map(shards, mesh=fine, in_specs=in_specs, out_specs=out_specs, check_vma=False)
```

time: 582 us -> 258 us (0.44)
  waiting for transfers between devices: 292 us -> 34.1 us
  blocking collectives: 167 us -> 32.5 us
  starting transfers between devices: 22.3 us -> 111 us
  matrix products: 37.9 us -> 0 us
  Pallas kernels: 0 us -> 37.2 us
  between operations: 14 us -> 1.19 us
  local copies, waits for them, and re-layouts: 37.2 us -> 29.1 us
    all_gather x4 -> x0, waiting for transfers between devices: 278 us -> none  [the longest x1 92.6 us: shards(): lax.all_gather(keys_local, 'seq', axis=0, tiled=True)]
    psum x1 -> x0, blocking collectives: 101 us -> none  [shards(): grad_taps, grad_gain = lax.psum((taps_local, gain_local), ('dp', 'seq'))]
    ppermute x4 -> x18, starting transfers between devices: 22.2 us -> 91.8 us  [the longest x7 42.7 us: swap(): return lax.ppermute(a, axis, [(0, 1), (1, 0)])]
    all_gather x2 -> x0, blocking collectives: 66.3 us -> none  [the longest x1 33.3 us: shards(): lax.all_gather(row_delta, 'seq', axis=0, tiled=True)]
    dot_general x13 -> x0, matrix products: 37.9 us -> none  [the longest x1 8.47 us: shards(): jnp.einsum('hqk,khd->qhd', dscore, key_heads, preferred_element_type=jnp....]
    pallas_call x0 -> x5, Pallas kernels: none -> 37.2 us  [call(): pl.pallas_call(body, out_shape=out_shape, in_specs=specs, out_specs=outs,...]
    all_to_all x0 -> x2, blocking collectives: none -> 32.5 us  [share(): return lax.all_to_all(wide, axes, 0, 0)]
    ppermute x4 -> x18, waiting for transfers between devices: 13.2 us -> 34.1 us  [the longest x1 14 us: shards(): after = lax.ppermute(gc[:8], ring, [(i + 1, i) for i in range(15)])]
  transfers between devices with their start and end apart: 8 -> 20, of which waited for: 5 -> 7; matrix products, arithmetic and copies ran while one was open for 10% -> 5% of each run, Pallas kernels for 0% -> 10%
where the time goes in v1:
time: 258 us; the launch traced here: 257 us
  starting transfers between devices  111 us (43%)
  Pallas kernels  37.2 us (14%)
  waiting for transfers between devices  34.1 us (13%)
  blocking collectives  32.5 us (13%)
  local copies, waits for them, and re-layouts  29.1 us (11%)
  other arithmetic  11.2 us (4%)
    ppermute x7, starting transfers between devices, swap(): return lax.ppermute(a, axis, [(0, 1), (1, 0)])  42.7 us
    pallas_call x5, Pallas kernels, call(): pl.pallas_call(body, out_shape=out_shape, in_specs=specs, out_specs=outs,...  37.2 us
    all_to_all x2, blocking collectives, share(): return lax.all_to_all(wide, axes, 0, 0)  32.5 us
    ppermute x9, starting transfers between devices, from_x(): return lax.ppermute(a, 'x', [((i + step) % 4, i) for i in range(4)])  28.9 us
    unnamed x84, local copies, waits for them, and re-layouts  27.1 us
    all_to_all x2, starting transfers between devices, share(): return lax.all_to_all(wide, axes, 0, 0)  19.7 us
    ppermute x1, starting transfers between devices, shards(): before = lax.ppermute(gc[BLOCK - 8:], ring, [(i, i + 1) for i in range(15)])  18.3 us
    ppermute x1, waiting for transfers between devices, shards(): after = lax.ppermute(gc[:8], ring, [(i + 1, i) for i in range(15)])  14 us
  transfers between devices with their start and end apart: 20, of which 7 were waited for; matrix products, arithmetic and copies ran while one was open for 5% of the time, Pallas kernels for 10%

profile of v1, /device:TPU:7, one launch (start us, length us, event | category | flops | bytes accessed | tf_op | source)
XLA Modules:
  0.0 256.6 jit_solution(18427110862497089885)
XLA Ops:
  0.6 15.6 %collective-permute-start.4 = (bf16[128,768]{1,0:T(8,128)(2,1)}, bf16[128,768]{1,0:T(8,128)(2,1)S(1)}, u32[]{:S(2)}, u32[]{:S(2)}) collective-permute-start(bf16[128,768]{1,0:T(8,128)(2,1)} %bitcast.24), channel_id=1, source_target_pairs={{0,8},{8,0},{1,9},{9,1},{2,10},{10,2},{3,11},{11,3},{4,12},{12,4},... | collective-permute-start | bytes 589832 | tf_op jit(solution)/shard_map/ppermute | solution.py:267
  17.2 2.9 %collective-permute-start = (bf16[128,384]{1,0:T(8,128)(2,1)S(1)}, bf16[128,384]{1,0:T(8,128)(2,1)S(1)}, u32[]{:S(2)}, u32[]{:S(2)}) collective-permute-start(bf16[128,384]{1,0:T(8,128)(2,1)S(1)} %broadcast_select_fusion.10), channel_id=1, source_target_pairs={{0,1},{1,0},{2,3},{3,2},{4,5},{5,4},{6,7},{7,6},{8,9},{9,8},{10,11... | collective-permute-start | bytes 294920 | tf_op jit(solution)/shard_map/ppermute | solution.py:267
  21.1 2.4 collective-permute-start.5
  27.6 5.0 %collective-permute-start.2 = (bf16[256,768]{1,0:T(8,128)(2,1)S(1)}, bf16[256,768]{1,0:T(8,128)(2,1)S(1)}, u32[]{:S(2)}, u32[]{:S(2)}) collective-permute-start(bf16[256,768]{1,0:T(8,128)(2,1)S(1)} %maximum_maximum_fusion), channel_id=1, source_target_pairs={{4,0},{6,2},{0,4},{2,6},{5,1},{7,3},{1,5},{3,7},{12,8},{14,10},{8,... | collective-permute-start | bytes 1179656 | tf_op jit(solution)/shard_map/ppermute | solution.py:271
  34.5 3.6 %collective-permute-start.6 = (bf16[128,768]{1,0:T(8,128)(2,1)S(1)}, bf16[128,768]{1,0:T(8,128)(2,1)S(1)}, u32[]{:S(2)}, u32[]{:S(2)}) collective-permute-start(bf16[128,768]{1,0:T(8,128)(2,1)S(1)} %collective-permute-done.4.s4), channel_id=1, source_target_pairs={{4,0},{6,2},{0,4},{2,6},{5,1},{7,3},{1,5},{3,7},{12,8},{14,10},{8,... | collective-permute-start | bytes 589832 | tf_op jit(solution)/shard_map/ppermute | solution.py:271
  38.2 4.0 %collective-permute-start.7 = (bf16[128,768]{1,0:T(8,128)(2,1)S(1)}, bf16[128,768]{1,0:T(8,128)(2,1)S(1)}, u32[]{:S(2)}, u32[]{:S(2)}) collective-permute-start(bf16[128,768]{1,0:T(8,128)(2,1)S(1)} %collective-permute-done.4.s4), channel_id=1, source_target_pairs={{6,0},{0,2},{2,4},{4,6},{7,1},{1,3},{3,5},{5,7},{14,8},{8,10},{10,... | collective-permute-start | bytes 589832 | tf_op jit(solution)/shard_map/ppermute | solution.py:271
  42.2 2.5 broadcast_select_fusion
  44.7 5.9 %collective-permute-done.6.s6 = bf16[128,768]{1,0:T(8,128)(2,1)S(1)} collective-permute-done((bf16[128,768]{1,0:T(8,128)(2,1)S(1)}, bf16[128,768]{1,0:T(8,128)(2,1)S(1)}, u32[]{:S(2)}, u32[]{:S(2)}) %collective-permute-start.6) | collective-permute-done | bytes 196640 | tf_op jit(solution)/shard_map/ppermute | solution.py:271
  50.6 7.3 %collective-permute-done.7.s7 = bf16[128,768]{1,0:T(8,128)(2,1)S(1)} collective-permute-done((bf16[128,768]{1,0:T(8,128)(2,1)S(1)}, bf16[128,768]{1,0:T(8,128)(2,1)S(1)}, u32[]{:S(2)}, u32[]{:S(2)}) %collective-permute-start.7) | collective-permute-done | bytes 196640 | tf_op jit(solution)/shard_map/ppermute | solution.py:271
  58.9 3.6 %collective-permute-start.9 = (bf16[512,768]{1,0:T(8,128)(2,1)}, bf16[512,768]{1,0:T(8,128)(2,1)S(1)}, u32[]{:S(2)}, u32[]{:S(2)}) collective-permute-start(bf16[512,768]{1,0:T(8,128)(2,1)} %pad_maximum_fusion.3), channel_id=1, source_target_pairs={{0,1},{1,0},{2,3},{3,2},{4,5},{5,4},{6,7},{7,6},{8,9},{9,8},{10,11... | collective-permute-start | bytes 2359304 | tf_op jit(solution)/shard_map/ppermute | solution.py:267
  66.6 11.8 %collective-permute-start.10 = (bf16[128,768]{1,0:T(8,128)(2,1)S(1)}, bf16[128,768]{1,0:T(8,128)(2,1)}, u32[]{:S(2)}, u32[]{:S(2)}) collective-permute-start(bf16[128,768]{1,0:T(8,128)(2,1)S(1)} %pad_maximum_fusion.4.d0), channel_id=1, source_target_pairs={{0,8},{8,0},{1,9},{9,1},{2,10},{10,2},{3,11},{11,3},{4,12},{12,4},... | collective-permute-start | bytes 589832 | tf_op jit(solution)/shard_map/ppermute | solution.py:267
  79.3 4.1 %collective-permute-done.10.d4 = bf16[128,768]{1,0:T(8,128)(2,1)} collective-permute-done((bf16[128,768]{1,0:T(8,128)(2,1)S(1)}, bf16[128,768]{1,0:T(8,128)(2,1)}, u32[]{:S(2)}, u32[]{:S(2)}) %collective-permute-start.10) | collective-permute-done | bytes 196640 | tf_op jit(solution)/shard_map/ppermute | solution.py:267
  83.3 3.2 %collective-permute-start.11 = (bf16[128,768]{1,0:T(8,128)(2,1)}, bf16[128,768]{1,0:T(8,128)(2,1)}, u32[]{:S(2)}, u32[]{:S(2)}) collective-permute-start(bf16[128,768]{1,0:T(8,128)(2,1)} %collective-permute-done.10.d4), channel_id=1, source_target_pairs={{2,0},{4,2},{6,4},{0,6},{3,1},{5,3},{7,5},{1,7},{10,8},{12,10},{14... | collective-permute-start | bytes 589832 | tf_op jit(solution)/shard_map/ppermute | solution.py:271
  86.5 4.1 %collective-permute-start.12 = (bf16[128,768]{1,0:T(8,128)(2,1)}, bf16[128,768]{1,0:T(8,128)(2,1)}, u32[]{:S(2)}, u32[]{:S(2)}) collective-permute-start(bf16[128,768]{1,0:T(8,128)(2,1)} %collective-permute-done.10.d4), channel_id=1, source_target_pairs={{4,0},{6,2},{0,4},{2,6},{5,1},{7,3},{1,5},{3,7},{12,8},{14,10},{8,... | collective-permute-start | bytes 589832 | tf_op jit(solution)/shard_map/ppermute | solution.py:271
  105.5 13.8 %shard_map.94 = (bf16[3,2048,128]{2,1,0:T(8,128)(2,1)S(1)}, bf16[3,2048,128]{2,1,0:T(8,128)(2,1)S(1)}, bf16[3,2048,128]{2,1,0:T(8,128)(2,1)S(1)}, bf16[160,768]{1,0:T(8,128)(2,1)S(1)}) custom-call(s32[3]{0:T(128)S(1)} %pad_add_fusion.pos, bf16[128,768]{1,0:T(8,128)(2,1)S(1)} %bitcast.27, bf16[256,768]{1,0:T(8,128)(2,1)S(1)} %copy-done.5, ...), custom_call_target="tpu_custom_call" | custom-call | tf_op jit(solution)/shard_map/pallas_call | solution.py:40
  119.3 10.2 %shard_map.95 = (bf16[3,256,128]{2,1,0:T(8,128)(2,1)S(1)}, f32[8,512]{1,0:T(8,128)S(1)}) custom-call(bf16[3,2048,128]{2,1,0:T(8,128)(2,1)S(1)} %get-tuple-element.14.q, bf16[3,2048,128]{2,1,0:T(8,128)(2,1)S(1)} %get-tuple-element.15.k, bf16[3,2048,128]{2,1,0:T(8,128)(2,1)S(1)} %get-tuple-element.16.v, bf16[128,768]{1,0:T(8,128)(2,1)S(1)} %pad_maximum_fusion.4.d0, ...), custom_call_target="tpu_custom_call" | custom-call | tf_op jit(solution)/shard_map/pallas_call | solution.py:40
  130.8 4.7 %all-to-all-start = ((f32[4,8,512]{2,1,0:T(8,128)}), f32[4,8,512]{2,1,0:T(8,128)}, u32[]{:S(2)}, u32[]{:S(2)}) async-start(f32[4,8,512]{2,1,0:T(8,128)} %broadcast_in_dim.10), calls=%async_computation | async-start | bytes 131072 | tf_op jit(solution)/shard_map/all_to_all | solution.py:276
  145.8 9.9 %shard_map.96 = (bf16[3,256,128]{2,1,0:T(8,128)(2,1)S(1)}, bf16[3,256,128]{2,1,0:T(8,128)(2,1)S(1)}) custom-call(s32[3]{0:T(128)S(1)} %pad_add_fusion.pos, bf16[3,2048,128]{2,1,0:T(8,128)(2,1)S(1)} %get-tuple-element.14.q, bf16[3,2048,128]{2,1,0:T(8,128)(2,1)S(1)} %copy-done.1, bf16[3,2048,128]{2,1,0:T(8,128)(2,1)S(1)} %copy-done.3, ...), custom_call_target="tpu_custom_call" | custom-call | tf_op jit(solution)/shard_map/pallas_call | solution.py:40
  160.6 4.6 %collective-permute-start.14 = (bf16[128,1152]{1,0:T(8,128)(2,1)S(1)}, bf16[128,1152]{1,0:T(8,128)(2,1)S(1)}, u32[]{:S(2)}, u32[]{:S(2)}) collective-permute-start(bf16[128,1152]{1,0:T(8,128)(2,1)S(1)} %get-tuple-element.31), channel_id=1, source_target_pairs={{0,1},{1,0},{2,3},{3,2},{4,5},{5,4},{6,7},{7,6},{8,9},{9,8},{10,11... | collective-permute-start | bytes 884744 | tf_op jit(solution)/shard_map/ppermute | solution.py:267
  171.6 13.2 %all_to_all.20 = f32[16,8,768]{2,1,0:T(8,128)S(1)} all-to-all(f32[16,8,768]{2,1,0:T(8,128)S(1)} %broadcast_in_dim.12), channel_id=1, replica_groups=mesh['y'=4,'zm'=2,'zl'=4,'zh'=2,'x'=4,'core'=2] {'y','x'}, dimensions={0} | all-to-all | bytes 786432 | tf_op jit(solution)/shard_map/all_to_all | solution.py:276
  184.9 19.3 %all_to_all.21 = f32[4,8,768]{2,1,0:T(8,128)S(1)} all-to-all(f32[4,8,768]{2,1,0:T(8,128)S(1)} %broadcast_in_dim.13), channel_id=1, replica_groups=mesh['y'=4,'zm'=2,'zl'=4,'zh'=2,'x'=4,'core'=2] {'zl'}, dimensions={0} | all-to-all | bytes 196608 | tf_op jit(solution)/shard_map/all_to_all | solution.py:276
  204.8 15.0 %all-to-all-start.3 = ((f32[4,8,768]{2,1,0:T(8,128)}), f32[4,8,768]{2,1,0:T(8,128)S(1)}, u32[]{:S(2)}, u32[]{:S(2)}) async-start(f32[4,8,768]{2,1,0:T(8,128)} %broadcast_in_dim.14), calls=%async_computation.3 | async-start | bytes 196608 | tf_op jit(solution)/shard_map/all_to_all | solution.py:276
  219.8 18.3 %collective-permute-start.15 = (f32[8,768]{1,0:T(8,128)S(1)}, f32[8,768]{1,0:T(8,128)S(1)}, u32[]{:S(2)}, u32[]{:S(2)}) collective-permute-start(f32[8,768]{1,0:T(8,128)S(1)} %get-tuple-element.34), channel_id=1, source_target_pairs={{0,1},{1,2},{2,3},{3,4},{4,5},{5,6},{6,7},{7,8},{8,9},{9,10},{10,1... | collective-permute-start | bytes 73736 | tf_op jit(solution)/shard_map/ppermute | solution.py:348
  240.0 14.0 %collective-permute-done.16.after = f32[8,768]{1,0:T(8,128)S(1)} collective-permute-done((f32[8,768]{1,0:T(8,128)S(1)}, f32[8,768]{1,0:T(8,128)S(1)}, u32[]{:S(2)}, u32[]{:S(2)}) %collective-permute-start.16) | collective-permute-done | bytes 24608 | tf_op jit(solution)/shard_map/ppermute | solution.py:349
  (134 shorter events, 56.6 us)
Async XLA Ops:
  0.6 41.6 %copy-start.35 = (bf16[768,768]{1,0:T(8,128)(2,1)S(1)}, bf16[768,768]{1,0:T(8,128)(2,1)}, u32[]{:S(2)}) copy-start(bf16[768,768]{1,0:T(8,128)(2,1)} %param.12) | copy-start | bytes 3538948
  0.6 20.4 %collective-permute-start.4 = (bf16[128,768]{1,0:T(8,128)(2,1)}, bf16[128,768]{1,0:T(8,128)(2,1)S(1)}, u32[]{:S(2)}, u32[]{:S(2)}) collective-permute-start(bf16[128,768]{1,0:T(8,128)(2,1)} %bitcast.24), channel_id=1, source_target_pairs={{0,8},{8,0},{1,9},{9,1},{2,10},{10,2},{3,11},{11,3},{4,12},{12,4},... | collective-permute-start | bytes 589832 | tf_op jit(solution)/shard_map/ppermute | solution.py:267
  17.2 6.3 %collective-permute-start = (bf16[128,384]{1,0:T(8,128)(2,1)S(1)}, bf16[128,384]{1,0:T(8,128)(2,1)S(1)}, u32[]{:S(2)}, u32[]{:S(2)}) collective-permute-start(bf16[128,384]{1,0:T(8,128)(2,1)S(1)} %broadcast_select_fusion.10), channel_id=1, source_target_pairs={{0,1},{1,0},{2,3},{3,2},{4,5},{5,4},{6,7},{7,6},{8,9},{9,8},{10,11... | collective-permute-start | bytes 294920 | tf_op jit(solution)/shard_map/ppermute | solution.py:267
  21.1 36.9 %copy-start.17 = (bf16[128,768]{1,0:T(8,128)(2,1)}, bf16[128,768]{1,0:T(8,128)(2,1)S(1)}, u32[]{:S(2)}) copy-start(bf16[128,768]{1,0:T(8,128)(2,1)S(1)} %collective-permute-done.4.s4) | copy-start | bytes 589828
  21.1 17.1 %collective-permute-start.5 = (bf16[128,768]{1,0:T(8,128)(2,1)S(1)}, bf16[128,768]{1,0:T(8,128)(2,1)S(1)}, u32[]{:S(2)}, u32[]{:S(2)}) collective-permute-start(bf16[128,768]{1,0:T(8,128)(2,1)S(1)} %collective-permute-done.4.s4), channel_id=1, source_target_pairs={{2,0},{4,2},{6,4},{0,6},{3,1},{5,3},{7,5},{1,7},{10,8},{12,10},{14... | collective-permute-start | bytes 589832 | tf_op jit(solution)/shard_map/ppermute | solution.py:271
  25.5 37.0 %collective-permute-start.1 = (bf16[256,768]{1,0:T(8,128)(2,1)S(1)}, bf16[256,768]{1,0:T(8,128)(2,1)S(1)}, u32[]{:S(2)}, u32[]{:S(2)}) collective-permute-start(bf16[256,768]{1,0:T(8,128)(2,1)S(1)} %maximum_maximum_fusion), channel_id=1, source_target_pairs={{2,0},{4,2},{6,4},{0,6},{3,1},{5,3},{7,5},{1,7},{10,8},{12,10},{14... | collective-permute-start | bytes 1179656 | tf_op jit(solution)/shard_map/ppermute | solution.py:271
  27.6 34.9 %collective-permute-start.2 = (bf16[256,768]{1,0:T(8,128)(2,1)S(1)}, bf16[256,768]{1,0:T(8,128)(2,1)S(1)}, u32[]{:S(2)}, u32[]{:S(2)}) collective-permute-start(bf16[256,768]{1,0:T(8,128)(2,1)S(1)} %maximum_maximum_fusion), channel_id=1, source_target_pairs={{4,0},{6,2},{0,4},{2,6},{5,1},{7,3},{1,5},{3,7},{12,8},{14,10},{8,... | collective-permute-start | bytes 1179656 | tf_op jit(solution)/shard_map/ppermute | solution.py:271
  32.6 30.0 %collective-permute-start.3 = (bf16[256,768]{1,0:T(8,128)(2,1)S(1)}, bf16[256,768]{1,0:T(8,128)(2,1)S(1)}, u32[]{:S(2)}, u32[]{:S(2)}) collective-permute-start(bf16[256,768]{1,0:T(8,128)(2,1)S(1)} %maximum_maximum_fusion), channel_id=1, source_target_pairs={{6,0},{0,2},{2,4},{4,6},{7,1},{1,3},{3,5},{5,7},{14,8},{8,10},{10,... | collective-permute-start | bytes 1179656 | tf_op jit(solution)/shard_map/ppermute | solution.py:271
  34.5 16.1 %collective-permute-start.6 = (bf16[128,768]{1,0:T(8,128)(2,1)S(1)}, bf16[128,768]{1,0:T(8,128)(2,1)S(1)}, u32[]{:S(2)}, u32[]{:S(2)}) collective-permute-start(bf16[128,768]{1,0:T(8,128)(2,1)S(1)} %collective-permute-done.4.s4), channel_id=1, source_target_pairs={{4,0},{6,2},{0,4},{2,6},{5,1},{7,3},{1,5},{3,7},{12,8},{14,10},{8,... | collective-permute-start | bytes 589832 | tf_op jit(solution)/shard_map/ppermute | solution.py:271
  38.2 19.8 %copy-start.19 = (bf16[128,768]{1,0:T(8,128)(2,1)}, bf16[128,768]{1,0:T(8,128)(2,1)S(1)}, u32[]{:S(2)}) copy-start(bf16[128,768]{1,0:T(8,128)(2,1)S(1)} %collective-permute-done.5.s5) | copy-start | bytes 589828
  38.2 19.7 %collective-permute-start.7 = (bf16[128,768]{1,0:T(8,128)(2,1)S(1)}, bf16[128,768]{1,0:T(8,128)(2,1)S(1)}, u32[]{:S(2)}, u32[]{:S(2)}) collective-permute-start(bf16[128,768]{1,0:T(8,128)(2,1)S(1)} %collective-permute-done.4.s4), channel_id=1, source_target_pairs={{6,0},{0,2},{2,4},{4,6},{7,1},{1,3},{3,5},{5,7},{14,8},{8,10},{10,... | collective-permute-start | bytes 589832 | tf_op jit(solution)/shard_map/ppermute | solution.py:271
  44.7 17.9 %copy-start.13 = (bf16[1,128,768]{2,1,0:T(8,128)(2,1)S(1)}, bf16[1,128,768]{2,1,0:T(8,128)(2,1)}, u32[]{:S(2)}) copy-start(bf16[1,128,768]{2,1,0:T(8,128)(2,1)} %param.7) | copy-start | bytes 589828
  58.9 34.2 %collective-permute-start.9 = (bf16[512,768]{1,0:T(8,128)(2,1)}, bf16[512,768]{1,0:T(8,128)(2,1)S(1)}, u32[]{:S(2)}, u32[]{:S(2)}) collective-permute-start(bf16[512,768]{1,0:T(8,128)(2,1)} %pad_maximum_fusion.3), channel_id=1, source_target_pairs={{0,1},{1,0},{2,3},{3,2},{4,5},{5,4},{6,7},{7,6},{8,9},{9,8},{10,11... | collective-permute-start | bytes 2359304 | tf_op jit(solution)/shard_map/ppermute | solution.py:267
  63.7 30.3 %collective-permute-start.8 = (bf16[512,768]{1,0:T(8,128)(2,1)}, bf16[512,768]{1,0:T(8,128)(2,1)S(1)}, u32[]{:S(2)}, u32[]{:S(2)}) collective-permute-start(bf16[512,768]{1,0:T(8,128)(2,1)} %pad_maximum_fusion.2), channel_id=1, source_target_pairs={{0,1},{1,0},{2,3},{3,2},{4,5},{5,4},{6,7},{7,6},{8,9},{9,8},{10,11... | collective-permute-start | bytes 2359304 | tf_op jit(solution)/shard_map/ppermute | solution.py:267
  66.6 16.7 %collective-permute-start.10 = (bf16[128,768]{1,0:T(8,128)(2,1)S(1)}, bf16[128,768]{1,0:T(8,128)(2,1)}, u32[]{:S(2)}, u32[]{:S(2)}) collective-permute-start(bf16[128,768]{1,0:T(8,128)(2,1)S(1)} %pad_maximum_fusion.4.d0), channel_id=1, source_target_pairs={{0,8},{8,0},{1,9},{9,1},{2,10},{10,2},{3,11},{11,3},{4,12},{12,4},... | collective-permute-start | bytes 589832 | tf_op jit(solution)/shard_map/ppermute | solution.py:267
  83.3 56.6 %collective-permute-start.11 = (bf16[128,768]{1,0:T(8,128)(2,1)}, bf16[128,768]{1,0:T(8,128)(2,1)}, u32[]{:S(2)}, u32[]{:S(2)}) collective-permute-start(bf16[128,768]{1,0:T(8,128)(2,1)} %collective-permute-done.10.d4), channel_id=1, source_target_pairs={{2,0},{4,2},{6,4},{0,6},{3,1},{5,3},{7,5},{1,7},{10,8},{12,10},{14... | collective-permute-start | bytes 589832 | tf_op jit(solution)/shard_map/ppermute | solution.py:271
  86.5 53.4 %collective-permute-start.12 = (bf16[128,768]{1,0:T(8,128)(2,1)}, bf16[128,768]{1,0:T(8,128)(2,1)}, u32[]{:S(2)}, u32[]{:S(2)}) collective-permute-start(bf16[128,768]{1,0:T(8,128)(2,1)} %collective-permute-done.10.d4), channel_id=1, source_target_pairs={{4,0},{6,2},{0,4},{2,6},{5,1},{7,3},{1,5},{3,7},{12,8},{14,10},{8,... | collective-permute-start | bytes 589832 | tf_op jit(solution)/shard_map/ppermute | solution.py:271
  90.7 49.2 %collective-permute-start.13 = (bf16[128,768]{1,0:T(8,128)(2,1)}, bf16[128,768]{1,0:T(8,128)(2,1)}, u32[]{:S(2)}, u32[]{:S(2)}) collective-permute-start(bf16[128,768]{1,0:T(8,128)(2,1)} %collective-permute-done.10.d4), channel_id=1, source_target_pairs={{6,0},{0,2},{2,4},{4,6},{7,1},{1,3},{3,5},{5,7},{14,8},{8,10},{10,... | collective-permute-start | bytes 589832 | tf_op jit(solution)/shard_map/ppermute | solution.py:271
  130.8 9.1 %all-to-all-start = ((f32[4,8,512]{2,1,0:T(8,128)}), f32[4,8,512]{2,1,0:T(8,128)}, u32[]{:S(2)}, u32[]{:S(2)}) async-start(f32[4,8,512]{2,1,0:T(8,128)} %broadcast_in_dim.10), calls=%async_computation | async-start | bytes 131072 | tf_op jit(solution)/shard_map/all_to_all | solution.py:276
  160.6 5.8 %collective-permute-start.14 = (bf16[128,1152]{1,0:T(8,128)(2,1)S(1)}, bf16[128,1152]{1,0:T(8,128)(2,1)S(1)}, u32[]{:S(2)}, u32[]{:S(2)}) collective-permute-start(bf16[128,1152]{1,0:T(8,128)(2,1)S(1)} %get-tuple-element.31), channel_id=1, source_target_pairs={{0,1},{1,0},{2,3},{3,2},{4,5},{5,4},{6,7},{7,6},{8,9},{9,8},{10,11... | collective-permute-start | bytes 884744 | tf_op jit(solution)/shard_map/ppermute | solution.py:267
  168.4 3.1 %collective-permute-start.17 = (f32[8,768]{1,0:T(8,128)S(1)}, f32[8,768]{1,0:T(8,128)S(1)}, u32[]{:S(2)}, u32[]{:S(2)}) collective-permute-start(f32[8,768]{1,0:T(8,128)S(1)} %get-tuple-element.24), channel_id=1, source_target_pairs={{0,1},{1,0},{2,3},{3,2},{4,5},{5,4},{6,7},{7,6},{8,9},{9,8},{10,11... | collective-permute-start | bytes 73736 | tf_op jit(solution)/shard_map/ppermute | solution.py:267
  204.8 50.6 %all-to-all-start.3 = ((f32[4,8,768]{2,1,0:T(8,128)}), f32[4,8,768]{2,1,0:T(8,128)S(1)}, u32[]{:S(2)}, u32[]{:S(2)}) async-start(f32[4,8,768]{2,1,0:T(8,128)} %broadcast_in_dim.14), calls=%async_computation.3 | async-start | bytes 196608 | tf_op jit(solution)/shard_map/all_to_all | solution.py:276
  219.8 20.2 %collective-permute-start.15 = (f32[8,768]{1,0:T(8,128)S(1)}, f32[8,768]{1,0:T(8,128)S(1)}, u32[]{:S(2)}, u32[]{:S(2)}) collective-permute-start(f32[8,768]{1,0:T(8,128)S(1)} %get-tuple-element.34), channel_id=1, source_target_pairs={{0,1},{1,2},{2,3},{3,4},{4,5},{5,6},{6,7},{7,8},{8,9},{9,10},{10,1... | collective-permute-start | bytes 73736 | tf_op jit(solution)/shard_map/ppermute | solution.py:348
  238.1 16.0 %collective-permute-start.16 = (f32[8,768]{1,0:T(8,128)S(1)}, f32[8,768]{1,0:T(8,128)S(1)}, u32[]{:S(2)}, u32[]{:S(2)}) collective-permute-start(f32[8,768]{1,0:T(8,128)S(1)} %get-tuple-element.33), channel_id=1, source_target_pairs={{1,0},{2,1},{3,2},{4,3},{5,4},{6,5},{7,6},{8,7},{9,8},{10,9},{11,1... | collective-permute-start | bytes 73736 | tf_op jit(solution)/shard_map/ppermute | solution.py:349
  (34 other events, 119.2 us)

commit v2 on v1

--- a/solution.py
+++ b/solution.py
@@ -34,7 +34,7 @@
     return pl.BlockSpec(memory_space=pltpu.SMEM)
 
 
-def call(body, out_shape, args, scratch=(), limit=40):
+def call(body, out_shape, args, scratch=(), limit=16):
     specs = [sspec() if a.dtype == jnp.int32 else vspec() for a in args]
     outs = jax.tree.map(lambda _: vspec(), out_shape)
     return pl.pallas_call(
@@ -74,18 +74,19 @@
 
 
 def hidden_body(
-    pos, s0, s1, s2, s3, s4, s5, s6, s7, e0, e1, w, gain, taps, q, k, v, ext, xs, ns, hs
+    pos, c0, c1, e0, e1, w, gain, taps, q, k, v, ext, xs, ns, hs
 ):
     core = pos[2]
     here = pl.multiple_of(core * BLOCK, BLOCK)
     there = pl.multiple_of((1 - core) * BLOCK, BLOCK)
-    for c, s in enumerate((s0, s1, s2, s3, s4, s5, s6, s7)):
-        other = e0 if c < 4 else e1
-        xs[c, pl.ds(here, BLOCK), :] = s[0:BLOCK, :]
-        xs[c, pl.ds(there, BLOCK), :] = other[(c % 4) * BLOCK : (c % 4 + 1) * BLOCK, :]
+    for c in range(CHUNKS):
+        own, other = ((c0, e0), (c1, e1))[c // 4]
+        sl = slice((c % 4) * BLOCK, (c % 4 + 1) * BLOCK)
+        xs[c, pl.ds(here, BLOCK), :] = own[sl, :]
+        xs[c, pl.ds(there, BLOCK), :] = other[sl, :]
     prev, nxt, prev_ok, nxt_ok = neighbours(pos, jnp.int32(0), jnp.int32(0))
     first = core == 0
-    ext[16:144, :] = s0[0:BLOCK, :]
+    ext[16:144, :] = c0[0:BLOCK, :]
 
     @pl.when(first)
     def _():
@@ -179,9 +180,12 @@
     stats[...] = jnp.transpose(sm[...])[0:8, :]
 
 
-def backward_body(pos, q, k, v, d0, d1, d2, d3, d4, d5, d6, d7, stats, dk, dv, ds):
-    for c, d in enumerate((d0, d1, d2, d3, d4, d5, d6, d7)):
-        low = BLOCK if c in (1, 2, 3) else 0
+def backward_body(pos, q, k, v, dq, d0, d4, b1, b2, b3, stats, mine, give, ds, gs):
+    core = pos[2]
+    here = pl.multiple_of(core * BLOCK, BLOCK)
+    there = pl.multiple_of((1 - core) * BLOCK, BLOCK)
+    blocks = ((d0, 0), (b1, 0), (b2, 0), (b3, 0), (d4, 0), (b1, BLOCK), (b2, BLOCK), (b3, BLOCK))
+    for c, (d, low) in enumerate(blocks):
         for h in range(OWN_HEADS):
             ds[h, c * CHUNK : c * CHUNK + BLOCK, :] = d[
                 low : low + BLOCK, h * 128 : (h + 1) * 128
@@ -210,8 +214,11 @@
 
         zero = jnp.zeros((CHUNK, HEAD_DIM), F32)
         acc_k, acc_v = lax.fori_loop(0, 4, step, (zero, zero))
-        dk[h, :, :] = (acc_k * SCALE).astype(BF16)
-        dv[h, :, :] = acc_v.astype(BF16)
+        gs[:, h * 128 : (h + 1) * 128] = dq[h]
+        gs[:, HALF + h * 128 : HALF + (h + 1) * 128] = (acc_k * SCALE).astype(BF16)
+        gs[:, 2 * HALF + h * 128 : 2 * HALF + (h + 1) * 128] = acc_v.astype(BF16)
+    mine[...] = gs[pl.ds(here, BLOCK), :]
+    give[...] = gs[pl.ds(there, BLOCK), :]
 
 
 def conv_body(mine, recv, w_own, w_oth, ext, gain, taps, gh, gc, usum, ns):
@@ -237,9 +244,11 @@
             gc[r : r + 64, j : j + 128] = gcv
             for t in range(5):
                 sums[t] = sums[t] + jnp.sum((gcv * near[t]).reshape(8, 8, 128), axis=0)
+        side, slot = divmod(j // 128, OWN_HEADS)
         for t in range(5):
-            usum[t : t + 1, j : j + 128] = jnp.sum(sums[t], axis=0, keepdims=True)
-        usum[5:8, j : j + 128] = jnp.zeros((3, 128), F32)
+            row = t * OWN_HEADS + slot
+            usum[side, row : row + 1, :] = jnp.sum(sums[t], axis=0, keepdims=True)
+    usum[:, 15:16, :] = jnp.zeros((2, 1, 128), F32)
 
 
 def final_body(gh, gc, before, after, ext, gain, taps, out, es):
@@ -290,19 +299,23 @@
         low, high = a[:, :HALF], a[:, HALF:]
         return jnp.where(first, low, high), jnp.where(first, high, low)
 
-    sig_z = swap(sig, "zh")
     keep, give = halves(cot)
     got = swap(give, "core")
     cot_own = jnp.concatenate(
         [jnp.where(first, keep, got), jnp.where(first, got, keep)], axis=1
     )
-    cot_z = swap(cot_own, "zh")
-    both = jnp.concatenate([sig, cot_own], axis=0)
-    near = [from_x(both, d) for d in (1, 2, 3)]
+    sig_z = swap(sig, "zh")
+    near = [from_x(sig, d) for d in (1, 2, 3)]
+    sig_z, near = lax.optimization_barrier((sig_z, near))
+    cot_z = swap(lax.optimization_barrier((cot_own, sig_z))[0], "zh")
     far = [from_x(sig_z, d) for d in (1, 2, 3)]
-    e0 = swap(jnp.concatenate([sig] + [n[:BLOCK] for n in near], axis=0), "core")
-    e1 = swap(jnp.concatenate([sig_z] + far, axis=0), "core")
-    cot_far = [from_x(cot_z, d) for d in (1, 2, 3)]
+    c0 = jnp.concatenate([sig] + near, axis=0)
+    e0 = swap(c0, "core")
+    far, cot_z = lax.optimization_barrier((far, cot_z))
+    c1 = jnp.concatenate([sig_z] + far, axis=0)
+    e1 = swap(c1, "core")
+    both = jnp.concatenate([cot_own, cot_z], axis=0)
+    cots = [from_x(both, d) for d in (1, 2, 3)]
 
     parts = [halves(w) for w in (w_query, w_key, w_value)]
     w_own = jnp.concatenate([p[0] for p in parts], axis=1)
@@ -312,7 +325,7 @@
     q, k, v, ext = call(
         hidden_body,
         (head_shape, head_shape, head_shape, jax.ShapeDtypeStruct((160, C), BF16)),
-        (pos, sig, *near, sig_z, *far, e0, e1, w_own, gain, conv_taps),
+        (pos, c0, c1, e0, e1, w_own, gain, conv_taps),
         (VM((CHUNKS, CHUNK, C), BF16), VM((288, C), F32), VM((CHUNK, C), BF16)),
     )
     part = jax.ShapeDtypeStruct((OWN_HEADS, CHUNK, HEAD_DIM), BF16)
@@ -326,21 +339,20 @@
             VM((2 * CHUNK, 128), F32),
         ),
     )
+    stats, cots = lax.optimization_barrier((stats, cots))
     stats_all = share(stats, "x", 4)
-    dk, dv = call(
+    grads = jax.ShapeDtypeStruct((BLOCK, 3 * HALF), BF16)
+    mine, give = call(
         backward_body,
-        (part, part),
-        (pos, q, k, v, cot_own, *near, cot_z, *cot_far, stats_all),
-        (VM((OWN_HEADS, BINS, HEAD_DIM), BF16),),
-    )
-    grads = jnp.concatenate([dq[h] for h in range(3)] + [dk[h] for h in range(3)] + [dv[h] for h in range(3)], axis=1)
-    mine = jnp.where(first, grads[:BLOCK], grads[BLOCK:])
-    give = jnp.where(first, grads[BLOCK:], grads[:BLOCK])
+        (grads, grads),
+        (pos, q, k, v, dq, cot_own, cot_z, *cots, stats_all),
+        (VM((OWN_HEADS, BINS, HEAD_DIM), BF16), VM((CHUNK, 3 * HALF), BF16)),
+    )
     recv = swap(give, "core")
     wide = jax.ShapeDtypeStruct((BLOCK, C), F32)
     gh, gc, usum = call(
         conv_body,
-        (wide, wide, jax.ShapeDtypeStruct((8, C), F32)),
+        (wide, wide, jax.ShapeDtypeStruct((2, 16, 128), F32)),
         (mine, recv, w_own, w_oth, ext, gain, conv_taps),
         (VM((160, C), F32),),
     )
@@ -353,10 +365,12 @@
         (gh, gc, before, after, ext, gain, conv_taps),
         (VM((144, C), F32),),
     )
-    usum = usum + swap(usum, "core")
-    usum = jnp.sum(share(usum, ("y", "x"), 16), axis=0)
-    usum = jnp.sum(share(usum, ("zl",), 4), axis=0)
-    usum = jnp.sum(share(usum, ("zm", "zh"), 4), axis=0)[:5]
+    wide = jnp.broadcast_to(usum[None], (16, 2, 16, 128)).reshape(32, 16, 128)
+    part = jnp.sum(lax.all_to_all(wide, ("y", "x", "core"), 0, 0), axis=0)
+    part = share(part.astype(BF16), ("zm", "zl", "zh"), 16).astype(F32)
+    part = jnp.sum(part, axis=0)
+    usum = lax.all_gather(part, "core", axis=0)[:, :15].reshape(2, 5, HALF)
+    usum = jnp.concatenate([usum[0], usum[1]], axis=1)
     grad_taps = usum * gain
     grad_gain = jnp.sum(usum * conv_taps, axis=0)
     return out[None], grad_taps, grad_gain

time: 258 us -> 190 us (0.74)
  local copies, waits for them, and re-layouts: 29.1 us -> 2.25 us
  starting transfers between devices: 111 us -> 97.4 us
  blocking collectives: 32.5 us -> 22.9 us
  waiting for transfers between devices: 34.1 us -> 24.9 us
  other arithmetic: 11.2 us -> 5.33 us
    all_to_all x2 -> x1, blocking collectives: 32.5 us -> 6.43 us  [share(): return lax.all_to_all(wide, axes, 0, 0)]
    unnamed x84 -> x14, local copies, waits for them, and re-layouts: 27.1 us -> 1.55 us
    all_to_all x0 -> x1, blocking collectives: none -> 14.7 us  [shards(): part = jnp.sum(lax.all_to_all(wide, ('y', 'x', 'core'), 0, 0), axis=0)]
    ppermute x9, waiting for transfers between devices: 13.2 us -> 0.03 us  [from_x(): return lax.ppermute(a, 'x', [((i + step) % 4, i) for i in range(4)])]
    all_to_all x2 -> x1, starting transfers between devices: 19.7 us -> 9.04 us  [share(): return lax.all_to_all(wide, axes, 0, 0)]
    ppermute x1, starting transfers between devices: 18.3 us -> 13.9 us  [shards(): before = lax.ppermute(gc[BLOCK - 8:], ring, [(i, i + 1) for i in range(15)])]
    ppermute x7 -> x6, waiting for transfers between devices: 6.87 us -> 10.8 us  [swap(): return lax.ppermute(a, axis, [(0, 1), (1, 0)])]
    concatenate x3 -> x2, other arithmetic: 3.04 us -> 0.09 us  [the longest x1 0.05 us: shards(): c0 = jnp.concatenate([sig] + near, axis=0)]
  transfers between devices with their start and end apart: 20 -> 18, of which waited for: 7 -> 3; matrix products, arithmetic and copies ran while one was open for 5% -> 3% of each run, Pallas kernels for 10% -> 13%
where the time goes in v2:
time: 190 us; the launch traced here: 189 us
  starting transfers between devices  97.4 us (51%)
  Pallas kernels  35.6 us (19%)
  waiting for transfers between devices  24.9 us (13%)
  blocking collectives  22.9 us (12%)
  other arithmetic  5.33 us (3%)
  local copies, waits for them, and re-layouts  2.25 us (1%)
    ppermute x6, starting transfers between devices, swap(): return lax.ppermute(a, axis, [(0, 1), (1, 0)])  44.9 us
    pallas_call x5, Pallas kernels, call(): pl.pallas_call(body, out_shape=out_shape, in_specs=specs, out_specs=outs,...  35.6 us
    ppermute x9, starting transfers between devices, from_x(): return lax.ppermute(a, 'x', [((i + step) % 4, i) for i in range(4)])  27.6 us
    all_to_all x1, blocking collectives, shards(): part = jnp.sum(lax.all_to_all(wide, ('y', 'x', 'core'), 0, 0), axis=0)  14.7 us
    ppermute x1, waiting for transfers between devices, shards(): after = lax.ppermute(gc[:8], ring, [(i + 1, i) for i in range(15)])  14 us
    ppermute x1, starting transfers between devices, shards(): before = lax.ppermute(gc[BLOCK - 8:], ring, [(i, i + 1) for i in range(15)])  13.9 us
    ppermute x6, waiting for transfers between devices, swap(): return lax.ppermute(a, axis, [(0, 1), (1, 0)])  10.8 us
    all_to_all x1, starting transfers between devices, share(): return lax.all_to_all(wide, axes, 0, 0)  9.04 us
  transfers between devices with their start and end apart: 18, of which 3 were waited for; matrix products, arithmetic and copies ran while one was open for 3% of the time, Pallas kernels for 13%

profile of v2, /device:TPU:7, one launch (start us, length us, event | category | flops | bytes accessed | tf_op | source)
XLA Modules:
  0.0 189.4 jit_solution(189841101827278421)
XLA Ops:
  0.6 15.4 %collective-permute-start = (bf16[128,768]{1,0:T(8,128)(2,1)}, bf16[128,768]{1,0:T(8,128)(2,1)}, u32[]{:S(2)}, u32[]{:S(2)}) collective-permute-start(bf16[128,768]{1,0:T(8,128)(2,1)} %bitcast.11), channel_id=1, source_target_pairs={{0,8},{8,0},{1,9},{9,1},{2,10},{10,2},{3,11},{11,3},{4,12},{12,4},... | collective-permute-start | bytes 589832 | tf_op jit(solution)/shard_map/ppermute | solution.py:276
  16.1 2.5 %collective-permute-start.1 = (bf16[128,768]{1,0:T(8,128)(2,1)}, bf16[128,768]{1,0:T(8,128)(2,1)S(1)}, u32[]{:S(2)}, u32[]{:S(2)}) collective-permute-start(bf16[128,768]{1,0:T(8,128)(2,1)} %bitcast.12), channel_id=1, source_target_pairs={{2,0},{4,2},{6,4},{0,6},{3,1},{5,3},{7,5},{1,7},{10,8},{12,10},{14... | collective-permute-start | bytes 589832 | tf_op jit(solution)/shard_map/ppermute | solution.py:280
  18.5 2.7 %collective-permute-start.2 = (bf16[128,768]{1,0:T(8,128)(2,1)}, bf16[128,768]{1,0:T(8,128)(2,1)S(1)}, u32[]{:S(2)}, u32[]{:S(2)}) collective-permute-start(bf16[128,768]{1,0:T(8,128)(2,1)} %bitcast.13), channel_id=1, source_target_pairs={{4,0},{6,2},{0,4},{2,6},{5,1},{7,3},{1,5},{3,7},{12,8},{14,10},{8,... | collective-permute-start | bytes 589832 | tf_op jit(solution)/shard_map/ppermute | solution.py:280
  21.3 3.7 %collective-permute-start.3 = (bf16[128,768]{1,0:T(8,128)(2,1)}, bf16[128,768]{1,0:T(8,128)(2,1)S(1)}, u32[]{:S(2)}, u32[]{:S(2)}) collective-permute-start(bf16[128,768]{1,0:T(8,128)(2,1)} %bitcast.14), channel_id=1, source_target_pairs={{6,0},{0,2},{2,4},{4,6},{7,1},{1,3},{3,5},{5,7},{14,8},{8,10},{10,... | collective-permute-start | bytes 589832 | tf_op jit(solution)/shard_map/ppermute | solution.py:280
  26.6 3.8 %collective-permute-start.7 = (bf16[128,384]{1,0:T(8,128)(2,1)}, bf16[128,384]{1,0:T(8,128)(2,1)S(1)}, u32[]{:S(2)}, u32[]{:S(2)}) collective-permute-start(bf16[128,384]{1,0:T(8,128)(2,1)} %broadcast_select_fusion.8), channel_id=1, source_target_pairs={{0,1},{1,0},{2,3},{3,2},{4,5},{5,4},{6,7},{7,6},{8,9},{9,8},{10,11... | collective-permute-start | bytes 294920 | tf_op jit(solution)/shard_map/ppermute | solution.py:276
  32.5 2.1 %collective-permute-start.4 = (bf16[128,768]{1,0:T(8,128)(2,1)}, bf16[128,768]{1,0:T(8,128)(2,1)S(1)}, u32[]{:S(2)}, u32[]{:S(2)}) collective-permute-start(bf16[128,768]{1,0:T(8,128)(2,1)} %collective-permute-done), channel_id=1, source_target_pairs={{2,0},{4,2},{6,4},{0,6},{3,1},{5,3},{7,5},{1,7},{10,8},{12,10},{14... | collective-permute-start | bytes 589832 | tf_op jit(solution)/shard_map/ppermute | solution.py:280
  34.6 4.9 %collective-permute-start.5 = (bf16[128,768]{1,0:T(8,128)(2,1)}, bf16[128,768]{1,0:T(8,128)(2,1)S(1)}, u32[]{:S(2)}, u32[]{:S(2)}) collective-permute-start(bf16[128,768]{1,0:T(8,128)(2,1)} %collective-permute-done), channel_id=1, source_target_pairs={{4,0},{6,2},{0,4},{2,6},{5,1},{7,3},{1,5},{3,7},{12,8},{14,10},{8,... | collective-permute-start | bytes 589832 | tf_op jit(solution)/shard_map/ppermute | solution.py:280
  39.5 2.7 %collective-permute-start.6 = (bf16[128,768]{1,0:T(8,128)(2,1)}, bf16[128,768]{1,0:T(8,128)(2,1)S(1)}, u32[]{:S(2)}, u32[]{:S(2)}) collective-permute-start(bf16[128,768]{1,0:T(8,128)(2,1)} %collective-permute-done), channel_id=1, source_target_pairs={{6,0},{0,2},{2,4},{4,6},{7,1},{1,3},{3,5},{5,7},{14,8},{8,10},{10,... | collective-permute-start | bytes 589832 | tf_op jit(solution)/shard_map/ppermute | solution.py:280
  42.3 2.1 %collective-permute-start.8 = (bf16[128,768]{1,0:T(8,128)(2,1)S(1)}, bf16[128,768]{1,0:T(8,128)(2,1)S(1)}, u32[]{:S(2)}, u32[]{:S(2)}) collective-permute-start(bf16[128,768]{1,0:T(8,128)(2,1)S(1)} %pad_maximum_fusion.4.d0), channel_id=1, source_target_pairs={{0,8},{8,0},{1,9},{9,1},{2,10},{10,2},{3,11},{11,3},{4,12},{12,4},... | collective-permute-start | bytes 589832 | tf_op jit(solution)/shard_map/ppermute | solution.py:276
  44.4 3.1 %collective-permute-start.9 = (bf16[512,768]{1,0:T(8,128)(2,1)S(1)}, bf16[512,768]{1,0:T(8,128)(2,1)S(1)}, u32[]{:S(2)}, u32[]{:S(2)}) collective-permute-start(bf16[512,768]{1,0:T(8,128)(2,1)S(1)} %pad_maximum_fusion.2.c0), channel_id=1, source_target_pairs={{0,1},{1,0},{2,3},{3,2},{4,5},{5,4},{6,7},{7,6},{8,9},{9,8},{10,11... | collective-permute-start | bytes 2359304 | tf_op jit(solution)/shard_map/ppermute | solution.py:276
  48.4 9.8 %collective-permute-done.8.d4 = bf16[128,768]{1,0:T(8,128)(2,1)S(1)} collective-permute-done((bf16[128,768]{1,0:T(8,128)(2,1)S(1)}, bf16[128,768]{1,0:T(8,128)(2,1)S(1)}, u32[]{:S(2)}, u32[]{:S(2)}) %collective-permute-start.8) | collective-permute-done | bytes 196640 | tf_op jit(solution)/shard_map/ppermute | solution.py:276
  58.3 16.6 %collective-permute-start.10 = (bf16[512,768]{1,0:T(8,128)(2,1)S(1)}, bf16[512,768]{1,0:T(8,128)(2,1)S(1)}, u32[]{:S(2)}, u32[]{:S(2)}) collective-permute-start(bf16[512,768]{1,0:T(8,128)(2,1)S(1)} %constant_dynamic-update-slice_fusion.c1), channel_id=1, source_target_pairs={{0,1},{1,0},{2,3},{3,2},{4,5},{5,4},{6,7},{7,6},{8,9},{9,8},{10,11... | collective-permute-start | bytes 2359304 | tf_op jit(solution)/shard_map/ppermute | solution.py:276
  75.1 2.7 %collective-permute-start.11 = (bf16[256,768]{1,0:T(8,128)(2,1)S(1)}, bf16[256,768]{1,0:T(8,128)(2,1)S(1)}, u32[]{:S(2)}, u32[]{:S(2)}) collective-permute-start(bf16[256,768]{1,0:T(8,128)(2,1)S(1)} %pad_maximum_fusion.3), channel_id=1, source_target_pairs={{2,0},{4,2},{6,4},{0,6},{3,1},{5,3},{7,5},{1,7},{10,8},{12,10},{14... | collective-permute-start | bytes 1179656 | tf_op jit(solution)/shard_map/ppermute | solution.py:280
  79.7 4.3 %collective-permute-start.13 = (bf16[256,768]{1,0:T(8,128)(2,1)S(1)}, bf16[256,768]{1,0:T(8,128)(2,1)S(1)}, u32[]{:S(2)}, u32[]{:S(2)}) collective-permute-start(bf16[256,768]{1,0:T(8,128)(2,1)S(1)} %pad_maximum_fusion.3), channel_id=1, source_target_pairs={{6,0},{0,2},{2,4},{4,6},{7,1},{1,3},{3,5},{5,7},{14,8},{8,10},{10,... | collective-permute-start | bytes 1179656 | tf_op jit(solution)/shard_map/ppermute | solution.py:280
  84.8 13.9 %shard_map.94 = (bf16[3,2048,128]{2,1,0:T(8,128)(2,1)S(1)}, bf16[3,2048,128]{2,1,0:T(8,128)(2,1)S(1)}, bf16[3,2048,128]{2,1,0:T(8,128)(2,1)S(1)}, bf16[160,768]{1,0:T(8,128)(2,1)S(1)}) custom-call(s32[3]{0:T(128)S(1)} %pad_add_fusion.pos, bf16[512,768]{1,0:T(8,128)(2,1)S(1)} %pad_maximum_fusion.2.c0, ...), custom_call_target="tpu_custom_call" | custom-call | tf_op jit(solution)/shard_map/pallas_call | solution.py:40
  98.7 9.0 %shard_map.95 = (bf16[3,256,128]{2,1,0:T(8,128)(2,1)S(1)}, f32[8,512]{1,0:T(8,128)S(1)}) custom-call(bf16[3,2048,128]{2,1,0:T(8,128)(2,1)S(1)} %get-tuple-element.35.q, bf16[3,2048,128]{2,1,0:T(8,128)(2,1)S(1)} %get-tuple-element.36.k, bf16[3,2048,128]{2,1,0:T(8,128)(2,1)S(1)} %get-tuple-element.37.v, bf16[128,768]{1,0:T(8,128)(2,1)S(1)} %pad_maximum_fusion.4.d0, ...), custom_call_target="tpu_custom_call" | custom-call | tf_op jit(solution)/shard_map/pallas_call | solution.py:40
  107.8 6.4 %all_to_all.15.stats = f32[4,8,512]{2,1,0:T(8,128)S(1)} all-to-all(f32[4,8,512]{2,1,0:T(8,128)S(1)} %broadcast_in_dim.8), channel_id=1, replica_groups=mesh['y'=4,'zm'=2,'zl'=4,'zh'=2,'x'=4,'core'=2] {'x'}, dimensions={0} | all-to-all | bytes 131072 | tf_op jit(solution)/shard_map/all_to_all | solution.py:285
  114.2 9.3 %shard_map.96 = (bf16[128,1152]{1,0:T(8,128)(2,1)S(1)}, bf16[128,1152]{1,0:T(8,128)(2,1)S(1)}) custom-call(s32[3]{0:T(128)S(1)} %pad_add_fusion.pos, bf16[3,2048,128]{2,1,0:T(8,128)(2,1)S(1)} %get-tuple-element.35.q, bf16[3,2048,128]{2,1,0:T(8,128)(2,1)S(1)} %get-tuple-element.36.k, bf16[3,2048,128]{2,1,0:T(8,128)(2,1)S(1)} %get-tuple-element.37.v, ...), custom_call_target="tpu_custom_call" | custom-call | tf_op jit(solution)/shard_map/pallas_call | solution.py:40
  123.5 3.9 %collective-permute-start.14 = (bf16[128,1152]{1,0:T(8,128)(2,1)S(1)}, bf16[128,1152]{1,0:T(8,128)(2,1)S(1)}, u32[]{:S(2)}, u32[]{:S(2)}) collective-permute-start(bf16[128,1152]{1,0:T(8,128)(2,1)S(1)} %get-tuple-element.46), channel_id=1, source_target_pairs={{0,1},{1,0},{2,3},{3,2},{4,5},{5,4},{6,7},{7,6},{8,9},{9,8},{10,11... | collective-permute-start | bytes 884744 | tf_op jit(solution)/shard_map/ppermute | solution.py:276
  128.6 2.0 %shard_map.97 = (f32[128,768]{1,0:T(8,128)S(1)}, f32[128,768]{1,0:T(8,128)S(1)}, f32[2,16,128]{2,1,0:T(8,128)S(1)}) custom-call(bf16[128,1152]{1,0:T(8,128)(2,1)S(1)} %get-tuple-element.45.mine, bf16[128,1152]{1,0:T(8,128)(2,1)S(1)} %collective-permute-done.14.recv, bf16[768,1152]{1,0:T(8,128)(2,1)S(1)} %pad_maximum_fusion.w.w_own, ...), custom_call_target="tpu_custom_call" | custom-call | tf_op jit(solution)/shard_map/pallas_call | solution.py:40
  130.6 14.7 %all_to_all.16 = f32[32,16,128]{2,1,0:T(8,128)S(1)} all-to-all(f32[32,16,128]{2,1,0:T(8,128)S(1)} %bitcast.8), channel_id=1, replica_groups=mesh['y'=4,'zm'=2,'zl'=4,'zh'=2,'x'=4,'core'=2] {'y','x','core'}, dimensions={0} | all-to-all | bytes 524288 | tf_op jit(solution)/shard_map/all_to_all | solution.py:369
  146.0 9.0 %all-to-all-start.2 = ((bf16[16,16,128]{2,1,0:T(8,128)(2,1)}), bf16[16,16,128]{2,1,0:T(8,128)(2,1)S(1)}, u32[]{:S(2)}, u32[]{:S(2)}) async-start(bf16[16,16,128]{2,1,0:T(8,128)(2,1)} %broadcast_in_dim.11), calls=%async_computation.2 | async-start | bytes 131072 | tf_op jit(solution)/shard_map/all_to_all | solution.py:285
  155.0 13.9 %collective-permute-start.15 = (f32[8,768]{1,0:T(8,128)S(1)}, f32[8,768]{1,0:T(8,128)S(1)}, u32[]{:S(2)}, u32[]{:S(2)}) collective-permute-start(f32[8,768]{1,0:T(8,128)S(1)} %get-tuple-element.58), channel_id=1, source_target_pairs={{0,1},{1,2},{2,3},{3,4},{4,5},{5,6},{6,7},{7,8},{8,9},{9,10},{10,1... | collective-permute-start | bytes 73736 | tf_op jit(solution)/shard_map/ppermute | solution.py:360
  170.9 14.0 %collective-permute-done.16.after = f32[8,768]{1,0:T(8,128)S(1)} collective-permute-done((f32[8,768]{1,0:T(8,128)S(1)}, f32[8,768]{1,0:T(8,128)S(1)}, u32[]{:S(2)}, u32[]{:S(2)}) %collective-permute-start.16) | collective-permute-done | bytes 24608 | tf_op jit(solution)/shard_map/ppermute | solution.py:361
  (57 shorter events, 15.7 us)
Async XLA Ops:
  0.6 31.8 %collective-permute-start = (bf16[128,768]{1,0:T(8,128)(2,1)}, bf16[128,768]{1,0:T(8,128)(2,1)}, u32[]{:S(2)}, u32[]{:S(2)}) collective-permute-start(bf16[128,768]{1,0:T(8,128)(2,1)} %bitcast.11), channel_id=1, source_target_pairs={{0,8},{8,0},{1,9},{9,1},{2,10},{10,2},{3,11},{11,3},{4,12},{12,4},... | collective-permute-start | bytes 589832 | tf_op jit(solution)/shard_map/ppermute | solution.py:276
  16.1 16.4 %collective-permute-start.1 = (bf16[128,768]{1,0:T(8,128)(2,1)}, bf16[128,768]{1,0:T(8,128)(2,1)S(1)}, u32[]{:S(2)}, u32[]{:S(2)}) collective-permute-start(bf16[128,768]{1,0:T(8,128)(2,1)} %bitcast.12), channel_id=1, source_target_pairs={{2,0},{4,2},{6,4},{0,6},{3,1},{5,3},{7,5},{1,7},{10,8},{12,10},{14... | collective-permute-start | bytes 589832 | tf_op jit(solution)/shard_map/ppermute | solution.py:280
  18.5 13.9 %collective-permute-start.2 = (bf16[128,768]{1,0:T(8,128)(2,1)}, bf16[128,768]{1,0:T(8,128)(2,1)S(1)}, u32[]{:S(2)}, u32[]{:S(2)}) collective-permute-start(bf16[128,768]{1,0:T(8,128)(2,1)} %bitcast.13), channel_id=1, source_target_pairs={{4,0},{6,2},{0,4},{2,6},{5,1},{7,3},{1,5},{3,7},{12,8},{14,10},{8,... | collective-permute-start | bytes 589832 | tf_op jit(solution)/shard_map/ppermute | solution.py:280
  21.3 11.2 %collective-permute-start.3 = (bf16[128,768]{1,0:T(8,128)(2,1)}, bf16[128,768]{1,0:T(8,128)(2,1)S(1)}, u32[]{:S(2)}, u32[]{:S(2)}) collective-permute-start(bf16[128,768]{1,0:T(8,128)(2,1)} %bitcast.14), channel_id=1, source_target_pairs={{6,0},{0,2},{2,4},{4,6},{7,1},{1,3},{3,5},{5,7},{14,8},{8,10},{10,... | collective-permute-start | bytes 589832 | tf_op jit(solution)/shard_map/ppermute | solution.py:280
  26.6 5.7 %copy-start.4 = (f32[768]{0:T(1024)S(1)}, f32[768]{0:T(1024)}, u32[]{:S(2)}) copy-start(f32[768]{0:T(1024)} %param.8) | copy-start | bytes 9220
  26.6 5.7 %copy-start.2 = (bf16[1,128,768]{2,1,0:T(8,128)(2,1)S(1)}, bf16[1,128,768]{2,1,0:T(8,128)(2,1)}, u32[]{:S(2)}) copy-start(bf16[1,128,768]{2,1,0:T(8,128)(2,1)} %param.13) | copy-start | bytes 589828
  26.6 17.7 %copy-start.3 = (bf16[1,128,768]{2,1,0:T(8,128)(2,1)S(1)}, bf16[1,128,768]{2,1,0:T(8,128)(2,1)}, u32[]{:S(2)}) copy-start(bf16[1,128,768]{2,1,0:T(8,128)(2,1)} %param.7) | copy-start | bytes 589828
  26.6 5.7 %collective-permute-start.7 = (bf16[128,384]{1,0:T(8,128)(2,1)}, bf16[128,384]{1,0:T(8,128)(2,1)S(1)}, u32[]{:S(2)}, u32[]{:S(2)}) collective-permute-start(bf16[128,384]{1,0:T(8,128)(2,1)} %broadcast_select_fusion.8), channel_id=1, source_target_pairs={{0,1},{1,0},{2,3},{3,2},{4,5},{5,4},{6,7},{7,6},{8,9},{9,8},{10,11... | collective-permute-start | bytes 294920 | tf_op jit(solution)/shard_map/ppermute | solution.py:276
  32.4 42.5 %copy-start.1 = (bf16[768,768]{1,0:T(8,128)(2,1)S(1)}, bf16[768,768]{1,0:T(8,128)(2,1)}, u32[]{:S(2)}) copy-start(bf16[768,768]{1,0:T(8,128)(2,1)} %param.10) | copy-start | bytes 3538948
  32.5 25.8 %collective-permute-start.4 = (bf16[128,768]{1,0:T(8,128)(2,1)}, bf16[128,768]{1,0:T(8,128)(2,1)S(1)}, u32[]{:S(2)}, u32[]{:S(2)}) collective-permute-start(bf16[128,768]{1,0:T(8,128)(2,1)} %collective-permute-done), channel_id=1, source_target_pairs={{2,0},{4,2},{6,4},{0,6},{3,1},{5,3},{7,5},{1,7},{10,8},{12,10},{14... | collective-permute-start | bytes 589832 | tf_op jit(solution)/shard_map/ppermute | solution.py:280
  34.6 23.7 %collective-permute-start.5 = (bf16[128,768]{1,0:T(8,128)(2,1)}, bf16[128,768]{1,0:T(8,128)(2,1)S(1)}, u32[]{:S(2)}, u32[]{:S(2)}) collective-permute-start(bf16[128,768]{1,0:T(8,128)(2,1)} %collective-permute-done), channel_id=1, source_target_pairs={{4,0},{6,2},{0,4},{2,6},{5,1},{7,3},{1,5},{3,7},{12,8},{14,10},{8,... | collective-permute-start | bytes 589832 | tf_op jit(solution)/shard_map/ppermute | solution.py:280
  39.5 18.7 %collective-permute-start.6 = (bf16[128,768]{1,0:T(8,128)(2,1)}, bf16[128,768]{1,0:T(8,128)(2,1)S(1)}, u32[]{:S(2)}, u32[]{:S(2)}) collective-permute-start(bf16[128,768]{1,0:T(8,128)(2,1)} %collective-permute-done), channel_id=1, source_target_pairs={{6,0},{0,2},{2,4},{4,6},{7,1},{1,3},{3,5},{5,7},{14,8},{8,10},{10,... | collective-permute-start | bytes 589832 | tf_op jit(solution)/shard_map/ppermute | solution.py:280
  42.3 16.0 %collective-permute-start.8 = (bf16[128,768]{1,0:T(8,128)(2,1)S(1)}, bf16[128,768]{1,0:T(8,128)(2,1)S(1)}, u32[]{:S(2)}, u32[]{:S(2)}) collective-permute-start(bf16[128,768]{1,0:T(8,128)(2,1)S(1)} %pad_maximum_fusion.4.d0), channel_id=1, source_target_pairs={{0,8},{8,0},{1,9},{9,1},{2,10},{10,2},{3,11},{11,3},{4,12},{12,4},... | collective-permute-start | bytes 589832 | tf_op jit(solution)/shard_map/ppermute | solution.py:276
  44.4 39.8 %collective-permute-start.9 = (bf16[512,768]{1,0:T(8,128)(2,1)S(1)}, bf16[512,768]{1,0:T(8,128)(2,1)S(1)}, u32[]{:S(2)}, u32[]{:S(2)}) collective-permute-start(bf16[512,768]{1,0:T(8,128)(2,1)S(1)} %pad_maximum_fusion.2.c0), channel_id=1, source_target_pairs={{0,1},{1,0},{2,3},{3,2},{4,5},{5,4},{6,7},{7,6},{8,9},{9,8},{10,11... | collective-permute-start | bytes 2359304 | tf_op jit(solution)/shard_map/ppermute | solution.py:276
  58.3 25.9 %collective-permute-start.10 = (bf16[512,768]{1,0:T(8,128)(2,1)S(1)}, bf16[512,768]{1,0:T(8,128)(2,1)S(1)}, u32[]{:S(2)}, u32[]{:S(2)}) collective-permute-start(bf16[512,768]{1,0:T(8,128)(2,1)S(1)} %constant_dynamic-update-slice_fusion.c1), channel_id=1, source_target_pairs={{0,1},{1,0},{2,3},{3,2},{4,5},{5,4},{6,7},{7,6},{8,9},{9,8},{10,11... | collective-permute-start | bytes 2359304 | tf_op jit(solution)/shard_map/ppermute | solution.py:276
  75.1 32.7 %collective-permute-start.11 = (bf16[256,768]{1,0:T(8,128)(2,1)S(1)}, bf16[256,768]{1,0:T(8,128)(2,1)S(1)}, u32[]{:S(2)}, u32[]{:S(2)}) collective-permute-start(bf16[256,768]{1,0:T(8,128)(2,1)S(1)} %pad_maximum_fusion.3), channel_id=1, source_target_pairs={{2,0},{4,2},{6,4},{0,6},{3,1},{5,3},{7,5},{1,7},{10,8},{12,10},{14... | collective-permute-start | bytes 1179656 | tf_op jit(solution)/shard_map/ppermute | solution.py:280
  77.7 30.0 %collective-permute-start.12 = (bf16[256,768]{1,0:T(8,128)(2,1)S(1)}, bf16[256,768]{1,0:T(8,128)(2,1)S(1)}, u32[]{:S(2)}, u32[]{:S(2)}) collective-permute-start(bf16[256,768]{1,0:T(8,128)(2,1)S(1)} %pad_maximum_fusion.3), channel_id=1, source_target_pairs={{4,0},{6,2},{0,4},{2,6},{5,1},{7,3},{1,5},{3,7},{12,8},{14,10},{8,... | collective-permute-start | bytes 1179656 | tf_op jit(solution)/shard_map/ppermute | solution.py:280
  79.7 28.1 %collective-permute-start.13 = (bf16[256,768]{1,0:T(8,128)(2,1)S(1)}, bf16[256,768]{1,0:T(8,128)(2,1)S(1)}, u32[]{:S(2)}, u32[]{:S(2)}) collective-permute-start(bf16[256,768]{1,0:T(8,128)(2,1)S(1)} %pad_maximum_fusion.3), channel_id=1, source_target_pairs={{6,0},{0,2},{2,4},{4,6},{7,1},{1,3},{3,5},{5,7},{14,8},{8,10},{10,... | collective-permute-start | bytes 1179656 | tf_op jit(solution)/shard_map/ppermute | solution.py:280
  84.1 0.7 copy-start
  123.5 5.1 %collective-permute-start.14 = (bf16[128,1152]{1,0:T(8,128)(2,1)S(1)}, bf16[128,1152]{1,0:T(8,128)(2,1)S(1)}, u32[]{:S(2)}, u32[]{:S(2)}) collective-permute-start(bf16[128,1152]{1,0:T(8,128)(2,1)S(1)} %get-tuple-element.46), channel_id=1, source_target_pairs={{0,1},{1,0},{2,3},{3,2},{4,5},{5,4},{6,7},{7,6},{8,9},{9,8},{10,11... | collective-permute-start | bytes 884744 | tf_op jit(solution)/shard_map/ppermute | solution.py:276
  146.0 40.3 %all-to-all-start.2 = ((bf16[16,16,128]{2,1,0:T(8,128)(2,1)}), bf16[16,16,128]{2,1,0:T(8,128)(2,1)S(1)}, u32[]{:S(2)}, u32[]{:S(2)}) async-start(bf16[16,16,128]{2,1,0:T(8,128)(2,1)} %broadcast_in_dim.11), calls=%async_computation.2 | async-start | bytes 131072 | tf_op jit(solution)/shard_map/all_to_all | solution.py:285
  155.0 15.9 %collective-permute-start.15 = (f32[8,768]{1,0:T(8,128)S(1)}, f32[8,768]{1,0:T(8,128)S(1)}, u32[]{:S(2)}, u32[]{:S(2)}) collective-permute-start(f32[8,768]{1,0:T(8,128)S(1)} %get-tuple-element.58), channel_id=1, source_target_pairs={{0,1},{1,2},{2,3},{3,4},{4,5},{5,6},{6,7},{7,8},{8,9},{9,10},{10,1... | collective-permute-start | bytes 73736 | tf_op jit(solution)/shard_map/ppermute | solution.py:360
  168.9 16.0 %collective-permute-start.16 = (f32[8,768]{1,0:T(8,128)S(1)}, f32[8,768]{1,0:T(8,128)S(1)}, u32[]{:S(2)}, u32[]{:S(2)}) collective-permute-start(f32[8,768]{1,0:T(8,128)S(1)} %get-tuple-element.57), channel_id=1, source_target_pairs={{1,0},{2,1},{3,2},{4,3},{5,4},{6,5},{7,6},{8,7},{9,8},{10,9},{11,1... | collective-permute-start | bytes 73736 | tf_op jit(solution)/shard_map/ppermute | solution.py:361

commit v3 on v2

--- a/solution.py
+++ b/solution.py
@@ -74,19 +74,19 @@
 
 
 def hidden_body(
-    pos, c0, c1, e0, e1, w, gain, taps, q, k, v, ext, xs, ns, hs
+    pos, near, other, w, gain, taps, q, k, v, ext, xs, ns, hs
 ):
     core = pos[2]
     here = pl.multiple_of(core * BLOCK, BLOCK)
     there = pl.multiple_of((1 - core) * BLOCK, BLOCK)
     for c in range(CHUNKS):
-        own, other = ((c0, e0), (c1, e1))[c // 4]
-        sl = slice((c % 4) * BLOCK, (c % 4 + 1) * BLOCK)
-        xs[c, pl.ds(here, BLOCK), :] = own[sl, :]
-        xs[c, pl.ds(there, BLOCK), :] = other[sl, :]
+        xa = lax.rem(pos[1] + c % 4, 4)
+        sl = slice((c // 4) * BLOCK, (c // 4 + 1) * BLOCK)
+        xs[c, pl.ds(here, BLOCK), :] = near[xa, sl, :]
+        xs[c, pl.ds(there, BLOCK), :] = other[xa, sl, :]
     prev, nxt, prev_ok, nxt_ok = neighbours(pos, jnp.int32(0), jnp.int32(0))
     first = core == 0
-    ext[16:144, :] = c0[0:BLOCK, :]
+    ext[16:144, :] = near[pos[1], 0:BLOCK, :]
 
     @pl.when(first)
     def _():
@@ -221,7 +221,7 @@
     give[...] = gs[pl.ds(there, BLOCK), :]
 
 
-def conv_body(mine, recv, w_own, w_oth, ext, gain, taps, gh, gc, usum, ns):
+def conv_body(pos, mine, recv, w_own, w_oth, ext, gain, taps, gh, gc, usum, inner_edge, outer_edge, ns):
     g = gain[0:1, :]
     for r in range(0, 160, 16):
         ns[r : r + 16, :] = normalize(ext[r : r + 16, :].astype(F32))
@@ -249,12 +249,17 @@
             row = t * OWN_HEADS + slot
             usum[side, row : row + 1, :] = jnp.sum(sums[t], axis=0, keepdims=True)
     usum[:, 15:16, :] = jnp.zeros((2, 1, 128), F32)
-
-
-def final_body(gh, gc, before, after, ext, gain, taps, out, es):
-    es[0:8, :] = before[...]
+    first = pos[2] == 0
+    head, tail = gc[0:8, :], gc[BLOCK - 8 : BLOCK, :]
+    inner_edge[...] = jnp.where(first, tail, head)
+    outer_edge[...] = jnp.where(first, head, tail)
+
+
+def final_body(pos, gh, gc, inside, outside, ext, gain, taps, out, es):
+    first = pos[2] == 0
+    es[0:8, :] = jnp.where(first, outside[...], inside[...])
     es[8:136, :] = gc[...]
-    es[136:144, :] = after[...]
+    es[136:144, :] = jnp.where(first, inside[...], outside[...])
     g = gain[0:1, :]
     tap = [taps[t : t + 1, :] for t in range(5)]
     for r in range(0, BLOCK, 16):
@@ -305,29 +310,24 @@
         [jnp.where(first, keep, got), jnp.where(first, got, keep)], axis=1
     )
     sig_z = swap(sig, "zh")
-    near = [from_x(sig, d) for d in (1, 2, 3)]
-    sig_z, near = lax.optimization_barrier((sig_z, near))
-    cot_z = swap(lax.optimization_barrier((cot_own, sig_z))[0], "zh")
-    far = [from_x(sig_z, d) for d in (1, 2, 3)]
-    c0 = jnp.concatenate([sig] + near, axis=0)
-    e0 = swap(c0, "core")
-    far, cot_z = lax.optimization_barrier((far, cot_z))
-    c1 = jnp.concatenate([sig_z] + far, axis=0)
-    e1 = swap(c1, "core")
-    both = jnp.concatenate([cot_own, cot_z], axis=0)
-    cots = [from_x(both, d) for d in (1, 2, 3)]
-
     parts = [halves(w) for w in (w_query, w_key, w_value)]
     w_own = jnp.concatenate([p[0] for p in parts], axis=1)
     w_oth = jnp.concatenate([p[1] for p in parts], axis=1)
+    sig_z, cot_own, w_own, w_oth = lax.optimization_barrier((sig_z, cot_own, w_own, w_oth))
+    cot_z = swap(cot_own, "zh")
+    near = share(jnp.concatenate([sig, sig_z], axis=0), "x", 4)
+    other = swap(near, "core")
 
     head_shape = jax.ShapeDtypeStruct((OWN_HEADS, BINS, HEAD_DIM), BF16)
     q, k, v, ext = call(
         hidden_body,
         (head_shape, head_shape, head_shape, jax.ShapeDtypeStruct((160, C), BF16)),
-        (pos, c0, c1, e0, e1, w_own, gain, conv_taps),
+        (pos, near, other, w_own, gain, conv_taps),
         (VM((CHUNKS, CHUNK, C), BF16), VM((288, C), F32), VM((CHUNK, C), BF16)),
     )
+    cot_z, q = lax.optimization_barrier((cot_z, q))
+    both = jnp.concatenate([cot_own, cot_z], axis=0)
+    cots = [from_x(both, d) for d in (1, 2, 3)]
     part = jax.ShapeDtypeStruct((OWN_HEADS, CHUNK, HEAD_DIM), BF16)
     dq, stats = call(
         forward_body,
@@ -350,19 +350,20 @@
     )
     recv = swap(give, "core")
     wide = jax.ShapeDtypeStruct((BLOCK, C), F32)
-    gh, gc, usum = call(
+    edge = jax.ShapeDtypeStruct((8, C), F32)
+    gh, gc, usum, inside, outside = call(
         conv_body,
-        (wide, wide, jax.ShapeDtypeStruct((2, 16, 128), F32)),
-        (mine, recv, w_own, w_oth, ext, gain, conv_taps),
+        (wide, wide, jax.ShapeDtypeStruct((2, 16, 128), F32), edge, edge),
+        (pos, mine, recv, w_own, w_oth, ext, gain, conv_taps),
         (VM((160, C), F32),),
     )
-    ring = ("zh", "x", "core")
-    before = lax.ppermute(gc[BLOCK - 8 :], ring, [(i, i + 1) for i in range(15)])
-    after = lax.ppermute(gc[:8], ring, [(i + 1, i) for i in range(15)])
+    inside = swap(inside, "core")
+    pairs = [(i, i + 1) for i in range(1, 15, 2)] + [(i + 1, i) for i in range(1, 15, 2)]
+    outside = lax.ppermute(outside, ("zh", "x", "core"), pairs)
     out = call(
         final_body,
         jax.ShapeDtypeStruct((BLOCK, C), BF16),
-        (gh, gc, before, after, ext, gain, conv_taps),
+        (pos, gh, gc, inside, outside, ext, gain, conv_taps),
         (VM((144, C), F32),),
     )
     wide = jnp.broadcast_to(usum[None], (16, 2, 16, 128)).reshape(32, 16, 128)

time: 190 us -> 195 us (1.026)
  blocking collectives: 22.9 us -> 39.9 us
  waiting for transfers between devices: 24.9 us -> 11.2 us
  starting transfers between devices: 97.4 us -> 90.1 us
  local copies, waits for them, and re-layouts: 2.25 us -> 9.04 us
  Pallas kernels: 35.6 us -> 37.9 us
    all_to_all x1 -> x2, blocking collectives: 6.43 us -> 25.2 us  [share(): return lax.all_to_all(wide, axes, 0, 0)]
    ppermute x9 -> x3, starting transfers between devices: 27.6 us -> 9.59 us  [from_x(): return lax.ppermute(a, 'x', [((i + step) % 4, i) for i in range(4)])]
    ppermute x2 -> x1, waiting for transfers between devices: 14 us -> 2.45 us  [shards(): outside = lax.ppermute(outside, ('zh', 'x', 'core'), pairs)]
    all_to_all x1, starting transfers between devices: 9.04 us -> 20.3 us  [share(): return lax.all_to_all(wide, axes, 0, 0)]
    ppermute x6, waiting for transfers between devices: 10.8 us -> 3.2 us  [swap(): return lax.ppermute(a, axis, [(0, 1), (1, 0)])]
    unnamed x14 -> x34, local copies, waits for them, and re-layouts: 1.55 us -> 8.25 us
    ppermute x9 -> x3, waiting for transfers between devices: 0.03 us -> 5.53 us  [from_x(): return lax.ppermute(a, 'x', [((i + step) % 4, i) for i in range(4)])]
    pallas_call x5, Pallas kernels: 35.6 us -> 37.9 us  [call(): pl.pallas_call(body, out_shape=out_shape, in_specs=specs, out_specs=outs,...]
  transfers between devices with their start and end apart: 18 -> 11, of which waited for: 3 -> 5; matrix products, arithmetic and copies ran while one was open for 3% -> 2% of each run, Pallas kernels for 13% -> 13%
where the time goes in v3:
time: 195 us; the launch traced here: 194 us
  starting transfers between devices  90.1 us (46%)
  blocking collectives  39.9 us (20%)
  Pallas kernels  37.9 us (19%)
  waiting for transfers between devices  11.2 us (6%)
  local copies, waits for them, and re-layouts  9.04 us (5%)
  other arithmetic  5.13 us (3%)
    ppermute x6, starting transfers between devices, swap(): return lax.ppermute(a, axis, [(0, 1), (1, 0)])  46.5 us
    pallas_call x5, Pallas kernels, call(): pl.pallas_call(body, out_shape=out_shape, in_specs=specs, out_specs=outs,...  37.9 us
    all_to_all x2, blocking collectives, share(): return lax.all_to_all(wide, axes, 0, 0)  25.2 us
    all_to_all x1, starting transfers between devices, share(): return lax.all_to_all(wide, axes, 0, 0)  20.3 us
    ppermute x1, starting transfers between devices, shards(): outside = lax.ppermute(outside, ('zh', 'x', 'core'), pairs)  13.7 us
    all_to_all x1, blocking collectives, shards(): part = jnp.sum(lax.all_to_all(wide, ('y', 'x', 'core'), 0, 0), axis=0)  12.9 us
    ppermute x3, starting transfers between devices, from_x(): return lax.ppermute(a, 'x', [((i + step) % 4, i) for i in range(4)])  9.59 us
    unnamed x34, local copies, waits for them, and re-layouts  8.25 us
  transfers between devices with their start and end apart: 11, of which 5 were waited for; matrix products, arithmetic and copies ran while one was open for 2% of the time, Pallas kernels for 13%

profile of v3, /device:TPU:7, one launch (start us, length us, event | category | flops | bytes accessed | tf_op | source)
XLA Modules:
  0.0 194.2 jit_solution(6601036164451601391)
XLA Ops:
  1.8 2.6 %collective-permute-start.1 = (bf16[128,384]{1,0:T(8,128)(2,1)S(1)}, bf16[128,384]{1,0:T(8,128)(2,1)S(1)}, u32[]{:S(2)}, u32[]{:S(2)}) collective-permute-start(bf16[128,384]{1,0:T(8,128)(2,1)S(1)} %broadcast_select_fusion.8), channel_id=1, source_target_pairs={{0,1},{1,0},{2,3},{3,2},{4,5},{5,4},{6,7},{7,6},{8,9},{9,8},{10,11... | collective-permute-start | bytes 294920 | tf_op jit(solution)/shard_map/ppermute | solution.py:281
  4.4 15.4 %collective-permute-start = (bf16[128,768]{1,0:T(8,128)(2,1)}, bf16[128,768]{1,0:T(8,128)(2,1)S(1)}, u32[]{:S(2)}, u32[]{:S(2)}) collective-permute-start(bf16[128,768]{1,0:T(8,128)(2,1)} %bitcast.11), channel_id=1, source_target_pairs={{0,8},{8,0},{1,9},{9,1},{2,10},{10,2},{3,11},{11,3},{4,12},{12,4},... | collective-permute-start | bytes 589832 | tf_op jit(solution)/shard_map/ppermute | solution.py:281
  23.3 2.0 %collective-permute-done = bf16[128,768]{1,0:T(8,128)(2,1)S(1)} collective-permute-done((bf16[128,768]{1,0:T(8,128)(2,1)}, bf16[128,768]{1,0:T(8,128)(2,1)S(1)}, u32[]{:S(2)}, u32[]{:S(2)}) %collective-permute-start) | collective-permute-done | bytes 196640 | tf_op jit(solution)/shard_map/ppermute | solution.py:281
  25.4 16.8 %all_to_all.20.near = bf16[4,256,768]{2,1,0:T(8,128)(2,1)} all-to-all(bf16[4,256,768]{2,1,0:T(8,128)(2,1)S(1)} %broadcast_in_dim.10), channel_id=1, replica_groups=mesh['y'=4,'zm'=2,'zl'=4,'zh'=2,'x'=4,'core'=2] {'x'}, dimensions={0} | all-to-all | bytes 3145728 | tf_op jit(solution)/shard_map/all_to_all | solution.py:290
  42.3 10.1 %collective-permute-start.3 = (bf16[4,256,768]{2,1,0:T(8,128)(2,1)}, bf16[4,256,768]{2,1,0:T(8,128)(2,1)}, u32[]{:S(2)}, u32[]{:S(2)}) collective-permute-start(bf16[4,256,768]{2,1,0:T(8,128)(2,1)} %all_to_all.20.near), channel_id=1, source_target_pairs={{0,1},{1,0},{2,3},{3,2},{4,5},{5,4},{6,7},{7,6},{8,9},{9,8},{10,11... | collective-permute-start | bytes 4718600 | tf_op jit(solution)/shard_map/ppermute | solution.py:281
  52.4 12.5 %collective-permute-start.2 = (bf16[128,768]{1,0:T(8,128)(2,1)}, bf16[128,768]{1,0:T(8,128)(2,1)S(1)}, u32[]{:S(2)}, u32[]{:S(2)}) collective-permute-start(bf16[128,768]{1,0:T(8,128)(2,1)} %pad_maximum_fusion.3.d0), channel_id=1, source_target_pairs={{0,8},{8,0},{1,9},{9,1},{2,10},{10,2},{3,11},{11,3},{4,12},{12,4},... | collective-permute-start | bytes 589832 | tf_op jit(solution)/shard_map/ppermute | solution.py:281
  66.8 15.1 %shard_map.94 = (bf16[3,2048,128]{2,1,0:T(8,128)(2,1)S(1)}, bf16[3,2048,128]{2,1,0:T(8,128)(2,1)S(1)}, bf16[3,2048,128]{2,1,0:T(8,128)(2,1)S(1)}, bf16[160,768]{1,0:T(8,128)(2,1)S(1)}) custom-call(s32[3]{0:T(128)S(1)} %pad_add_fusion.pos, bf16[4,256,768]{2,1,0:T(8,128)(2,1)} %all_to_all.20.near, bf16[4,256,768]{2,1,0:T(8,128)(2,1)} %collective-permute-done.3.other, ...), custom_call_target="tpu_custom_call" | custom-call | tf_op jit(solution)/shard_map/pallas_call | solution.py:40
  81.9 1.9 collective-permute-start.4
  83.9 4.9 %collective-permute-start.5 = (bf16[256,768]{1,0:T(8,128)(2,1)S(1)}, bf16[256,768]{1,0:T(8,128)(2,1)S(1)}, u32[]{:S(2)}, u32[]{:S(2)}) collective-permute-start(bf16[256,768]{1,0:T(8,128)(2,1)S(1)} %constant_dynamic-update-slice_fusion), channel_id=1, source_target_pairs={{4,0},{6,2},{0,4},{2,6},{5,1},{7,3},{1,5},{3,7},{12,8},{14,10},{8,... | collective-permute-start | bytes 1179656 | tf_op jit(solution)/shard_map/ppermute | solution.py:285
  88.7 2.8 %collective-permute-start.6 = (bf16[256,768]{1,0:T(8,128)(2,1)S(1)}, bf16[256,768]{1,0:T(8,128)(2,1)S(1)}, u32[]{:S(2)}, u32[]{:S(2)}) collective-permute-start(bf16[256,768]{1,0:T(8,128)(2,1)S(1)} %constant_dynamic-update-slice_fusion), channel_id=1, source_target_pairs={{6,0},{0,2},{2,4},{4,6},{7,1},{1,3},{3,5},{5,7},{14,8},{8,10},{10,... | collective-permute-start | bytes 1179656 | tf_op jit(solution)/shard_map/ppermute | solution.py:285
  91.6 9.0 %shard_map.95 = (bf16[3,256,128]{2,1,0:T(8,128)(2,1)S(1)}, f32[8,512]{1,0:T(8,128)S(1)}) custom-call(bf16[3,2048,128]{2,1,0:T(8,128)(2,1)S(1)} %get-tuple-element.30.q, bf16[3,2048,128]{2,1,0:T(8,128)(2,1)S(1)} %get-tuple-element.31.k, bf16[3,2048,128]{2,1,0:T(8,128)(2,1)S(1)} %get-tuple-element.32.v, bf16[128,768]{1,0:T(8,128)(2,1)S(1)} %copy-done, ...), custom_call_target="tpu_custom_call" | custom-call | tf_op jit(solution)/shard_map/pallas_call | solution.py:40
  100.6 3.6 %collective-permute-done.5.b2 = bf16[256,768]{1,0:T(8,128)(2,1)S(1)} collective-permute-done((bf16[256,768]{1,0:T(8,128)(2,1)S(1)}, bf16[256,768]{1,0:T(8,128)(2,1)S(1)}, u32[]{:S(2)}, u32[]{:S(2)}) %collective-permute-start.5) | collective-permute-done | bytes 393248 | tf_op jit(solution)/shard_map/ppermute | solution.py:285
  104.2 1.9 collective-permute-done.6.b3
  106.1 8.3 %all_to_all.21.stats = f32[4,8,512]{2,1,0:T(8,128)S(1)} all-to-all(f32[4,8,512]{2,1,0:T(8,128)S(1)} %broadcast_in_dim.11), channel_id=1, replica_groups=mesh['y'=4,'zm'=2,'zl'=4,'zh'=2,'x'=4,'core'=2] {'x'}, dimensions={0} | all-to-all | bytes 131072 | tf_op jit(solution)/shard_map/all_to_all | solution.py:290
  114.4 9.3 %shard_map.96 = (bf16[128,1152]{1,0:T(8,128)(2,1)S(1)}, bf16[128,1152]{1,0:T(8,128)(2,1)S(1)}) custom-call(s32[3]{0:T(128)S(1)} %pad_add_fusion.pos, bf16[3,2048,128]{2,1,0:T(8,128)(2,1)S(1)} %get-tuple-element.30.q, bf16[3,2048,128]{2,1,0:T(8,128)(2,1)S(1)} %get-tuple-element.31.k, bf16[3,2048,128]{2,1,0:T(8,128)(2,1)S(1)} %get-tuple-element.32.v, ...), custom_call_target="tpu_custom_call" | custom-call | tf_op jit(solution)/shard_map/pallas_call | solution.py:40
  123.7 3.7 %collective-permute-start.7 = (bf16[128,1152]{1,0:T(8,128)(2,1)S(1)}, bf16[128,1152]{1,0:T(8,128)(2,1)S(1)}, u32[]{:S(2)}, u32[]{:S(2)}) collective-permute-start(bf16[128,1152]{1,0:T(8,128)(2,1)S(1)} %get-tuple-element.41), channel_id=1, source_target_pairs={{0,1},{1,0},{2,3},{3,2},{4,5},{5,4},{6,7},{7,6},{8,9},{9,8},{10,11... | collective-permute-start | bytes 884744 | tf_op jit(solution)/shard_map/ppermute | solution.py:281
  128.6 2.5 %shard_map.97 = (f32[128,768]{1,0:T(8,128)S(1)}, f32[128,768]{1,0:T(8,128)S(1)}, f32[2,16,128]{2,1,0:T(8,128)S(1)}, f32[8,768]{1,0:T(8,128)S(1)}, f32[8,768]{1,0:T(8,128)S(1)}) custom-call(s32[3]{0:T(128)S(1)} %pad_add_fusion.pos, bf16[128,1152]{1,0:T(8,128)(2,1)S(1)} %get-tuple-element.40.mine, bf16[128,1152]{1,0:T(8,128)(2,1)S(1)} %collective-permute-done.7.recv, ...), custom_call_target="tpu_custom_call" | custom-call | tf_op jit(solution)/shard_map/pallas_call | solution.py:40
  133.3 12.9 %all_to_all.22 = f32[32,16,128]{2,1,0:T(8,128)S(1)} all-to-all(f32[32,16,128]{2,1,0:T(8,128)S(1)} %bitcast.8), channel_id=1, replica_groups=mesh['y'=4,'zm'=2,'zl'=4,'zh'=2,'x'=4,'core'=2] {'y','x','core'}, dimensions={0} | all-to-all | bytes 524288 | tf_op jit(solution)/shard_map/all_to_all | solution.py:370
  146.9 20.3 %all-to-all-start.3 = ((bf16[16,16,128]{2,1,0:T(8,128)(2,1)}), bf16[16,16,128]{2,1,0:T(8,128)(2,1)S(1)}, u32[]{:S(2)}, u32[]{:S(2)}) async-start(bf16[16,16,128]{2,1,0:T(8,128)(2,1)} %broadcast_in_dim.14), calls=%async_computation.3 | async-start | bytes 131072 | tf_op jit(solution)/shard_map/all_to_all | solution.py:290
  167.2 2.1 %collective-permute-start.8 = (f32[8,768]{1,0:T(8,128)}, f32[8,768]{1,0:T(8,128)S(1)}, u32[]{:S(2)}, u32[]{:S(2)}) collective-permute-start(f32[8,768]{1,0:T(8,128)} %copy-done.10), channel_id=1, source_target_pairs={{0,1},{1,0},{2,3},{3,2},{4,5},{5,4},{6,7},{7,6},{8,9},{9,8},{10,11... | collective-permute-start | bytes 73736 | tf_op jit(solution)/shard_map/ppermute | solution.py:281
  169.4 13.7 %collective-permute-start.9 = (f32[8,768]{1,0:T(8,128)}, f32[8,768]{1,0:T(8,128)S(1)}, u32[]{:S(2)}, u32[]{:S(2)}) collective-permute-start(f32[8,768]{1,0:T(8,128)} %copy-done.9), channel_id=1, source_target_pairs={{1,2},{3,4},{5,6},{7,8},{9,10},{11,12},{13,14},{2,1},{4,3},{6,5},{... | collective-permute-start | bytes 73736 | tf_op jit(solution)/shard_map/ppermute | solution.py:362
  183.1 2.5 %collective-permute-done.9.outside = f32[8,768]{1,0:T(8,128)S(1)} collective-permute-done((f32[8,768]{1,0:T(8,128)}, f32[8,768]{1,0:T(8,128)S(1)}, u32[]{:S(2)}, u32[]{:S(2)}) %collective-permute-start.9) | collective-permute-done | bytes 24608 | tf_op jit(solution)/shard_map/ppermute | solution.py:362
  189.2 1.9 shard_map.98
  191.2 1.8 all-gather
  (63 shorter events, 15.4 us)
Async XLA Ops:
  0.6 20.5 %copy-start.11 = (bf16[768,768]{1,0:T(8,128)(2,1)S(1)}, bf16[768,768]{1,0:T(8,128)(2,1)}, u32[]{:S(2)}) copy-start(bf16[768,768]{1,0:T(8,128)(2,1)} %param.12) | copy-start | bytes 3538948
  0.6 20.5 %copy-start.12 = (bf16[768,768]{1,0:T(8,128)(2,1)S(1)}, bf16[768,768]{1,0:T(8,128)(2,1)}, u32[]{:S(2)}) copy-start(bf16[768,768]{1,0:T(8,128)(2,1)} %param.11) | copy-start | bytes 3538948
  1.8 20.0 %collective-permute-start.1 = (bf16[128,384]{1,0:T(8,128)(2,1)S(1)}, bf16[128,384]{1,0:T(8,128)(2,1)S(1)}, u32[]{:S(2)}, u32[]{:S(2)}) collective-permute-start(bf16[128,384]{1,0:T(8,128)(2,1)S(1)} %broadcast_select_fusion.8), channel_id=1, source_target_pairs={{0,1},{1,0},{2,3},{3,2},{4,5},{5,4},{6,7},{7,6},{8,9},{9,8},{10,11... | collective-permute-start | bytes 294920 | tf_op jit(solution)/shard_map/ppermute | solution.py:281
  4.4 20.9 %collective-permute-start = (bf16[128,768]{1,0:T(8,128)(2,1)}, bf16[128,768]{1,0:T(8,128)(2,1)S(1)}, u32[]{:S(2)}, u32[]{:S(2)}) collective-permute-start(bf16[128,768]{1,0:T(8,128)(2,1)} %bitcast.11), channel_id=1, source_target_pairs={{0,8},{8,0},{1,9},{9,1},{2,10},{10,2},{3,11},{11,3},{4,12},{12,4},... | collective-permute-start | bytes 589832 | tf_op jit(solution)/shard_map/ppermute | solution.py:281
  21.6 0.9 copy-start.13
  21.6 3.6 %copy-start.14 = (bf16[1,128,768]{2,1,0:T(8,128)(2,1)S(1)}, bf16[1,128,768]{2,1,0:T(8,128)(2,1)}, u32[]{:S(2)}) copy-start(bf16[1,128,768]{2,1,0:T(8,128)(2,1)} %param.7) | copy-start | bytes 589828
  25.4 27.0 %copy-start.15 = (f32[768]{0:T(1024)S(1)}, f32[768]{0:T(1024)}, u32[]{:S(2)}) copy-start(f32[768]{0:T(1024)} %param.8) | copy-start | bytes 9220
  42.3 23.7 %collective-permute-start.3 = (bf16[4,256,768]{2,1,0:T(8,128)(2,1)}, bf16[4,256,768]{2,1,0:T(8,128)(2,1)}, u32[]{:S(2)}, u32[]{:S(2)}) collective-permute-start(bf16[4,256,768]{2,1,0:T(8,128)(2,1)} %all_to_all.20.near), channel_id=1, source_target_pairs={{0,1},{1,0},{2,3},{3,2},{4,5},{5,4},{6,7},{7,6},{8,9},{9,8},{10,11... | collective-permute-start | bytes 4718600 | tf_op jit(solution)/shard_map/ppermute | solution.py:281
  52.4 29.5 %collective-permute-start.2 = (bf16[128,768]{1,0:T(8,128)(2,1)}, bf16[128,768]{1,0:T(8,128)(2,1)S(1)}, u32[]{:S(2)}, u32[]{:S(2)}) collective-permute-start(bf16[128,768]{1,0:T(8,128)(2,1)} %pad_maximum_fusion.3.d0), channel_id=1, source_target_pairs={{0,8},{8,0},{1,9},{9,1},{2,10},{10,2},{3,11},{11,3},{4,12},{12,4},... | collective-permute-start | bytes 589832 | tf_op jit(solution)/shard_map/ppermute | solution.py:281
  66.0 25.6 %copy-start = (bf16[128,768]{1,0:T(8,128)(2,1)S(1)}, bf16[128,768]{1,0:T(8,128)(2,1)}, u32[]{:S(2)}) copy-start(bf16[128,768]{1,0:T(8,128)(2,1)} %pad_maximum_fusion.3.d0) | copy-start | bytes 589828
  66.0 0.8 copy-start.3
  81.9 46.7 %copy-start.1 = (bf16[160,768]{1,0:T(8,128)(2,1)}, bf16[160,768]{1,0:T(8,128)(2,1)S(1)}, u32[]{:S(2)}) copy-start(bf16[160,768]{1,0:T(8,128)(2,1)S(1)} %get-tuple-element.43.ext) | copy-start | bytes 737284
  81.9 18.6 %collective-permute-start.4 = (bf16[256,768]{1,0:T(8,128)(2,1)S(1)}, bf16[256,768]{1,0:T(8,128)(2,1)S(1)}, u32[]{:S(2)}, u32[]{:S(2)}) collective-permute-start(bf16[256,768]{1,0:T(8,128)(2,1)S(1)} %constant_dynamic-update-slice_fusion), channel_id=1, source_target_pairs={{2,0},{4,2},{6,4},{0,6},{3,1},{5,3},{7,5},{1,7},{10,8},{12,10},{14... | collective-permute-start | bytes 1179656 | tf_op jit(solution)/shard_map/ppermute | solution.py:285
  83.9 20.3 %collective-permute-start.5 = (bf16[256,768]{1,0:T(8,128)(2,1)S(1)}, bf16[256,768]{1,0:T(8,128)(2,1)S(1)}, u32[]{:S(2)}, u32[]{:S(2)}) collective-permute-start(bf16[256,768]{1,0:T(8,128)(2,1)S(1)} %constant_dynamic-update-slice_fusion), channel_id=1, source_target_pairs={{4,0},{6,2},{0,4},{2,6},{5,1},{7,3},{1,5},{3,7},{12,8},{14,10},{8,... | collective-permute-start | bytes 1179656 | tf_op jit(solution)/shard_map/ppermute | solution.py:285
  88.7 17.4 %collective-permute-start.6 = (bf16[256,768]{1,0:T(8,128)(2,1)S(1)}, bf16[256,768]{1,0:T(8,128)(2,1)S(1)}, u32[]{:S(2)}, u32[]{:S(2)}) collective-permute-start(bf16[256,768]{1,0:T(8,128)(2,1)S(1)} %constant_dynamic-update-slice_fusion), channel_id=1, source_target_pairs={{6,0},{0,2},{2,4},{4,6},{7,1},{1,3},{3,5},{5,7},{14,8},{8,10},{10,... | collective-permute-start | bytes 1179656 | tf_op jit(solution)/shard_map/ppermute | solution.py:285
  123.7 4.9 %collective-permute-start.7 = (bf16[128,1152]{1,0:T(8,128)(2,1)S(1)}, bf16[128,1152]{1,0:T(8,128)(2,1)S(1)}, u32[]{:S(2)}, u32[]{:S(2)}) collective-permute-start(bf16[128,1152]{1,0:T(8,128)(2,1)S(1)} %get-tuple-element.41), channel_id=1, source_target_pairs={{0,1},{1,0},{2,3},{3,2},{4,5},{5,4},{6,7},{7,6},{8,9},{9,8},{10,11... | collective-permute-start | bytes 884744 | tf_op jit(solution)/shard_map/ppermute | solution.py:281
  131.2 0.8 copy-start.5
  131.9 0.8 copy-start.7
  146.9 44.2 %all-to-all-start.3 = ((bf16[16,16,128]{2,1,0:T(8,128)(2,1)}), bf16[16,16,128]{2,1,0:T(8,128)(2,1)S(1)}, u32[]{:S(2)}, u32[]{:S(2)}) async-start(bf16[16,16,128]{2,1,0:T(8,128)(2,1)} %broadcast_in_dim.14), calls=%async_computation.3 | async-start | bytes 131072 | tf_op jit(solution)/shard_map/all_to_all | solution.py:290
  167.2 15.8 %collective-permute-start.8 = (f32[8,768]{1,0:T(8,128)}, f32[8,768]{1,0:T(8,128)S(1)}, u32[]{:S(2)}, u32[]{:S(2)}) collective-permute-start(f32[8,768]{1,0:T(8,128)} %copy-done.10), channel_id=1, source_target_pairs={{0,1},{1,0},{2,3},{3,2},{4,5},{5,4},{6,7},{7,6},{8,9},{9,8},{10,11... | collective-permute-start | bytes 73736 | tf_op jit(solution)/shard_map/ppermute | solution.py:281
  169.4 16.2 %collective-permute-start.9 = (f32[8,768]{1,0:T(8,128)}, f32[8,768]{1,0:T(8,128)S(1)}, u32[]{:S(2)}, u32[]{:S(2)}) collective-permute-start(f32[8,768]{1,0:T(8,128)} %copy-done.9), channel_id=1, source_target_pairs={{1,2},{3,4},{5,6},{7,8},{9,10},{11,12},{13,14},{2,1},{4,3},{6,5},{... | collective-permute-start | bytes 73736 | tf_op jit(solution)/shard_map/ppermute | solution.py:362
  185.5 0.9 copy-start.2
  187.2 1.0 copy-start.6
  188.2 1.0 copy-start.8
  (3 other events, 2.0 us)

commit v4 on v3

--- a/solution.py
+++ b/solution.py
@@ -131,107 +131,129 @@
 KB = 512
 
 
-def forward_body(q, k, v, d0, d4, dq, stats, ds, ss, sm):
-    for g, d in enumerate((d0, d4)):
-        for h in range(OWN_HEADS):
-            ds[h, g * CHUNK : g * CHUNK + BLOCK, :] = d[0:BLOCK, h * 128 : (h + 1) * 128]
-            ds[h, g * CHUNK + BLOCK : (g + 1) * CHUNK, :] = d[
-                0:BLOCK, HALF + h * 128 : HALF + (h + 1) * 128
-            ]
+def forward_body(q, k, v, d, dq, stats, ds, ss, sm):
+    for h in range(OWN_HEADS):
+        ds[h, 0:BLOCK, :] = d[:, h * 128 : (h + 1) * 128]
+        ds[h, BLOCK:CHUNK, :] = d[:, HALF + h * 128 : HALF + (h + 1) * 128]
     sm[...] = jnp.zeros_like(sm)
     lane = lax.broadcasted_iota(jnp.int32, (CHUNK, 128), 1)
 
     def head(h, _):
-        for g in range(2):
-            qh = q[h, g * 1024 : g * 1024 + CHUNK, :]
-            top = None
-            for b in range(0, BINS, KB):
-                s = nt(qh, k[h, b : b + KB, :])
-                ss[:, b : b + KB] = s
-                m = jnp.max(s, axis=1, keepdims=True)
-                top = m if top is None else jnp.maximum(top, m)
-            total = jnp.zeros((CHUNK, 1), F32)
-            out = jnp.zeros((CHUNK, HEAD_DIM), F32)
-            for b in range(0, BINS, KB):
-                p = jnp.exp((ss[:, b : b + KB] - top) * SCALE)
-                total = total + jnp.sum(p, axis=1, keepdims=True)
-                out = out + nn(p.astype(BF16), v[h, b : b + KB, :])
-                if g == 0:
-                    ss[:, b : b + KB] = p
-            inverse = 1.0 / total
-            attended = (out * inverse).astype(BF16).astype(F32)
-            do = ds[h, g * CHUNK : (g + 1) * CHUNK, :]
-            delta = jnp.sum(do.astype(F32) * attended, axis=1, keepdims=True)
-            log_total = top * SCALE + jnp.log(total)
-            sl = slice(g * CHUNK, (g + 1) * CHUNK)
-            sm[sl, :] = jnp.where(
-                lane == h, log_total, jnp.where(lane == h + OWN_HEADS, delta, sm[sl, :])
-            )
-            if g == 0:
-                acc = jnp.zeros((CHUNK, HEAD_DIM), F32)
-                for b in range(0, BINS, KB):
-                    dp = nt(do, v[h, b : b + KB, :])
-                    dsc = (ss[:, b : b + KB] * inverse * (dp - delta)).astype(BF16)
-                    acc = acc + nn(dsc, k[h, b : b + KB, :])
-                dq[h, :, :] = (acc * SCALE).astype(BF16)
+        qh = q[h, 0:CHUNK, :]
+        top = None
+        for b in range(0, BINS, KB):
+            s = nt(qh, k[h, b : b + KB, :])
+            ss[:, b : b + KB] = s
+            m = jnp.max(s, axis=1, keepdims=True)
+            top = m if top is None else jnp.maximum(top, m)
+        total = jnp.zeros((CHUNK, 1), F32)
+        out = jnp.zeros((CHUNK, HEAD_DIM), F32)
+        for b in range(0, BINS, KB):
+            p = jnp.exp((ss[:, b : b + KB] - top) * SCALE)
+            total = total + jnp.sum(p, axis=1, keepdims=True)
+            out = out + nn(p.astype(BF16), v[h, b : b + KB, :])
+            ss[:, b : b + KB] = p
+        inverse = 1.0 / total
+        attended = (out * inverse).astype(BF16).astype(F32)
+        do = ds[h]
+        delta = jnp.sum(do.astype(F32) * attended, axis=1, keepdims=True)
+        log_total = top * SCALE + jnp.log(total)
+        sm[...] = jnp.where(lane == h, log_total, jnp.where(lane == h + OWN_HEADS, delta, sm[...]))
+        acc = jnp.zeros((CHUNK, HEAD_DIM), F32)
+        for b in range(0, BINS, KB):
+            dp = nt(do, v[h, b : b + KB, :])
+            dsc = (ss[:, b : b + KB] * inverse * (dp - delta)).astype(BF16)
+            acc = acc + nn(dsc, k[h, b : b + KB, :])
+        dq[h, :, :] = (acc * SCALE).astype(BF16)
         return 0
 
     lax.fori_loop(0, OWN_HEADS, head, 0)
     stats[...] = jnp.transpose(sm[...])[0:8, :]
 
 
-def backward_body(pos, q, k, v, dq, d0, d4, b1, b2, b3, stats, mine, give, ds, gs):
+EDGE = 16
+WIDE = CHUNK + 2 * EDGE
+WINDOW = BLOCK + 2 * EDGE
+
+
+def backward_body(pos, q, k, v, dq, cots, stats, mine, give, ds, gs, kx, vx, qx, dx_, st):
     core = pos[2]
-    here = pl.multiple_of(core * BLOCK, BLOCK)
-    there = pl.multiple_of((1 - core) * BLOCK, BLOCK)
-    blocks = ((d0, 0), (b1, 0), (b2, 0), (b3, 0), (d4, 0), (b1, BLOCK), (b2, BLOCK), (b3, BLOCK))
-    for c, (d, low) in enumerate(blocks):
+
+    def place(c):
+        return lax.rem(pos[0] + lax.div(c, 4), 2) * 4 + lax.rem(pos[1] + c, 4)
+
+    for c in range(CHUNKS):
+        at = place(jnp.int32(c))
         for h in range(OWN_HEADS):
-            ds[h, c * CHUNK : c * CHUNK + BLOCK, :] = d[
-                low : low + BLOCK, h * 128 : (h + 1) * 128
-            ]
-            ds[h, c * CHUNK + BLOCK : (c + 1) * CHUNK, :] = d[
-                low : low + BLOCK, HALF + h * 128 : HALF + (h + 1) * 128
-            ]
+            lo = c * CHUNK
+            ds[h, lo : lo + BLOCK, :] = cots[at, :, h * 128 : (h + 1) * 128]
+            ds[h, lo + BLOCK : lo + CHUNK, :] = cots[at, :, HALF + h * 128 : HALF + (h + 1) * 128]
+    prev, nxt, _, _ = neighbours(pos, jnp.int32(0), jnp.int32(0))
+    low = pl.multiple_of(prev * CHUNK + CHUNK - EDGE, EDGE)
+    high = pl.multiple_of(nxt * CHUNK, EDGE)
     for h in range(OWN_HEADS):
-        kh = k[h, 0:CHUNK, :]
-        vh = v[h, 0:CHUNK, :]
+        for src, dst in ((k, kx), (v, vx)):
+            dst[h, 0:EDGE, :] = src[h, pl.ds(low, EDGE), :]
+            dst[h, EDGE : EDGE + CHUNK, :] = src[h, 0:CHUNK, :]
+            dst[h, EDGE + CHUNK : WIDE, :] = src[h, pl.ds(high, EDGE), :]
+        for src, dst in ((q, qx), (ds, dx_)):
+            dst[h, 0:EDGE, :] = src[h, pl.ds(low, EDGE), :]
+            dst[h, EDGE : 2 * EDGE, :] = src[h, pl.ds(high, EDGE), :]
+    low_stats = jnp.transpose(jnp.tile(stats[place(prev), :, 128:256], (16, 1)))
+    high_stats = jnp.transpose(jnp.tile(stats[place(nxt), :, 0:128], (16, 1)))
+    st[0:EDGE, :] = low_stats[128 - EDGE : 128, :]
+    st[EDGE : 2 * EDGE, :] = high_stats[0:EDGE, :]
+    for h in range(OWN_HEADS):
+        kh = kx[h]
+        vh = vx[h]
 
         def step(dx, carry):
             acc_k, acc_v = carry
-            xa = lax.rem(pos[1] + dx, 4)
             for dz in range(2):
-                at = pl.multiple_of(dz * 1024 + dx * CHUNK, CHUNK)
+                c = dz * 4 + dx
+                at = pl.multiple_of(c * CHUNK, CHUNK)
                 qc = q[h, pl.ds(at, CHUNK), :]
                 dc = ds[h, pl.ds(at, CHUNK), :]
-                log_total = stats[xa, h : h + 1, dz * CHUNK : (dz + 1) * CHUNK]
-                delta = stats[xa, h + OWN_HEADS : h + OWN_HEADS + 1, dz * CHUNK : (dz + 1) * CHUNK]
+                row = place(c)
+                log_total = stats[row, h : h + 1, :]
+                delta = stats[row, h + OWN_HEADS : h + OWN_HEADS + 1, :]
                 p = jnp.exp(nt(kh, qc) * SCALE - log_total)
                 acc_v = acc_v + nn(p.astype(BF16), dc)
                 dsc = (p * (nt(vh, dc) - delta)).astype(BF16)
                 acc_k = acc_k + nn(dsc, qc)
             return acc_k, acc_v
 
-        zero = jnp.zeros((CHUNK, HEAD_DIM), F32)
+        zero = jnp.zeros((WIDE, HEAD_DIM), F32)
         acc_k, acc_v = lax.fori_loop(0, 4, step, (zero, zero))
-        gs[:, h * 128 : (h + 1) * 128] = dq[h]
+        p = jnp.exp(nt(qx[h], k[h]) * SCALE - st[:, h : h + 1])
+        dsc = (p * (nt(dx_[h], v[h]) - st[:, h + OWN_HEADS : h + OWN_HEADS + 1])).astype(BF16)
+        dqx = (nn(dsc, k[h]) * SCALE).astype(BF16)
+        cols = slice(h * 128, (h + 1) * 128)
+        gs[0:EDGE, cols] = dqx[0:EDGE]
+        gs[EDGE : EDGE + CHUNK, cols] = dq[h]
+        gs[EDGE + CHUNK : WIDE, cols] = dqx[EDGE : 2 * EDGE]
         gs[:, HALF + h * 128 : HALF + (h + 1) * 128] = (acc_k * SCALE).astype(BF16)
         gs[:, 2 * HALF + h * 128 : 2 * HALF + (h + 1) * 128] = acc_v.astype(BF16)
-    mine[...] = gs[pl.ds(here, BLOCK), :]
-    give[...] = gs[pl.ds(there, BLOCK), :]
-
-
-def conv_body(pos, mine, recv, w_own, w_oth, ext, gain, taps, gh, gc, usum, inner_edge, outer_edge, ns):
+    mine[...] = gs[pl.ds(pl.multiple_of(core * BLOCK, BLOCK), WINDOW), :]
+    give[...] = gs[pl.ds(pl.multiple_of((1 - core) * BLOCK, BLOCK), WINDOW), :]
+
+
+def conv_body(pos, mine, recv, w_own, w_oth, ext, gain, taps, out, usum, ns, gh, gc):
+    _, _, prev_ok, nxt_ok = neighbours(pos, jnp.int32(0), jnp.int32(0))
+    first = pos[2] == 0
+    low_ok = jnp.where(first, prev_ok, 1.0)
+    high_ok = jnp.where(first, 1.0, nxt_ok)
     g = gain[0:1, :]
-    for r in range(0, 160, 16):
+    for r in range(0, WINDOW, 16):
         ns[r : r + 16, :] = normalize(ext[r : r + 16, :].astype(F32))
     gh[...] = nt(mine[...], w_own[...]) + nt(recv[...], w_oth[...])
     for j in range(0, C, 128):
         tap = [taps[t : t + 1, j : j + 128] for t in range(5)]
-        sums = [jnp.zeros((8, 128), F32) for _ in range(5)]
         gj = g[:, j : j + 128]
-        for r in range(0, BLOCK, 64):
-            near = [ns[14 + r + t : 78 + r + t, j : j + 128] for t in range(5)]
+        cols = slice(j, j + 128)
+
+        def grad(r, n):
+            near = [ns[r - 2 + t : r - 2 + t + n, cols] for t in range(5)]
             u = tap[0] * (near[0] * gj)
             for t in range(1, 5):
                 u = u + tap[t] * (near[t] * gj)
@@ -240,38 +262,34 @@
             slope = 0.5 * (1.0 + th) + 0.5 * u * (1.0 - th * th) * GELU_ROOT * (
                 1.0 + 3.0 * 0.044715 * u * u
             )
-            gcv = gh[r : r + 64, j : j + 128] * slope
-            gc[r : r + 64, j : j + 128] = gcv
+            return near, gh[r : r + n, cols] * slope
+
+        _, edge = grad(8, 8)
+        gc[8:16, cols] = edge * low_ok
+        _, edge = grad(144, 8)
+        gc[144:152, cols] = edge * high_ok
+        sums = [jnp.zeros((8, 128), F32) for _ in range(5)]
+        for r in range(EDGE, EDGE + BLOCK, 64):
+            near, val = grad(r, 64)
+            gc[r : r + 64, cols] = val
             for t in range(5):
-                sums[t] = sums[t] + jnp.sum((gcv * near[t]).reshape(8, 8, 128), axis=0)
+                sums[t] = sums[t] + jnp.sum((val * near[t]).reshape(8, 8, 128), axis=0)
         side, slot = divmod(j // 128, OWN_HEADS)
         for t in range(5):
             row = t * OWN_HEADS + slot
             usum[side, row : row + 1, :] = jnp.sum(sums[t], axis=0, keepdims=True)
     usum[:, 15:16, :] = jnp.zeros((2, 1, 128), F32)
-    first = pos[2] == 0
-    head, tail = gc[0:8, :], gc[BLOCK - 8 : BLOCK, :]
-    inner_edge[...] = jnp.where(first, tail, head)
-    outer_edge[...] = jnp.where(first, head, tail)
-
-
-def final_body(pos, gh, gc, inside, outside, ext, gain, taps, out, es):
-    first = pos[2] == 0
-    es[0:8, :] = jnp.where(first, outside[...], inside[...])
-    es[8:136, :] = gc[...]
-    es[136:144, :] = jnp.where(first, inside[...], outside[...])
-    g = gain[0:1, :]
     tap = [taps[t : t + 1, :] for t in range(5)]
-    for r in range(0, BLOCK, 16):
-        gn = tap[0] * es[10 + r : 26 + r, :]
+    for r in range(EDGE, EDGE + BLOCK, 16):
+        gn = tap[0] * gc[r + 2 : r + 18, :]
         for t in range(1, 5):
-            gn = gn + tap[t] * es[10 + r - t : 26 + r - t, :]
-        x = ext[16 + r : 32 + r, :].astype(F32)
+            gn = gn + tap[t] * gc[r + 2 - t : r + 18 - t, :]
+        x = ext[r : r + 16, :].astype(F32)
         inv = lax.rsqrt(jnp.mean(x * x, axis=-1, keepdims=True) + EPSILON)
         scaled = gn * g
         inner = jnp.mean(scaled * x, axis=-1, keepdims=True)
         res = gh[r : r + 16, :] + inv * scaled - x * (inv * inv * inv * inner)
-        out[r : r + 16, :] = res.astype(BF16)
+        out[r - EDGE : r - EDGE + 16, :] = res.astype(BF16)
 
 
 AXES = ("y", "zm", "zl", "zh", "x", "core")
@@ -313,8 +331,8 @@
     parts = [halves(w) for w in (w_query, w_key, w_value)]
     w_own = jnp.concatenate([p[0] for p in parts], axis=1)
     w_oth = jnp.concatenate([p[1] for p in parts], axis=1)
+    cots = lax.all_gather(cot_own, ("zh", "x"), axis=0)
     sig_z, cot_own, w_own, w_oth = lax.optimization_barrier((sig_z, cot_own, w_own, w_oth))
-    cot_z = swap(cot_own, "zh")
     near = share(jnp.concatenate([sig, sig_z], axis=0), "x", 4)
     other = swap(near, "core")
 
@@ -325,46 +343,40 @@
         (pos, near, other, w_own, gain, conv_taps),
         (VM((CHUNKS, CHUNK, C), BF16), VM((288, C), F32), VM((CHUNK, C), BF16)),
     )
-    cot_z, q = lax.optimization_barrier((cot_z, q))
-    both = jnp.concatenate([cot_own, cot_z], axis=0)
-    cots = [from_x(both, d) for d in (1, 2, 3)]
     part = jax.ShapeDtypeStruct((OWN_HEADS, CHUNK, HEAD_DIM), BF16)
     dq, stats = call(
         forward_body,
-        (part, jax.ShapeDtypeStruct((8, 2 * CHUNK), F32)),
-        (q, k, v, cot_own, cot_z),
+        (part, jax.ShapeDtypeStruct((8, CHUNK), F32)),
+        (q, k, v, cot_own),
         (
-            VM((OWN_HEADS, 2 * CHUNK, HEAD_DIM), BF16),
+            VM((OWN_HEADS, CHUNK, HEAD_DIM), BF16),
             VM((CHUNK, BINS), F32),
-            VM((2 * CHUNK, 128), F32),
+            VM((CHUNK, 128), F32),
         ),
     )
     stats, cots = lax.optimization_barrier((stats, cots))
-    stats_all = share(stats, "x", 4)
-    grads = jax.ShapeDtypeStruct((BLOCK, 3 * HALF), BF16)
+    stats_all = share(stats, ("zh", "x"), 8)
+    grads = jax.ShapeDtypeStruct((WINDOW, 3 * HALF), BF16)
     mine, give = call(
         backward_body,
         (grads, grads),
-        (pos, q, k, v, dq, cot_own, cot_z, *cots, stats_all),
-        (VM((OWN_HEADS, BINS, HEAD_DIM), BF16), VM((CHUNK, 3 * HALF), BF16)),
+        (pos, q, k, v, dq, cots, stats_all),
+        (
+            VM((OWN_HEADS, BINS, HEAD_DIM), BF16),
+            VM((WIDE, 3 * HALF), BF16),
+            VM((OWN_HEADS, WIDE, HEAD_DIM), BF16),
+            VM((OWN_HEADS, WIDE, HEAD_DIM), BF16),
+            VM((OWN_HEADS, 2 * EDGE, HEAD_DIM), BF16),
+            VM((OWN_HEADS, 2 * EDGE, HEAD_DIM), BF16),
+            VM((2 * EDGE, 128), F32),
+        ),
     )
     recv = swap(give, "core")
-    wide = jax.ShapeDtypeStruct((BLOCK, C), F32)
-    edge = jax.ShapeDtypeStruct((8, C), F32)
-    gh, gc, usum, inside, outside = call(
+    out, usum = call(
         conv_body,
-        (wide, wide, jax.ShapeDtypeStruct((2, 16, 128), F32), edge, edge),
+        (jax.ShapeDtypeStruct((BLOCK, C), BF16), jax.ShapeDtypeStruct((2, 16, 128), F32)),
         (pos, mine, recv, w_own, w_oth, ext, gain, conv_taps),
-        (VM((160, C), F32),),
-    )
-    inside = swap(inside, "core")
-    pairs = [(i, i + 1) for i in range(1, 15, 2)] + [(i + 1, i) for i in range(1, 15, 2)]
-    outside = lax.ppermute(outside, ("zh", "x", "core"), pairs)
-    out = call(
-        final_body,
-        jax.ShapeDtypeStruct((BLOCK, C), BF16),
-        (pos, gh, gc, inside, outside, ext, gain, conv_taps),
-        (VM((144, C), F32),),
+        (VM((WINDOW, C), F32), VM((WINDOW, C), F32), VM((WINDOW, C), F32)),
     )
     wide = jnp.broadcast_to(usum[None], (16, 2, 16, 128)).reshape(32, 16, 128)
     part = jnp.sum(lax.all_to_all(wide, ("y", "x", "core"), 0, 0), axis=0)

time: 195 us -> 251 us (1.29)
  waiting for transfers between devices: 11.2 us -> 84.6 us
  starting transfers between devices: 90.1 us -> 40.4 us
  blocking collectives: 39.9 us -> 53.3 us
  between operations: 1 us -> 14.2 us
  local copies, waits for them, and re-layouts: 9.04 us -> 14.3 us
  Pallas kernels: 37.9 us -> 34.8 us
    all_gather x0 -> x1, waiting for transfers between devices: none -> 66.2 us  [shards(): cots = lax.all_gather(cot_own, ('zh', 'x'), axis=0)]
    ppermute x4 -> x0, starting transfers between devices: 23.3 us -> none  [the longest x1 13.7 us: shards(): outside = lax.ppermute(outside, ('zh', 'x', 'core'), pairs)]
    all_to_all x1, starting transfers between devices: 20.3 us -> 6.48 us  [share(): return lax.all_to_all(wide, axes, 0, 0)]
    ppermute x6 -> x4, starting transfers between devices: 46.5 us -> 33.9 us  [swap(): return lax.ppermute(a, axis, [(0, 1), (1, 0)])]
    all_to_all x1, waiting for transfers between devices: 0.01 us -> 11 us  [share(): return lax.all_to_all(wide, axes, 0, 0)]
    all_to_all x2, blocking collectives: 25.2 us -> 35.6 us  [share(): return lax.all_to_all(wide, axes, 0, 0)]
    ppermute x4 -> x0, waiting for transfers between devices: 7.98 us -> none  [the longest x3 5.53 us: from_x(): return lax.ppermute(a, 'x', [((i + step) % 4, i) for i in range(4)])]
    unnamed x34 -> x39, local copies, waits for them, and re-layouts: 8.25 us -> 13 us
  transfers between devices with their start and end apart: 11 -> 6, of which waited for: 5 -> 5; matrix products, arithmetic and copies ran while one was open for 2% -> 1% of each run, Pallas kernels for 13% -> 8%
where the time goes in v4:
time: 251 us; the launch traced here: 248 us
  waiting for transfers between devices  84.6 us (34%)
  blocking collectives  53.3 us (21%)
  starting transfers between devices  40.4 us (16%)
  Pallas kernels  34.8 us (14%)
  local copies, waits for them, and re-layouts  14.3 us (6%)
  between operations  14.2 us (6%)
  other arithmetic  6.86 us (3%)
    all_gather x1, waiting for transfers between devices, shards(): cots = lax.all_gather(cot_own, ('zh', 'x'), axis=0)  66.2 us
    all_to_all x2, blocking collectives, share(): return lax.all_to_all(wide, axes, 0, 0)  35.6 us
    pallas_call x4, Pallas kernels, call(): pl.pallas_call(body, out_shape=out_shape, in_specs=specs, out_specs=outs,...  34.8 us
    ppermute x4, starting transfers between devices, swap(): return lax.ppermute(a, axis, [(0, 1), (1, 0)])  33.9 us
    all_to_all x1, blocking collectives, shards(): part = jnp.sum(lax.all_to_all(wide, ('y', 'x', 'core'), 0, 0), axis=0)  14.4 us
    unnamed x39, local copies, waits for them, and re-layouts  13 us
    all_to_all x1, waiting for transfers between devices, share(): return lax.all_to_all(wide, axes, 0, 0)  11 us
    ppermute x4, waiting for transfers between devices, swap(): return lax.ppermute(a, axis, [(0, 1), (1, 0)])  6.67 us
  transfers between devices with their start and end apart: 6, of which 5 were waited for; matrix products, arithmetic and copies ran while one was open for 1% of the time, Pallas kernels for 8%

profile of v4, /device:TPU:7, one launch (start us, length us, event | category | flops | bytes accessed | tf_op | source)
XLA Modules:
  0.0 248.4 jit_solution(3612842112589151865)
XLA Ops:
  8.3 2.6 %collective-permute-start.1 = (bf16[128,384]{1,0:T(8,128)(2,1)S(1)}, bf16[128,384]{1,0:T(8,128)(2,1)S(1)}, u32[]{:S(2)}, u32[]{:S(2)}) collective-permute-start(bf16[128,384]{1,0:T(8,128)(2,1)S(1)} %broadcast_select_fusion.8), channel_id=1, source_target_pairs={{0,1},{1,0},{2,3},{3,2},{4,5},{5,4},{6,7},{7,6},{8,9},{9,8},{10,11... | collective-permute-start | bytes 294920 | tf_op jit(solution)/shard_map/ppermute | solution.py:299
  10.9 15.4 %collective-permute-start = (bf16[128,768]{1,0:T(8,128)(2,1)}, bf16[128,768]{1,0:T(8,128)(2,1)}, u32[]{:S(2)}, u32[]{:S(2)}) collective-permute-start(bf16[128,768]{1,0:T(8,128)(2,1)} %bitcast.13), channel_id=1, source_target_pairs={{0,8},{8,0},{1,9},{9,1},{2,10},{10,2},{3,11},{11,3},{4,12},{12,4},... | collective-permute-start | bytes 589832 | tf_op jit(solution)/shard_map/ppermute | solution.py:299
  26.3 1.4 broadcast_select_fusion.2
  29.8 2.1 collective-permute-done
  34.3 6.5 %all-to-all-start = ((bf16[4,256,768]{2,1,0:T(8,128)(2,1)}), bf16[4,256,768]{2,1,0:T(8,128)(2,1)}, u32[]{:S(2)}, u32[]{:S(2)}) async-start(bf16[4,256,768]{2,1,0:T(8,128)(2,1)} %broadcast_in_dim.10), calls=%async_computation | async-start | bytes 3145728 | tf_op jit(solution)/shard_map/all_to_all | solution.py:308
  41.5 11.0 %all-to-all-done.near = bf16[4,256,768]{2,1,0:T(8,128)(2,1)} async-done(((bf16[4,256,768]{2,1,0:T(8,128)(2,1)}), bf16[4,256,768]{2,1,0:T(8,128)(2,1)}, u32[]{:S(2)}, u32[]{:S(2)}) %all-to-all-start) | async-done | bytes 1572896 | tf_op jit(solution)/shard_map/all_to_all | solution.py:308
  52.5 10.1 %collective-permute-start.2 = (bf16[4,256,768]{2,1,0:T(8,128)(2,1)}, bf16[4,256,768]{2,1,0:T(8,128)(2,1)}, u32[]{:S(2)}, u32[]{:S(2)}) collective-permute-start(bf16[4,256,768]{2,1,0:T(8,128)(2,1)} %all-to-all-done.near), channel_id=1, source_target_pairs={{0,1},{1,0},{2,3},{3,2},{4,5},{5,4},{6,7},{7,6},{8,9},{9,8},{10,11... | collective-permute-start | bytes 4718600 | tf_op jit(solution)/shard_map/ppermute | solution.py:299
  62.7 3.2 %collective-permute-done.2.other = bf16[4,256,768]{2,1,0:T(8,128)(2,1)} collective-permute-done((bf16[4,256,768]{2,1,0:T(8,128)(2,1)}, bf16[4,256,768]{2,1,0:T(8,128)(2,1)}, u32[]{:S(2)}, u32[]{:S(2)}) %collective-permute-start.2) | collective-permute-done | bytes 1572896 | tf_op jit(solution)/shard_map/ppermute | solution.py:299
  66.7 15.1 %shard_map.94 = (bf16[3,2048,128]{2,1,0:T(8,128)(2,1)S(1)}, bf16[3,2048,128]{2,1,0:T(8,128)(2,1)S(1)}, bf16[3,2048,128]{2,1,0:T(8,128)(2,1)S(1)}, bf16[160,768]{1,0:T(8,128)(2,1)S(1)}) custom-call(s32[3]{0:T(128)S(1)} %pad_add_fusion.pos, bf16[4,256,768]{2,1,0:T(8,128)(2,1)} %all-to-all-done.near, bf16[4,256,768]{2,1,0:T(8,128)(2,1)} %collective-permute-done.2.other, ...), custom_call_target="tpu_custom_call" | custom-call | tf_op jit(solution)/shard_map/pallas_call | solution.py:40
  82.5 5.9 %shard_map.95 = (bf16[3,256,128]{2,1,0:T(8,128)(2,1)S(1)}, f32[8,256]{1,0:T(8,128)S(1)}) custom-call(bf16[3,2048,128]{2,1,0:T(8,128)(2,1)S(1)} %get-tuple-element.21.q, bf16[3,2048,128]{2,1,0:T(8,128)(2,1)S(1)} %get-tuple-element.22.k, bf16[3,2048,128]{2,1,0:T(8,128)(2,1)S(1)} %get-tuple-element.23.v, bf16[128,768]{1,0:T(8,128)(2,1)S(1)} %copy-done.6), custom_call_target="tpu_custom_call" | custom-call | tf_op jit(solution)/shard_map/pallas_call | solution.py:40
  92.7 66.2 %all-gather.4.cloned.1.call-done = bf16[1024,768]{1,0:T(8,128)(2,1)} async-done(((bf16[128,768]{1,0:T(8,128)(2,1)}), bf16[1024,768]{1,0:T(8,128)(2,1)}) %all-gather.4.cloned.1.call-update) | async-done | bytes 1572880 | tf_op jit(solution)/shard_map/all_gather | solution.py:334
  158.8 15.9 %all_to_all.20.stats = f32[8,8,256]{2,1,0:T(8,128)S(1)} all-to-all(f32[8,8,256]{2,1,0:T(8,128)S(1)} %broadcast_in_dim.11), channel_id=1, replica_groups=mesh['y'=4,'zm'=2,'zl'=4,'zh'=2,'x'=4,'core'=2] {'zh','x'}, dimensions={0} | all-to-all | bytes 131072 | tf_op jit(solution)/shard_map/all_to_all | solution.py:308
  174.7 1.4 copy-done.1
  176.1 1.4 copy-done.3
  177.5 1.4 copy-done.5
  178.9 1.4 copy-done.7
  181.3 9.9 %shard_map.96 = (bf16[160,1152]{1,0:T(8,128)(2,1)S(1)}, bf16[160,1152]{1,0:T(8,128)(2,1)S(1)}) custom-call(s32[3]{0:T(128)S(1)} %pad_add_fusion.pos, bf16[3,2048,128]{2,1,0:T(8,128)(2,1)S(1)} %copy-done.1, bf16[3,2048,128]{2,1,0:T(8,128)(2,1)S(1)} %copy-done.3, bf16[3,2048,128]{2,1,0:T(8,128)(2,1)S(1)} %copy-done.5, bf16[3,256,128]{2,1,0:T(8,128)(2,1)S(1)} %copy-done.13, ...), custom_call_target="tpu_custom_call" | custom-call | tf_op jit(solution)/shard_map/pallas_call | solution.py:40
  191.2 5.7 %collective-permute-start.3 = (bf16[160,1152]{1,0:T(8,128)(2,1)S(1)}, bf16[160,1152]{1,0:T(8,128)(2,1)S(1)}, u32[]{:S(2)}, u32[]{:S(2)}) collective-permute-start(bf16[160,1152]{1,0:T(8,128)(2,1)S(1)} %get-tuple-element.30), channel_id=1, source_target_pairs={{0,1},{1,0},{2,3},{3,2},{4,5},{5,4},{6,7},{7,6},{8,9},{9,8},{10,11... | collective-permute-start | bytes 1105928 | tf_op jit(solution)/shard_map/ppermute | solution.py:299
  196.9 1.3 collective-permute-done.3.recv
  198.2 3.9 %shard_map.97 = (bf16[128,768]{1,0:T(8,128)(2,1)}, f32[2,16,128]{2,1,0:T(8,128)S(1)}) custom-call(s32[3]{0:T(128)S(1)} %pad_add_fusion.pos, bf16[160,1152]{1,0:T(8,128)(2,1)S(1)} %get-tuple-element.29.mine, bf16[160,1152]{1,0:T(8,128)(2,1)S(1)} %collective-permute-done.3.recv, bf16[768,1152]{1,0:T(8,128)(2,1)S(1)} %pad_maximum_fusion.w.w_own, ...), custom_call_target="tpu_custom_call" | custom-call | tf_op jit(solution)/shard_map/pallas_call | solution.py:40
  202.1 14.4 %all_to_all.21 = f32[32,16,128]{2,1,0:T(8,128)S(1)} all-to-all(f32[32,16,128]{2,1,0:T(8,128)S(1)} %bitcast.10), channel_id=1, replica_groups=mesh['y'=4,'zm'=2,'zl'=4,'zh'=2,'x'=4,'core'=2] {'y','x','core'}, dimensions={0} | all-to-all | bytes 524288 | tf_op jit(solution)/shard_map/all_to_all | solution.py:382
  216.6 19.7 %all_to_all.22 = bf16[16,16,128]{2,1,0:T(8,128)(2,1)S(1)} all-to-all(bf16[16,16,128]{2,1,0:T(8,128)(2,1)S(1)} %broadcast_in_dim.14), channel_id=1, replica_groups=mesh['y'=4,'zm'=2,'zl'=4,'zh'=2,'x'=4,'core'=2] {'zm','zl','zh'}, dimensions={0} | all-to-all | bytes 131072 | tf_op jit(solution)/shard_map/all_to_all | solution.py:308
  236.3 3.3 %all-gather.1 = f32[32,128]{1,0:T(8,128)S(1)} all-gather(f32[16,128]{1,0:T(8,128)S(1)} %convert_reduce_fusion), channel_id=3, replica_groups=mesh['y'=4,'zm'=2,'zl'=4,'zh'=2,'x'=4,'core'=2] {'core'}, dimensions={0}, use_global_device_ids=true | all-gather | bytes 24576 | tf_op jit(solution)/shard_map/all_gather | solution.py:385
  239.6 1.9 multiply_reduce_fusion
  (57 shorter events, 12.9 us)
Async XLA Ops:
  7.2 20.5 %copy-start.14 = (bf16[768,768]{1,0:T(8,128)(2,1)S(1)}, bf16[768,768]{1,0:T(8,128)(2,1)}, u32[]{:S(2)}) copy-start(bf16[768,768]{1,0:T(8,128)(2,1)} %param.12) | copy-start | bytes 3538948
  7.2 20.5 %copy-start.15 = (bf16[768,768]{1,0:T(8,128)(2,1)S(1)}, bf16[768,768]{1,0:T(8,128)(2,1)}, u32[]{:S(2)}) copy-start(bf16[768,768]{1,0:T(8,128)(2,1)} %param.11) | copy-start | bytes 3538948
  8.3 20.0 %collective-permute-start.1 = (bf16[128,384]{1,0:T(8,128)(2,1)S(1)}, bf16[128,384]{1,0:T(8,128)(2,1)S(1)}, u32[]{:S(2)}, u32[]{:S(2)}) collective-permute-start(bf16[128,384]{1,0:T(8,128)(2,1)S(1)} %broadcast_select_fusion.8), channel_id=1, source_target_pairs={{0,1},{1,0},{2,3},{3,2},{4,5},{5,4},{6,7},{7,6},{8,9},{9,8},{10,11... | collective-permute-start | bytes 294920 | tf_op jit(solution)/shard_map/ppermute | solution.py:299
  10.9 21.0 %collective-permute-start = (bf16[128,768]{1,0:T(8,128)(2,1)}, bf16[128,768]{1,0:T(8,128)(2,1)}, u32[]{:S(2)}, u32[]{:S(2)}) collective-permute-start(bf16[128,768]{1,0:T(8,128)(2,1)} %bitcast.13), channel_id=1, source_target_pairs={{0,8},{8,0},{1,9},{9,1},{2,10},{10,2},{3,11},{11,3},{4,12},{12,4},... | collective-permute-start | bytes 589832 | tf_op jit(solution)/shard_map/ppermute | solution.py:299
  28.1 0.9 copy-start.16
  34.3 28.4 %copy-start.17 = (f32[768]{0:T(1024)S(1)}, f32[768]{0:T(1024)}, u32[]{:S(2)}) copy-start(f32[768]{0:T(1024)} %param.8) | copy-start | bytes 9220
  34.3 18.2 %all-to-all-start = ((bf16[4,256,768]{2,1,0:T(8,128)(2,1)}), bf16[4,256,768]{2,1,0:T(8,128)(2,1)}, u32[]{:S(2)}, u32[]{:S(2)}) async-start(bf16[4,256,768]{2,1,0:T(8,128)(2,1)} %broadcast_in_dim.10), calls=%async_computation | async-start | bytes 3145728 | tf_op jit(solution)/shard_map/all_to_all | solution.py:308
  40.7 118.1 %all-gather.4.cloned.1.call-start = ((), (), s32[]{:S(2)}) async-start(), calls=%async_computation.4 | async-start | bytes 1769472 | tf_op jit(solution)/shard_map/all_gather | solution.py:334
  52.5 13.5 %collective-permute-start.2 = (bf16[4,256,768]{2,1,0:T(8,128)(2,1)}, bf16[4,256,768]{2,1,0:T(8,128)(2,1)}, u32[]{:S(2)}, u32[]{:S(2)}) collective-permute-start(bf16[4,256,768]{2,1,0:T(8,128)(2,1)} %all-to-all-done.near), channel_id=1, source_target_pairs={{0,1},{1,0},{2,3},{3,2},{4,5},{5,4},{6,7},{7,6},{8,9},{9,8},{10,11... | collective-permute-start | bytes 4718600 | tf_op jit(solution)/shard_map/ppermute | solution.py:299
  62.7 19.8 %copy-start.6 = (bf16[128,768]{1,0:T(8,128)(2,1)S(1)}, bf16[128,768]{1,0:T(8,128)(2,1)}, u32[]{:S(2)}) copy-start(bf16[128,768]{1,0:T(8,128)(2,1)} %pad_maximum_fusion.3.d) | copy-start | bytes 589828
  66.0 0.7 copy-start.10
  81.8 0.7 copy-start.8
  88.4 1.2 copy-start
  89.6 1.2 copy-start.2
  90.8 1.2 copy-start.4
  174.7 1.4 copy-start.1
  176.1 1.4 copy-start.3
  177.5 1.4 copy-start.5
  178.9 1.4 copy-start.7
  180.3 0.9 copy-start.13
  181.3 17.0 %copy-start.9 = (bf16[160,768]{1,0:T(8,128)(2,1)S(1)}, bf16[160,768]{1,0:T(8,128)(2,1)}, u32[]{:S(2)}) copy-start(bf16[160,768]{1,0:T(8,128)(2,1)} %copy-done.8) | copy-start | bytes 737284
  181.3 17.0 %copy-start.11 = (f32[5,768]{1,0:T(8,128)S(1)}, f32[5,768]{1,0:T(8,128)}, u32[]{:S(2)}) copy-start(f32[5,768]{1,0:T(8,128)} %taps.3) | copy-start | bytes 46084
  191.2 7.0 %collective-permute-start.3 = (bf16[160,1152]{1,0:T(8,128)(2,1)S(1)}, bf16[160,1152]{1,0:T(8,128)(2,1)S(1)}, u32[]{:S(2)}, u32[]{:S(2)}) collective-permute-start(bf16[160,1152]{1,0:T(8,128)(2,1)S(1)} %get-tuple-element.30), channel_id=1, source_target_pairs={{0,1},{1,0},{2,3},{3,2},{4,5},{5,4},{6,7},{7,6},{8,9},{9,8},{10,11... | collective-permute-start | bytes 1105928 | tf_op jit(solution)/shard_map/ppermute | solution.py:299
  198.2 41.4 %copy-start.18 = (f32[768]{0:T(1024)S(1)}, f32[768]{0:T(1024)}, u32[]{:S(2)}) copy-start(f32[768]{0:T(1024)} %param.8) | copy-start | bytes 9220
  (1 other events, 0.7 us)
Sparse Core Ops, SparseCore 0:
  45.3 113.4 all-gather.3

commit v5 on v4

--- a/solution.py
+++ b/solution.py
@@ -74,7 +74,7 @@
 
 
 def hidden_body(
-    pos, near, other, w, gain, taps, q, k, v, ext, xs, ns, hs
+    pos, near, other, w, taps, q, k, v, ext, xs, ns, hs
 ):
     core = pos[2]
     here = pl.multiple_of(core * BLOCK, BLOCK)
@@ -102,7 +102,7 @@
         dz = lax.div(c, 4)
         dx = lax.rem(c, 4)
         prev, nxt, prev_ok, nxt_ok = neighbours(pos, dz, dx)
-        g = gain[0:1, :]
+        g = taps[5:6, :]
         ns[0:16, :] = normalize(xs[prev, 240:256, :].astype(F32)) * g * prev_ok
         ns[272:288, :] = normalize(xs[nxt, 0:16, :].astype(F32)) * g * nxt_ok
         for r in range(0, CHUNK, 16):
@@ -131,40 +131,49 @@
 KB = 512
 
 
-def forward_body(q, k, v, d, dq, stats, ds, ss, sm):
-    for h in range(OWN_HEADS):
-        ds[h, 0:BLOCK, :] = d[:, h * 128 : (h + 1) * 128]
-        ds[h, BLOCK:CHUNK, :] = d[:, HALF + h * 128 : HALF + (h + 1) * 128]
+def forward_body(q, k, v, d0, d4, dq, stats, ds, ss, sm):
+    for g, d in enumerate((d0, d4)):
+        for h in range(OWN_HEADS):
+            ds[h, g * CHUNK : g * CHUNK + BLOCK, :] = d[0:BLOCK, h * 128 : (h + 1) * 128]
+            ds[h, g * CHUNK + BLOCK : (g + 1) * CHUNK, :] = d[
+                0:BLOCK, HALF + h * 128 : HALF + (h + 1) * 128
+            ]
     sm[...] = jnp.zeros_like(sm)
     lane = lax.broadcasted_iota(jnp.int32, (CHUNK, 128), 1)
 
     def head(h, _):
-        qh = q[h, 0:CHUNK, :]
-        top = None
-        for b in range(0, BINS, KB):
-            s = nt(qh, k[h, b : b + KB, :])
-            ss[:, b : b + KB] = s
-            m = jnp.max(s, axis=1, keepdims=True)
-            top = m if top is None else jnp.maximum(top, m)
-        total = jnp.zeros((CHUNK, 1), F32)
-        out = jnp.zeros((CHUNK, HEAD_DIM), F32)
-        for b in range(0, BINS, KB):
-            p = jnp.exp((ss[:, b : b + KB] - top) * SCALE)
-            total = total + jnp.sum(p, axis=1, keepdims=True)
-            out = out + nn(p.astype(BF16), v[h, b : b + KB, :])
-            ss[:, b : b + KB] = p
-        inverse = 1.0 / total
-        attended = (out * inverse).astype(BF16).astype(F32)
-        do = ds[h]
-        delta = jnp.sum(do.astype(F32) * attended, axis=1, keepdims=True)
-        log_total = top * SCALE + jnp.log(total)
-        sm[...] = jnp.where(lane == h, log_total, jnp.where(lane == h + OWN_HEADS, delta, sm[...]))
-        acc = jnp.zeros((CHUNK, HEAD_DIM), F32)
-        for b in range(0, BINS, KB):
-            dp = nt(do, v[h, b : b + KB, :])
-            dsc = (ss[:, b : b + KB] * inverse * (dp - delta)).astype(BF16)
-            acc = acc + nn(dsc, k[h, b : b + KB, :])
-        dq[h, :, :] = (acc * SCALE).astype(BF16)
+        for g in range(2):
+            qh = q[h, g * 1024 : g * 1024 + CHUNK, :]
+            top = None
+            for b in range(0, BINS, KB):
+                s = nt(qh, k[h, b : b + KB, :])
+                ss[:, b : b + KB] = s
+                m = jnp.max(s, axis=1, keepdims=True)
+                top = m if top is None else jnp.maximum(top, m)
+            total = jnp.zeros((CHUNK, 1), F32)
+            out = jnp.zeros((CHUNK, HEAD_DIM), F32)
+            for b in range(0, BINS, KB):
+                p = jnp.exp((ss[:, b : b + KB] - top) * SCALE)
+                total = total + jnp.sum(p, axis=1, keepdims=True)
+                out = out + nn(p.astype(BF16), v[h, b : b + KB, :])
+                if g == 0:
+                    ss[:, b : b + KB] = p
+            inverse = 1.0 / total
+            attended = (out * inverse).astype(BF16).astype(F32)
+            do = ds[h, g * CHUNK : (g + 1) * CHUNK, :]
+            delta = jnp.sum(do.astype(F32) * attended, axis=1, keepdims=True)
+            log_total = top * SCALE + jnp.log(total)
+            sl = slice(g * CHUNK, (g + 1) * CHUNK)
+            sm[sl, :] = jnp.where(
+                lane == h, log_total, jnp.where(lane == h + OWN_HEADS, delta, sm[sl, :])
+            )
+            if g == 0:
+                acc = jnp.zeros((CHUNK, HEAD_DIM), F32)
+                for b in range(0, BINS, KB):
+                    dp = nt(do, v[h, b : b + KB, :])
+                    dsc = (ss[:, b : b + KB] * inverse * (dp - delta)).astype(BF16)
+                    acc = acc + nn(dsc, k[h, b : b + KB, :])
+                dq[h, :, :] = (acc * SCALE).astype(BF16)
         return 0
 
     lax.fori_loop(0, OWN_HEADS, head, 0)
@@ -176,18 +185,21 @@
 WINDOW = BLOCK + 2 * EDGE
 
 
-def backward_body(pos, q, k, v, dq, cots, stats, mine, give, ds, gs, kx, vx, qx, dx_, st):
+def backward_body(
+    pos, q, k, v, dq, d0, d4, b1, b2, b3, stats, mine, give, ds, gs, kx, vx, qx, dx_, st
+):
     core = pos[2]
 
     def place(c):
-        return lax.rem(pos[0] + lax.div(c, 4), 2) * 4 + lax.rem(pos[1] + c, 4)
-
-    for c in range(CHUNKS):
-        at = place(jnp.int32(c))
+        return lax.rem(pos[1] + c, 4)
+
+    blocks = ((d0, 0), (b1, 0), (b2, 0), (b3, 0), (d4, 0), (b1, BLOCK), (b2, BLOCK), (b3, BLOCK))
+    for c, (d, low) in enumerate(blocks):
         for h in range(OWN_HEADS):
             lo = c * CHUNK
-            ds[h, lo : lo + BLOCK, :] = cots[at, :, h * 128 : (h + 1) * 128]
-            ds[h, lo + BLOCK : lo + CHUNK, :] = cots[at, :, HALF + h * 128 : HALF + (h + 1) * 128]
+            rows = slice(low, low + BLOCK)
+            ds[h, lo : lo + BLOCK, :] = d[rows, h * 128 : (h + 1) * 128]
+            ds[h, lo + BLOCK : lo + CHUNK, :] = d[rows, HALF + h * 128 : HALF + (h + 1) * 128]
     prev, nxt, _, _ = neighbours(pos, jnp.int32(0), jnp.int32(0))
     low = pl.multiple_of(prev * CHUNK + CHUNK - EDGE, EDGE)
     high = pl.multiple_of(nxt * CHUNK, EDGE)
@@ -199,8 +211,11 @@
         for src, dst in ((q, qx), (ds, dx_)):
             dst[h, 0:EDGE, :] = src[h, pl.ds(low, EDGE), :]
             dst[h, EDGE : 2 * EDGE, :] = src[h, pl.ds(high, EDGE), :]
-    low_stats = jnp.transpose(jnp.tile(stats[place(prev), :, 128:256], (16, 1)))
-    high_stats = jnp.transpose(jnp.tile(stats[place(nxt), :, 0:128], (16, 1)))
+    low_half, high_half = lax.div(prev, 4), lax.div(nxt, 4)
+    low_rows = jnp.where(low_half == 0, stats[place(prev), :, 128:256], stats[place(prev), :, 384:512])
+    high_rows = jnp.where(high_half == 0, stats[place(nxt), :, 0:128], stats[place(nxt), :, 256:384])
+    low_stats = jnp.transpose(jnp.tile(low_rows, (16, 1)))
+    high_stats = jnp.transpose(jnp.tile(high_rows, (16, 1)))
     st[0:EDGE, :] = low_stats[128 - EDGE : 128, :]
     st[EDGE : 2 * EDGE, :] = high_stats[0:EDGE, :]
     for h in range(OWN_HEADS):
@@ -215,8 +230,9 @@
                 qc = q[h, pl.ds(at, CHUNK), :]
                 dc = ds[h, pl.ds(at, CHUNK), :]
                 row = place(c)
-                log_total = stats[row, h : h + 1, :]
-                delta = stats[row, h + OWN_HEADS : h + OWN_HEADS + 1, :]
+                lanes = slice(dz * CHUNK, (dz + 1) * CHUNK)
+                log_total = stats[row, h : h + 1, lanes]
+                delta = stats[row, h + OWN_HEADS : h + OWN_HEADS + 1, lanes]
                 p = jnp.exp(nt(kh, qc) * SCALE - log_total)
                 acc_v = acc_v + nn(p.astype(BF16), dc)
                 dsc = (p * (nt(vh, dc) - delta)).astype(BF16)
@@ -238,12 +254,12 @@
     give[...] = gs[pl.ds(pl.multiple_of((1 - core) * BLOCK, BLOCK), WINDOW), :]
 
 
-def conv_body(pos, mine, recv, w_own, w_oth, ext, gain, taps, out, usum, ns, gh, gc):
+def conv_body(pos, mine, recv, w_own, w_oth, ext, taps, out, usum, ns, gh, gc):
     _, _, prev_ok, nxt_ok = neighbours(pos, jnp.int32(0), jnp.int32(0))
     first = pos[2] == 0
     low_ok = jnp.where(first, prev_ok, 1.0)
     high_ok = jnp.where(first, 1.0, nxt_ok)
-    g = gain[0:1, :]
+    g = taps[5:6, :]
     for r in range(0, WINDOW, 16):
         ns[r : r + 16, :] = normalize(ext[r : r + 16, :].astype(F32))
     gh[...] = nt(mine[...], w_own[...]) + nt(recv[...], w_oth[...])
@@ -331,36 +347,42 @@
     parts = [halves(w) for w in (w_query, w_key, w_value)]
     w_own = jnp.concatenate([p[0] for p in parts], axis=1)
     w_oth = jnp.concatenate([p[1] for p in parts], axis=1)
-    cots = lax.all_gather(cot_own, ("zh", "x"), axis=0)
-    sig_z, cot_own, w_own, w_oth = lax.optimization_barrier((sig_z, cot_own, w_own, w_oth))
+    coef = jnp.concatenate([conv_taps, gain, jnp.zeros((2, C), F32)], axis=0)
+    sig_z, cot_own, w_own, w_oth, coef = lax.optimization_barrier(
+        (sig_z, cot_own, w_own, w_oth, coef)
+    )
+    cot_z = swap(cot_own, "zh")
     near = share(jnp.concatenate([sig, sig_z], axis=0), "x", 4)
+    near, cot_z = lax.optimization_barrier((near, cot_z))
     other = swap(near, "core")
+    both = jnp.concatenate([cot_own, cot_z], axis=0)
+    cots = [from_x(both, d) for d in (1, 2, 3)]
 
     head_shape = jax.ShapeDtypeStruct((OWN_HEADS, BINS, HEAD_DIM), BF16)
     q, k, v, ext = call(
         hidden_body,
         (head_shape, head_shape, head_shape, jax.ShapeDtypeStruct((160, C), BF16)),
-        (pos, near, other, w_own, gain, conv_taps),
+        (pos, near, other, w_own, coef),
         (VM((CHUNKS, CHUNK, C), BF16), VM((288, C), F32), VM((CHUNK, C), BF16)),
     )
     part = jax.ShapeDtypeStruct((OWN_HEADS, CHUNK, HEAD_DIM), BF16)
     dq, stats = call(
         forward_body,
-        (part, jax.ShapeDtypeStruct((8, CHUNK), F32)),
-        (q, k, v, cot_own),
+        (part, jax.ShapeDtypeStruct((8, 2 * CHUNK), F32)),
+        (q, k, v, cot_own, cot_z),
         (
-            VM((OWN_HEADS, CHUNK, HEAD_DIM), BF16),
+            VM((OWN_HEADS, 2 * CHUNK, HEAD_DIM), BF16),
             VM((CHUNK, BINS), F32),
-            VM((CHUNK, 128), F32),
+            VM((2 * CHUNK, 128), F32),
         ),
     )
     stats, cots = lax.optimization_barrier((stats, cots))
-    stats_all = share(stats, ("zh", "x"), 8)
+    stats_all = share(stats, "x", 4)
     grads = jax.ShapeDtypeStruct((WINDOW, 3 * HALF), BF16)
     mine, give = call(
         backward_body,
         (grads, grads),
-        (pos, q, k, v, dq, cots, stats_all),
+        (pos, q, k, v, dq, cot_own, cot_z, *cots, stats_all),
         (
             VM((OWN_HEADS, BINS, HEAD_DIM), BF16),
             VM((WIDE, 3 * HALF), BF16),
@@ -375,7 +397,7 @@
     out, usum = call(
         conv_body,
         (jax.ShapeDtypeStruct((BLOCK, C), BF16), jax.ShapeDtypeStruct((2, 16, 128), F32)),
-        (pos, mine, recv, w_own, w_oth, ext, gain, conv_taps),
+        (pos, mine, recv, w_own, w_oth, ext, coef),
         (VM((WINDOW, C), F32), VM((WINDOW, C), F32), VM((WINDOW, C), F32)),
     )
     wide = jnp.broadcast_to(usum[None], (16, 2, 16, 128)).reshape(32, 16, 128)

time: 251 us -> 178 us (0.71)
  waiting for transfers between devices: 84.6 us -> 10.5 us
  between operations: 14.2 us -> 0.9 us
  starting transfers between devices: 40.4 us -> 49.3 us
  local copies, waits for them, and re-layouts: 14.3 us -> 5.97 us
  blocking collectives: 53.3 us -> 60.9 us
  Pallas kernels: 34.8 us -> 39.8 us
    all_gather x1 -> x0, waiting for transfers between devices: 66.2 us -> none  [shards(): cots = lax.all_gather(cot_own, ('zh', 'x'), axis=0)]
    unnamed x39 -> x18, local copies, waits for them, and re-layouts: 13 us -> 2.99 us
    ppermute x0 -> x3, starting transfers between devices: none -> 9.58 us  [from_x(): return lax.ppermute(a, 'x', [((i + step) % 4, i) for i in range(4)])]
    all_to_all x1, waiting for transfers between devices: 11 us -> 2.07 us  [share(): return lax.all_to_all(wide, axes, 0, 0)]
    all_to_all x2, blocking collectives: 35.6 us -> 43.1 us  [share(): return lax.all_to_all(wide, axes, 0, 0)]
    pallas_call x4, Pallas kernels: 34.8 us -> 39.8 us  [call(): pl.pallas_call(body, out_shape=out_shape, in_specs=specs, out_specs=outs,...]
    ppermute x4 -> x5, waiting for transfers between devices: 6.67 us -> 8.45 us  [swap(): return lax.ppermute(a, axis, [(0, 1), (1, 0)])]
    ppermute x4 -> x5, starting transfers between devices: 33.9 us -> 35.2 us  [swap(): return lax.ppermute(a, axis, [(0, 1), (1, 0)])]
  transfers between devices with their start and end apart: 6 -> 9, of which waited for: 5 -> 3; matrix products, arithmetic and copies ran while one was open for 1% -> 4% of each run, Pallas kernels for 8% -> 14%
where the time goes in v5:
time: 178 us; the launch traced here: 175 us
  blocking collectives  60.9 us (34%)
  starting transfers between devices  49.3 us (28%)
  Pallas kernels  39.8 us (22%)
  waiting for transfers between devices  10.5 us (6%)
  other arithmetic  7.41 us (4%)
  local copies, waits for them, and re-layouts  5.97 us (3%)
    all_to_all x2, blocking collectives, share(): return lax.all_to_all(wide, axes, 0, 0)  43.1 us
    pallas_call x4, Pallas kernels, call(): pl.pallas_call(body, out_shape=out_shape, in_specs=specs, out_specs=outs,...  39.8 us
    ppermute x5, starting transfers between devices, swap(): return lax.ppermute(a, axis, [(0, 1), (1, 0)])  35.2 us
    all_to_all x1, blocking collectives, shards(): part = jnp.sum(lax.all_to_all(wide, ('y', 'x', 'core'), 0, 0), axis=0)  14.6 us
    ppermute x3, starting transfers between devices, from_x(): return lax.ppermute(a, 'x', [((i + step) % 4, i) for i in range(4)])  9.58 us
    ppermute x5, waiting for transfers between devices, swap(): return lax.ppermute(a, axis, [(0, 1), (1, 0)])  8.45 us
    all_to_all x1, starting transfers between devices, share(): return lax.all_to_all(wide, axes, 0, 0)  4.51 us
  transfers between devices with their start and end apart: 9, of which 3 were waited for; matrix products, arithmetic and copies ran while one was open for 4% of the time, Pallas kernels for 14%

profile of v5, /device:TPU:7, one launch (start us, length us, event | category | flops | bytes accessed | tf_op | source)
XLA Modules:
  0.0 174.8 jit_solution(13342070799323201748)
XLA Ops:
  0.7 15.6 %collective-permute-start = (bf16[128,768]{1,0:T(8,128)(2,1)}, bf16[128,768]{1,0:T(8,128)(2,1)}, u32[]{:S(2)}, u32[]{:S(2)}) collective-permute-start(bf16[128,768]{1,0:T(8,128)(2,1)} %bitcast.11), channel_id=1, source_target_pairs={{0,8},{8,0},{1,9},{9,1},{2,10},{10,2},{3,11},{11,3},{4,12},{12,4},... | collective-permute-start | bytes 589832 | tf_op jit(solution)/shard_map/ppermute | solution.py:315
  17.3 2.9 %collective-permute-start.1 = (bf16[128,384]{1,0:T(8,128)(2,1)S(1)}, bf16[128,384]{1,0:T(8,128)(2,1)S(1)}, u32[]{:S(2)}, u32[]{:S(2)}) collective-permute-start(bf16[128,384]{1,0:T(8,128)(2,1)S(1)} %broadcast_select_fusion.8), channel_id=1, source_target_pairs={{0,1},{1,0},{2,3},{3,2},{4,5},{5,4},{6,7},{7,6},{8,9},{9,8},{10,11... | collective-permute-start | bytes 294920 | tf_op jit(solution)/shard_map/ppermute | solution.py:315
  20.2 1.4 broadcast_select_fusion.2
  25.2 1.2 broadcast_in_dim.13
  26.4 4.5 %all-to-all-start = ((bf16[4,256,768]{2,1,0:T(8,128)(2,1)}), bf16[4,256,768]{2,1,0:T(8,128)(2,1)}, u32[]{:S(2)}, u32[]{:S(2)}) async-start(bf16[4,256,768]{2,1,0:T(8,128)(2,1)} %broadcast_in_dim.13), calls=%async_computation | async-start | bytes 3145728 | tf_op jit(solution)/shard_map/all_to_all | solution.py:324
  31.0 9.8 %collective-permute-start.2 = (bf16[128,768]{1,0:T(8,128)(2,1)}, bf16[128,768]{1,0:T(8,128)(2,1)}, u32[]{:S(2)}, u32[]{:S(2)}) collective-permute-start(bf16[128,768]{1,0:T(8,128)(2,1)} %pad_maximum_fusion.3.d0), channel_id=1, source_target_pairs={{0,8},{8,0},{1,9},{9,1},{2,10},{10,2},{3,11},{11,3},{4,12},{12,4},... | collective-permute-start | bytes 589832 | tf_op jit(solution)/shard_map/ppermute | solution.py:315
  40.7 7.3 %collective-permute-done.2.d4 = bf16[128,768]{1,0:T(8,128)(2,1)} collective-permute-done((bf16[128,768]{1,0:T(8,128)(2,1)}, bf16[128,768]{1,0:T(8,128)(2,1)}, u32[]{:S(2)}, u32[]{:S(2)}) %collective-permute-start.2) | collective-permute-done | bytes 196640 | tf_op jit(solution)/shard_map/ppermute | solution.py:315
  48.1 2.1 %all-to-all-done.near = bf16[4,256,768]{2,1,0:T(8,128)(2,1)} async-done(((bf16[4,256,768]{2,1,0:T(8,128)(2,1)}), bf16[4,256,768]{2,1,0:T(8,128)(2,1)}, u32[]{:S(2)}, u32[]{:S(2)}) %all-to-all-start) | async-done | bytes 1572896 | tf_op jit(solution)/shard_map/all_to_all | solution.py:324
  50.1 2.7 %collective-permute-start.3 = (bf16[4,256,768]{2,1,0:T(8,128)(2,1)}, bf16[4,256,768]{2,1,0:T(8,128)(2,1)}, u32[]{:S(2)}, u32[]{:S(2)}) collective-permute-start(bf16[4,256,768]{2,1,0:T(8,128)(2,1)} %all-to-all-done.near), channel_id=1, source_target_pairs={{0,1},{1,0},{2,3},{3,2},{4,5},{5,4},{6,7},{7,6},{8,9},{9,8},{10,11... | collective-permute-start | bytes 4718600 | tf_op jit(solution)/shard_map/ppermute | solution.py:315
  52.8 1.6 constant_dynamic-update-slice_fusion.1
  54.5 1.6 constant_dynamic-update-slice_fusion
  56.1 1.9 %collective-permute-start.4 = (bf16[256,768]{1,0:T(8,128)(2,1)}, bf16[256,768]{1,0:T(8,128)(2,1)}, u32[]{:S(2)}, u32[]{:S(2)}) collective-permute-start(bf16[256,768]{1,0:T(8,128)(2,1)} %constant_dynamic-update-slice_fusion), channel_id=1, source_target_pairs={{2,0},{4,2},{6,4},{0,6},{3,1},{5,3},{7,5},{1,7},{10,8},{12,10},{14... | collective-permute-start | bytes 1179656 | tf_op jit(solution)/shard_map/ppermute | solution.py:319
  58.0 4.9 %collective-permute-start.5 = (bf16[256,768]{1,0:T(8,128)(2,1)}, bf16[256,768]{1,0:T(8,128)(2,1)}, u32[]{:S(2)}, u32[]{:S(2)}) collective-permute-start(bf16[256,768]{1,0:T(8,128)(2,1)} %constant_dynamic-update-slice_fusion), channel_id=1, source_target_pairs={{4,0},{6,2},{0,4},{2,6},{5,1},{7,3},{1,5},{3,7},{12,8},{14,10},{8,... | collective-permute-start | bytes 1179656 | tf_op jit(solution)/shard_map/ppermute | solution.py:319
  62.9 2.8 %collective-permute-start.6 = (bf16[256,768]{1,0:T(8,128)(2,1)}, bf16[256,768]{1,0:T(8,128)(2,1)}, u32[]{:S(2)}, u32[]{:S(2)}) collective-permute-start(bf16[256,768]{1,0:T(8,128)(2,1)} %constant_dynamic-update-slice_fusion), channel_id=1, source_target_pairs={{6,0},{0,2},{2,4},{4,6},{7,1},{1,3},{3,5},{5,7},{14,8},{8,10},{10,... | collective-permute-start | bytes 1179656 | tf_op jit(solution)/shard_map/ppermute | solution.py:319
  66.6 15.2 %shard_map.94 = (bf16[3,2048,128]{2,1,0:T(8,128)(2,1)S(1)}, bf16[3,2048,128]{2,1,0:T(8,128)(2,1)S(1)}, bf16[3,2048,128]{2,1,0:T(8,128)(2,1)S(1)}, bf16[160,768]{1,0:T(8,128)(2,1)S(1)}) custom-call(s32[3]{0:T(128)S(1)} %pad_add_fusion.pos, bf16[4,256,768]{2,1,0:T(8,128)(2,1)} %all-to-all-done.near, bf16[4,256,768]{2,1,0:T(8,128)(2,1)} %collective-permute-done.3.other, ...), custom_call_target="tpu_custom_call" | custom-call | tf_op jit(solution)/shard_map/pallas_call | solution.py:40
  81.8 10.0 %shard_map.95 = (bf16[3,256,128]{2,1,0:T(8,128)(2,1)S(1)}, f32[8,512]{1,0:T(8,128)S(1)}) custom-call(bf16[3,2048,128]{2,1,0:T(8,128)(2,1)S(1)} %get-tuple-element.29.q, bf16[3,2048,128]{2,1,0:T(8,128)(2,1)S(1)} %get-tuple-element.30.k, bf16[3,2048,128]{2,1,0:T(8,128)(2,1)S(1)} %get-tuple-element.31.v, bf16[128,768]{1,0:T(8,128)(2,1)S(1)} %copy-done, ...), custom_call_target="tpu_custom_call" | custom-call | tf_op jit(solution)/shard_map/pallas_call | solution.py:40
  91.8 6.8 %all_to_all.20.stats = f32[4,8,512]{2,1,0:T(8,128)S(1)} all-to-all(f32[4,8,512]{2,1,0:T(8,128)S(1)} %broadcast_in_dim.14), channel_id=1, replica_groups=mesh['y'=4,'zm'=2,'zl'=4,'zh'=2,'x'=4,'core'=2] {'x'}, dimensions={0} | all-to-all | bytes 131072 | tf_op jit(solution)/shard_map/all_to_all | solution.py:324
  98.6 10.7 %shard_map.96 = (bf16[160,1152]{1,0:T(8,128)(2,1)S(1)}, bf16[160,1152]{1,0:T(8,128)(2,1)S(1)}) custom-call(s32[3]{0:T(128)S(1)} %pad_add_fusion.pos, bf16[3,2048,128]{2,1,0:T(8,128)(2,1)S(1)} %get-tuple-element.29.q, bf16[3,2048,128]{2,1,0:T(8,128)(2,1)S(1)} %get-tuple-element.30.k, bf16[3,2048,128]{2,1,0:T(8,128)(2,1)S(1)} %get-tuple-element.31.v, ...), custom_call_target="tpu_custom_call" | custom-call | tf_op jit(solution)/shard_map/pallas_call | solution.py:40
  109.4 4.3 %collective-permute-start.7 = (bf16[160,1152]{1,0:T(8,128)(2,1)S(1)}, bf16[160,1152]{1,0:T(8,128)(2,1)S(1)}, u32[]{:S(2)}, u32[]{:S(2)}) collective-permute-start(bf16[160,1152]{1,0:T(8,128)(2,1)S(1)} %get-tuple-element.40), channel_id=1, source_target_pairs={{0,1},{1,0},{2,3},{3,2},{4,5},{5,4},{6,7},{7,6},{8,9},{9,8},{10,11... | collective-permute-start | bytes 1105928 | tf_op jit(solution)/shard_map/ppermute | solution.py:315
  114.8 3.9 %shard_map.97 = (bf16[128,768]{1,0:T(8,128)(2,1)}, f32[2,16,128]{2,1,0:T(8,128)S(1)}) custom-call(s32[3]{0:T(128)S(1)} %pad_add_fusion.pos, bf16[160,1152]{1,0:T(8,128)(2,1)S(1)} %get-tuple-element.39.mine, bf16[160,1152]{1,0:T(8,128)(2,1)S(1)} %collective-permute-done.7.recv, bf16[768,1152]{1,0:T(8,128)(2,1)S(1)} %pad_maximum_fusion.w.w_own, ...), custom_call_target="tpu_custom_call" | custom-call | tf_op jit(solution)/shard_map/pallas_call | solution.py:40
  118.7 14.6 %all_to_all.21 = f32[32,16,128]{2,1,0:T(8,128)S(1)} all-to-all(f32[32,16,128]{2,1,0:T(8,128)S(1)} %bitcast.8), channel_id=1, replica_groups=mesh['y'=4,'zm'=2,'zl'=4,'zh'=2,'x'=4,'core'=2] {'y','x','core'}, dimensions={0} | all-to-all | bytes 524288 | tf_op jit(solution)/shard_map/all_to_all | solution.py:404
  133.3 36.2 %all_to_all.22 = bf16[16,16,128]{2,1,0:T(8,128)(2,1)S(1)} all-to-all(bf16[16,16,128]{2,1,0:T(8,128)(2,1)S(1)} %broadcast_in_dim.17), channel_id=1, replica_groups=mesh['y'=4,'zm'=2,'zl'=4,'zh'=2,'x'=4,'core'=2] {'zm','zl','zh'}, dimensions={0} | all-to-all | bytes 131072 | tf_op jit(solution)/shard_map/all_to_all | solution.py:324
  169.5 3.3 %all-gather = f32[32,128]{1,0:T(8,128)S(1)} all-gather(f32[16,128]{1,0:T(8,128)S(1)} %convert_reduce_fusion), channel_id=2, replica_groups=mesh['y'=4,'zm'=2,'zl'=4,'zh'=2,'x'=4,'core'=2] {'core'}, dimensions={0}, use_global_device_ids=true | all-gather | bytes 24576 | tf_op jit(solution)/shard_map/all_gather | solution.py:407
  172.9 1.9 %multiply_reduce_fusion = (f32[768]{0:T(1024)}, f32[5,768]{1,0:T(8,128)}) fusion(f32[5,768]{1,0:T(8,128)S(1)} %constant_dynamic-update-slice_fusion.2, f32[5,768]{1,0:T(8,128)} %param.9, f32[768]{0:T(1024)S(1)} %copy-done.7), kind=kLoop, calls=%fused_computation.16 | loop fusion | flops 10752 | bytes 52224 | tf_op jit(solution)/shard_map/reduce_sum | solution.py:410
  (45 shorter events, 6.7 us)
Async XLA Ops:
  0.6 20.9 %copy-start.7 = (f32[768]{0:T(1024)S(1)}, f32[768]{0:T(1024)}, u32[]{:S(2)}) copy-start(f32[768]{0:T(1024)} %param.8) | copy-start | bytes 9220
  0.6 20.9 %copy-start.2 = (bf16[768,768]{1,0:T(8,128)(2,1)S(1)}, bf16[768,768]{1,0:T(8,128)(2,1)}, u32[]{:S(2)}) copy-start(bf16[768,768]{1,0:T(8,128)(2,1)} %param.12) | copy-start | bytes 3538948
  0.7 23.6 %collective-permute-start = (bf16[128,768]{1,0:T(8,128)(2,1)}, bf16[128,768]{1,0:T(8,128)(2,1)}, u32[]{:S(2)}, u32[]{:S(2)}) collective-permute-start(bf16[128,768]{1,0:T(8,128)(2,1)} %bitcast.11), channel_id=1, source_target_pairs={{0,8},{8,0},{1,9},{9,1},{2,10},{10,2},{3,11},{11,3},{4,12},{12,4},... | collective-permute-start | bytes 589832 | tf_op jit(solution)/shard_map/ppermute | solution.py:315
  16.2 5.3 %copy-start.3 = (bf16[768,768]{1,0:T(8,128)(2,1)S(1)}, bf16[768,768]{1,0:T(8,128)(2,1)}, u32[]{:S(2)}) copy-start(bf16[768,768]{1,0:T(8,128)(2,1)} %param.11) | copy-start | bytes 3538948
  17.3 6.2 %collective-permute-start.1 = (bf16[128,384]{1,0:T(8,128)(2,1)S(1)}, bf16[128,384]{1,0:T(8,128)(2,1)S(1)}, u32[]{:S(2)}, u32[]{:S(2)}) collective-permute-start(bf16[128,384]{1,0:T(8,128)(2,1)S(1)} %broadcast_select_fusion.8), channel_id=1, source_target_pairs={{0,1},{1,0},{2,3},{3,2},{4,5},{5,4},{6,7},{7,6},{8,9},{9,8},{10,11... | collective-permute-start | bytes 294920 | tf_op jit(solution)/shard_map/ppermute | solution.py:315
  22.1 0.7 copy-start.6
  22.1 1.4 copy-start.4
  22.1 2.1 %copy-start.5 = (bf16[1,128,768]{2,1,0:T(8,128)(2,1)S(1)}, bf16[1,128,768]{2,1,0:T(8,128)(2,1)}, u32[]{:S(2)}) copy-start(bf16[1,128,768]{2,1,0:T(8,128)(2,1)} %param.7) | copy-start | bytes 589828
  26.4 23.7 %all-to-all-start = ((bf16[4,256,768]{2,1,0:T(8,128)(2,1)}), bf16[4,256,768]{2,1,0:T(8,128)(2,1)}, u32[]{:S(2)}, u32[]{:S(2)}) async-start(bf16[4,256,768]{2,1,0:T(8,128)(2,1)} %broadcast_in_dim.13), calls=%async_computation | async-start | bytes 3145728 | tf_op jit(solution)/shard_map/all_to_all | solution.py:324
  31.0 17.1 %collective-permute-start.2 = (bf16[128,768]{1,0:T(8,128)(2,1)}, bf16[128,768]{1,0:T(8,128)(2,1)}, u32[]{:S(2)}, u32[]{:S(2)}) collective-permute-start(bf16[128,768]{1,0:T(8,128)(2,1)} %pad_maximum_fusion.3.d0), channel_id=1, source_target_pairs={{0,8},{8,0},{1,9},{9,1},{2,10},{10,2},{3,11},{11,3},{4,12},{12,4},... | collective-permute-start | bytes 589832 | tf_op jit(solution)/shard_map/ppermute | solution.py:315
  50.1 15.6 %collective-permute-start.3 = (bf16[4,256,768]{2,1,0:T(8,128)(2,1)}, bf16[4,256,768]{2,1,0:T(8,128)(2,1)}, u32[]{:S(2)}, u32[]{:S(2)}) collective-permute-start(bf16[4,256,768]{2,1,0:T(8,128)(2,1)} %all-to-all-done.near), channel_id=1, source_target_pairs={{0,1},{1,0},{2,3},{3,2},{4,5},{5,4},{6,7},{7,6},{8,9},{9,8},{10,11... | collective-permute-start | bytes 4718600 | tf_op jit(solution)/shard_map/ppermute | solution.py:315
  56.1 35.7 %collective-permute-start.4 = (bf16[256,768]{1,0:T(8,128)(2,1)}, bf16[256,768]{1,0:T(8,128)(2,1)}, u32[]{:S(2)}, u32[]{:S(2)}) collective-permute-start(bf16[256,768]{1,0:T(8,128)(2,1)} %constant_dynamic-update-slice_fusion), channel_id=1, source_target_pairs={{2,0},{4,2},{6,4},{0,6},{3,1},{5,3},{7,5},{1,7},{10,8},{12,10},{14... | collective-permute-start | bytes 1179656 | tf_op jit(solution)/shard_map/ppermute | solution.py:319
  58.0 33.8 %collective-permute-start.5 = (bf16[256,768]{1,0:T(8,128)(2,1)}, bf16[256,768]{1,0:T(8,128)(2,1)}, u32[]{:S(2)}, u32[]{:S(2)}) collective-permute-start(bf16[256,768]{1,0:T(8,128)(2,1)} %constant_dynamic-update-slice_fusion), channel_id=1, source_target_pairs={{4,0},{6,2},{0,4},{2,6},{5,1},{7,3},{1,5},{3,7},{12,8},{14,10},{8,... | collective-permute-start | bytes 1179656 | tf_op jit(solution)/shard_map/ppermute | solution.py:319
  62.9 28.9 %collective-permute-start.6 = (bf16[256,768]{1,0:T(8,128)(2,1)}, bf16[256,768]{1,0:T(8,128)(2,1)}, u32[]{:S(2)}, u32[]{:S(2)}) collective-permute-start(bf16[256,768]{1,0:T(8,128)(2,1)} %constant_dynamic-update-slice_fusion), channel_id=1, source_target_pairs={{6,0},{0,2},{2,4},{4,6},{7,1},{1,3},{3,5},{5,7},{14,8},{8,10},{10,... | collective-permute-start | bytes 1179656 | tf_op jit(solution)/shard_map/ppermute | solution.py:319
  65.8 16.0 %copy-start = (bf16[128,768]{1,0:T(8,128)(2,1)S(1)}, bf16[128,768]{1,0:T(8,128)(2,1)}, u32[]{:S(2)}) copy-start(bf16[128,768]{1,0:T(8,128)(2,1)} %pad_maximum_fusion.3.d0) | copy-start | bytes 589828
  65.8 0.8 copy-start.1
  109.4 5.4 %collective-permute-start.7 = (bf16[160,1152]{1,0:T(8,128)(2,1)S(1)}, bf16[160,1152]{1,0:T(8,128)(2,1)S(1)}, u32[]{:S(2)}, u32[]{:S(2)}) collective-permute-start(bf16[160,1152]{1,0:T(8,128)(2,1)S(1)} %get-tuple-element.40), channel_id=1, source_target_pairs={{0,1},{1,0},{2,3},{3,2},{4,5},{5,4},{6,7},{7,6},{8,9},{9,8},{10,11... | collective-permute-start | bytes 1105928 | tf_op jit(solution)/shard_map/ppermute | solution.py:315

commit v6 on v5

--- a/solution.py
+++ b/solution.py
@@ -34,8 +34,10 @@
     return pl.BlockSpec(memory_space=pltpu.SMEM)
 
 
-def call(body, out_shape, args, scratch=(), limit=16):
+def call(body, out_shape, args, scratch=(), limit=16, held=()):
     specs = [sspec() if a.dtype == jnp.int32 else vspec() for a in args]
+    for i in held:
+        specs[i] = pl.BlockSpec(memory_space=pltpu.HBM)
     outs = jax.tree.map(lambda _: vspec(), out_shape)
     return pl.pallas_call(
         body,
@@ -73,59 +75,130 @@
     return rows * lax.rsqrt(jnp.mean(rows * rows, axis=-1, keepdims=True) + EPSILON)
 
 
-def hidden_body(
-    pos, near, other, w, taps, q, k, v, ext, xs, ns, hs
+def activate(ns, r, n, cols, tap):
+    u = tap[0] * ns[r - 2 : r - 2 + n, cols]
+    for t in range(1, 5):
+        u = u + tap[t] * ns[r - 2 + t : r - 2 + t + n, cols]
+    inner = GELU_ROOT * (u + 0.044715 * u * u * u)
+    return 0.5 * u * (1.0 + jnp.tanh(inner))
+
+
+def hidden_chunk(xs, c, low, high, taps, ns, hs):
+    g = taps[5:6, :]
+    ns[0:16, :] = normalize(low) * g
+    ns[272:288, :] = normalize(high) * g
+    for r in range(0, CHUNK, 16):
+        ns[16 + r : 32 + r, :] = normalize(xs[c, r : r + 16, :].astype(F32)) * g
+    for j in range(0, C, 128):
+        tap = [taps[t : t + 1, j : j + 128] for t in range(5)]
+        cols = slice(j, j + 128)
+        for r in range(0, CHUNK, 64):
+            act = activate(ns, 16 + r, 64, cols, tap)
+            x = xs[c, r : r + 64, cols].astype(F32)
+            hs[r : r + 64, cols] = (x + act).astype(BF16)
+
+
+def project(rows, w, q, k, v, at, n):
+    y = nn(rows, w[...]).astype(BF16)
+    for h in range(OWN_HEADS):
+        q[h, pl.ds(at, n), :] = y[:, h * 128 : (h + 1) * 128]
+        k[h, pl.ds(at, n), :] = y[:, HALF + h * 128 : HALF + (h + 1) * 128]
+        v[h, pl.ds(at, n), :] = y[:, 2 * HALF + h * 128 : 2 * HALF + (h + 1) * 128]
+
+
+def assemble(pos, near, other, xs):
+    here = pl.multiple_of(pos[2] * BLOCK, BLOCK)
+    there = pl.multiple_of((1 - pos[2]) * BLOCK, BLOCK)
+    for c in range(4):
+        xa = lax.rem(pos[1] + c, 4)
+        xs[c, pl.ds(here, BLOCK), :] = near[xa]
+        xs[c, pl.ds(there, BLOCK), :] = other[xa]
+
+
+def own_half_body(pos, near, other, w, taps, q, k, v, xs, ns, hs):
+    assemble(pos, near, other, xs)
+
+    def chunk(c, _):
+        xa = lax.rem(pos[1] + c, 4)
+        low = xs[lax.rem(c + 3, 4), 240:256, :].astype(F32) * (xa > 0).astype(F32)
+        high = xs[lax.rem(c + 1, 4), 0:16, :].astype(F32) * (xa < 3).astype(F32)
+        hidden_chunk(xs, c, low, high, taps, ns, hs)
+        project(hs[...], w, q, k, v, pl.multiple_of(c * CHUNK, CHUNK), CHUNK)
+        return 0
+
+    lax.fori_loop(0, 4, chunk, 0)
+
+
+def far_half_body(
+    pos, near, other, own_in, q0, k0, v0, w, taps, q, k, v, ext, xs, ns, hs, rs, own, sem
 ):
-    core = pos[2]
-    here = pl.multiple_of(core * BLOCK, BLOCK)
-    there = pl.multiple_of((1 - core) * BLOCK, BLOCK)
-    for c in range(CHUNKS):
-        xa = lax.rem(pos[1] + c % 4, 4)
-        sl = slice((c // 4) * BLOCK, (c // 4 + 1) * BLOCK)
-        xs[c, pl.ds(here, BLOCK), :] = near[xa, sl, :]
-        xs[c, pl.ds(there, BLOCK), :] = other[xa, sl, :]
-    prev, nxt, prev_ok, nxt_ok = neighbours(pos, jnp.int32(0), jnp.int32(0))
-    first = core == 0
-    ext[16:144, :] = near[pos[1], 0:BLOCK, :]
-
-    @pl.when(first)
+    pairs = ((own_in, own), (q0, q), (k0, k), (v0, v))
+    copies = [
+        pltpu.make_async_copy(src, dst if i == 0 else dst.at[:, 0:1024, :], sem.at[i])
+        for i, (src, dst) in enumerate(pairs)
+    ]
+    for copy in copies:
+        copy.start()
+    assemble(pos, near, other, xs)
+    copies[0].wait()
+    zh, x, core = pos[0], pos[1], pos[2]
+
+    def chunk(c, _):
+        xa = lax.rem(x + c, 4)
+        lo, hi = lax.rem(c + 3, 4), lax.rem(c + 1, 4)
+        wrap_lo, wrap_hi = (xa == 0).astype(F32), (xa == 3).astype(F32)
+        low_ok, high_ok = (zh == 0).astype(F32), (zh == 1).astype(F32)
+        low = xs[lo, 240:256, :].astype(F32) * (1.0 - wrap_lo)
+        low = low + own[lo, 240:256, :].astype(F32) * (wrap_lo * low_ok)
+        high = xs[hi, 0:16, :].astype(F32) * (1.0 - wrap_hi)
+        high = high + own[hi, 0:16, :].astype(F32) * (wrap_hi * high_ok)
+        hidden_chunk(xs, c, low, high, taps, ns, hs)
+        project(hs[...], w, q, k, v, pl.multiple_of(1024 + c * CHUNK, CHUNK), CHUNK)
+        return 0
+
+    lax.fori_loop(0, 4, chunk, 0)
+
+    edge = lax.rem(jnp.where(zh == 0, 3, 4) - x, 4)
+
+    @pl.when(zh == 0)
     def _():
-        ext[0:16, :] = (xs[prev, 240:256, :].astype(F32) * prev_ok).astype(BF16)
-        ext[144:160, :] = xs[0, 128:144, :]
-
-    @pl.when(jnp.logical_not(first))
+        rs[0:32, :] = own[edge, 224:256, :]
+        rs[32:48, :] = xs[lax.rem(edge + 1, 4), 0:16, :]
+
+    @pl.when(zh == 1)
     def _():
-        ext[0:16, :] = xs[0, 112:128, :]
-        ext[144:160, :] = (xs[nxt, 0:16, :].astype(F32) * nxt_ok).astype(BF16)
-
-    def chunk(c, _):
-        dz = lax.div(c, 4)
-        dx = lax.rem(c, 4)
-        prev, nxt, prev_ok, nxt_ok = neighbours(pos, dz, dx)
-        g = taps[5:6, :]
-        ns[0:16, :] = normalize(xs[prev, 240:256, :].astype(F32)) * g * prev_ok
-        ns[272:288, :] = normalize(xs[nxt, 0:16, :].astype(F32)) * g * nxt_ok
-        for r in range(0, CHUNK, 16):
-            ns[16 + r : 32 + r, :] = normalize(xs[c, r : r + 16, :].astype(F32)) * g
-        for j in range(0, C, 128):
-            tap = [taps[t : t + 1, j : j + 128] for t in range(5)]
-            for r in range(0, CHUNK, 64):
-                u = tap[0] * ns[14 + r : 78 + r, j : j + 128]
-                for t in range(1, 5):
-                    u = u + tap[t] * ns[14 + r + t : 78 + r + t, j : j + 128]
-                inner = GELU_ROOT * (u + 0.044715 * u * u * u)
-                act = 0.5 * u * (1.0 + jnp.tanh(inner))
-                x = xs[c, r : r + 64, j : j + 128].astype(F32)
-                hs[r : r + 64, j : j + 128] = (x + act).astype(BF16)
-        y = nn(hs[...], w[...]).astype(BF16)
-        at = pl.multiple_of(c * CHUNK, CHUNK)
-        for h in range(OWN_HEADS):
-            q[h, pl.ds(at, CHUNK), :] = y[:, h * 128 : (h + 1) * 128]
-            k[h, pl.ds(at, CHUNK), :] = y[:, HALF + h * 128 : HALF + (h + 1) * 128]
-            v[h, pl.ds(at, CHUNK), :] = y[:, 2 * HALF + h * 128 : 2 * HALF + (h + 1) * 128]
-        return 0
-
-    lax.fori_loop(0, CHUNKS, chunk, 0)
+        rs[0:16, :] = xs[lax.rem(edge + 3, 4), 240:256, :]
+        rs[16:48, :] = own[edge, 0:32, :]
+
+    for r in range(0, 48, 16):
+        ns[r : r + 16, :] = normalize(rs[r : r + 16, :].astype(F32)) * taps[5:6, :]
+    for j in range(0, C, 128):
+        tap = [taps[t : t + 1, j : j + 128] for t in range(5)]
+        cols = slice(j, j + 128)
+        act = activate(ns, 16, 16, cols, tap)
+        hs[0:16, cols] = (rs[16:32, cols].astype(F32) + act).astype(BF16)
+    for copy in copies[1:]:
+        copy.wait()
+    at = pl.multiple_of(edge * CHUNK + jnp.where(zh == 0, 240, 0), 16)
+    project(hs[0:16, :], w, q, k, v, at, 16)
+
+    ext[16:144, :] = own[0, pl.ds(pl.multiple_of(core * BLOCK, BLOCK), BLOCK), :]
+
+    @pl.when(core == 0)
+    def _():
+        ext[144:160, :] = own[0, 128:144, :]
+        inside = (x > 0).astype(F32)
+        across = (1.0 - inside) * (zh == 1).astype(F32)
+        low = own[3, 240:256, :].astype(F32) * inside + xs[3, 240:256, :].astype(F32) * across
+        ext[0:16, :] = low.astype(BF16)
+
+    @pl.when(core == 1)
+    def _():
+        ext[0:16, :] = own[0, 112:128, :]
+        inside = (x < 3).astype(F32)
+        across = (1.0 - inside) * (zh == 0).astype(F32)
+        high = own[1, 0:16, :].astype(F32) * inside + xs[1, 0:16, :].astype(F32) * across
+        ext[144:160, :] = high.astype(BF16)
 
 
 KB = 512
@@ -348,22 +421,39 @@
     w_own = jnp.concatenate([p[0] for p in parts], axis=1)
     w_oth = jnp.concatenate([p[1] for p in parts], axis=1)
     coef = jnp.concatenate([conv_taps, gain, jnp.zeros((2, C), F32)], axis=0)
-    sig_z, cot_own, w_own, w_oth, coef = lax.optimization_barrier(
-        (sig_z, cot_own, w_own, w_oth, coef)
-    )
+    near = share(sig, "x", 4)
+    sig_z, cot_own, w_own, w_oth, coef, near = lax.optimization_barrier(
+        (sig_z, cot_own, w_own, w_oth, coef, near)
+    )
+    near_other = swap(near, "core")
     cot_z = swap(cot_own, "zh")
-    near = share(jnp.concatenate([sig, sig_z], axis=0), "x", 4)
-    near, cot_z = lax.optimization_barrier((near, cot_z))
-    other = swap(near, "core")
+    far = share(sig_z, "x", 4)
+    half_shape = jax.ShapeDtypeStruct((OWN_HEADS, 1024, HEAD_DIM), BF16)
+    rows_shape = jax.ShapeDtypeStruct((4, CHUNK, C), BF16)
+    q0, k0, v0, own = call(
+        own_half_body,
+        (half_shape, half_shape, half_shape, rows_shape),
+        (pos, near, near_other, w_own, coef),
+        (VM((288, C), F32), VM((CHUNK, C), BF16)),
+    )
+    far, q0, cot_z = lax.optimization_barrier((far, q0, cot_z))
+    far_other = swap(far, "core")
     both = jnp.concatenate([cot_own, cot_z], axis=0)
     cots = [from_x(both, d) for d in (1, 2, 3)]
-
     head_shape = jax.ShapeDtypeStruct((OWN_HEADS, BINS, HEAD_DIM), BF16)
     q, k, v, ext = call(
-        hidden_body,
+        far_half_body,
         (head_shape, head_shape, head_shape, jax.ShapeDtypeStruct((160, C), BF16)),
-        (pos, near, other, w_own, coef),
-        (VM((CHUNKS, CHUNK, C), BF16), VM((288, C), F32), VM((CHUNK, C), BF16)),
+        (pos, far, far_other, own, q0, k0, v0, w_own, coef),
+        (
+            VM((4, CHUNK, C), BF16),
+            VM((288, C), F32),
+            VM((CHUNK, C), BF16),
+            VM((48, C), BF16),
+            VM((4, CHUNK, C), BF16),
+            pltpu.SemaphoreType.DMA((4,)),
+        ),
+        held=(3, 4, 5, 6),
     )
     part = jax.ShapeDtypeStruct((OWN_HEADS, CHUNK, HEAD_DIM), BF16)
     dq, stats = call(

time: 178 us -> 183 us (1.028)
  blocking collectives: 60.9 us -> 45.2 us
  local copies, waits for them, and re-layouts: 5.97 us -> 17.6 us
  starting transfers between devices: 49.3 us -> 57.1 us
    all_to_all x2, blocking collectives: 43.1 us -> 29.6 us  [share(): return lax.all_to_all(wide, axes, 0, 0)]
    unnamed x18 -> x36, local copies, waits for them, and re-layouts: 2.99 us -> 12.8 us
    all_to_all x1 -> x2, starting transfers between devices: 4.51 us -> 10.4 us  [share(): return lax.all_to_all(wide, axes, 0, 0)]
    ppermute x5 -> x6, waiting for transfers between devices: 8.45 us -> 4.45 us  [swap(): return lax.ppermute(a, axis, [(0, 1), (1, 0)])]
    all_to_all x1 -> x2, waiting for transfers between devices: 2.07 us -> 5.79 us  [share(): return lax.all_to_all(wide, axes, 0, 0)]
    ppermute x5 -> x6, starting transfers between devices: 35.2 us -> 37.7 us  [swap(): return lax.ppermute(a, axis, [(0, 1), (1, 0)])]
    broadcast_in_dim x3 -> x4, local copies, waits for them, and re-layouts: 1.26 us -> 3.79 us  [share(): wide = jnp.broadcast_to(a[None], (size,) + a.shape)]
    all_to_all x1, blocking collectives: 14.6 us -> 12.3 us  [shards(): part = jnp.sum(lax.all_to_all(wide, ('y', 'x', 'core'), 0, 0), axis=0)]
  transfers between devices with their start and end apart: 9 -> 11, of which waited for: 3 -> 3; matrix products, arithmetic and copies ran while one was open for 4% -> 6% of each run, Pallas kernels for 14% -> 15%
where the time goes in v6:
time: 183 us; the launch traced here: 179 us
  starting transfers between devices  57.1 us (31%)
  blocking collectives  45.2 us (25%)
  Pallas kernels  41.3 us (23%)
  local copies, waits for them, and re-layouts  17.6 us (10%)
  waiting for transfers between devices  10.3 us (6%)
  other arithmetic  6.68 us (4%)
    pallas_call x5, Pallas kernels, call(): pl.pallas_call(body, out_shape=out_shape, in_specs=specs, out_specs=outs,...  41.3 us
    ppermute x6, starting transfers between devices, swap(): return lax.ppermute(a, axis, [(0, 1), (1, 0)])  37.7 us
    all_to_all x2, blocking collectives, share(): return lax.all_to_all(wide, axes, 0, 0)  29.6 us
    unnamed x36, local copies, waits for them, and re-layouts  12.8 us
    all_to_all x1, blocking collectives, shards(): part = jnp.sum(lax.all_to_all(wide, ('y', 'x', 'core'), 0, 0), axis=0)  12.3 us
    all_to_all x2, starting transfers between devices, share(): return lax.all_to_all(wide, axes, 0, 0)  10.4 us
    ppermute x3, starting transfers between devices, from_x(): return lax.ppermute(a, 'x', [((i + step) % 4, i) for i in range(4)])  8.97 us
    all_to_all x2, waiting for transfers between devices, share(): return lax.all_to_all(wide, axes, 0, 0)  5.79 us
  transfers between devices with their start and end apart: 11, of which 3 were waited for; matrix products, arithmetic and copies ran while one was open for 6% of the time, Pallas kernels for 15%

profile of v6, /device:TPU:7, one launch (start us, length us, event | category | flops | bytes accessed | tf_op | source)
XLA Modules:
  0.0 179.1 jit_solution(16782416970039144833)
XLA Ops:
  0.6 15.6 %collective-permute-start = (bf16[128,768]{1,0:T(8,128)(2,1)}, bf16[128,768]{1,0:T(8,128)(2,1)}, u32[]{:S(2)}, u32[]{:S(2)}) collective-permute-start(bf16[128,768]{1,0:T(8,128)(2,1)} %bitcast.11), channel_id=1, source_target_pairs={{0,8},{8,0},{1,9},{9,1},{2,10},{10,2},{3,11},{11,3},{4,12},{12,4},... | collective-permute-start | bytes 589832 | tf_op jit(solution)/shard_map/ppermute | solution.py:388
  17.8 2.9 %collective-permute-start.1 = (bf16[128,384]{1,0:T(8,128)(2,1)}, bf16[128,384]{1,0:T(8,128)(2,1)}, u32[]{:S(2)}, u32[]{:S(2)}) collective-permute-start(bf16[128,384]{1,0:T(8,128)(2,1)} %broadcast_select_fusion.8), channel_id=1, source_target_pairs={{0,1},{1,0},{2,3},{3,2},{4,5},{5,4},{6,7},{7,6},{8,9},{9,8},{10,11... | collective-permute-start | bytes 294920 | tf_op jit(solution)/shard_map/ppermute | solution.py:388
  20.7 1.9 %broadcast_in_dim.15 = bf16[4,128,768]{2,1,0:T(8,128)(2,1)} broadcast(bf16[128,768]{1,0:T(8,128)(2,1)} %bitcast.12), dimensions={1,2} | broadcast | bytes 983040 | tf_op jit(solution)/shard_map/broadcast_in_dim | solution.py:396
  22.6 4.5 %all-to-all-start = ((bf16[4,128,768]{2,1,0:T(8,128)(2,1)}), bf16[4,128,768]{2,1,0:T(8,128)(2,1)}, u32[]{:S(2)}, u32[]{:S(2)}) async-start(bf16[4,128,768]{2,1,0:T(8,128)(2,1)} %broadcast_in_dim.15), calls=%async_computation | async-start | bytes 1572864 | tf_op jit(solution)/shard_map/all_to_all | solution.py:397
  31.9 5.8 %all-to-all-done.near = bf16[4,128,768]{2,1,0:T(8,128)(2,1)} async-done(((bf16[4,128,768]{2,1,0:T(8,128)(2,1)}), bf16[4,128,768]{2,1,0:T(8,128)(2,1)}, u32[]{:S(2)}, u32[]{:S(2)}) %all-to-all-start) | async-done | bytes 786464 | tf_op jit(solution)/shard_map/all_to_all | solution.py:397
  37.7 2.9 %collective-permute-start.2 = (bf16[4,128,768]{2,1,0:T(8,128)(2,1)}, bf16[4,128,768]{2,1,0:T(8,128)(2,1)}, u32[]{:S(2)}, u32[]{:S(2)}) collective-permute-start(bf16[4,128,768]{2,1,0:T(8,128)(2,1)} %all-to-all-done.near), channel_id=1, source_target_pairs={{0,1},{1,0},{2,3},{3,2},{4,5},{5,4},{6,7},{7,6},{8,9},{9,8},{10,11... | collective-permute-start | bytes 2359304 | tf_op jit(solution)/shard_map/ppermute | solution.py:388
  42.4 6.0 %all-to-all-start.1 = ((bf16[4,128,768]{2,1,0:T(8,128)(2,1)}), bf16[4,128,768]{2,1,0:T(8,128)(2,1)}, u32[]{:S(2)}, u32[]{:S(2)}) async-start(bf16[4,128,768]{2,1,0:T(8,128)(2,1)} %broadcast_in_dim.16), calls=%async_computation.1 | async-start | bytes 1572864 | tf_op jit(solution)/shard_map/all_to_all | solution.py:397
  48.4 3.9 %collective-permute-start.3 = (bf16[128,768]{1,0:T(8,128)(2,1)}, bf16[128,768]{1,0:T(8,128)(2,1)}, u32[]{:S(2)}, u32[]{:S(2)}) collective-permute-start(bf16[128,768]{1,0:T(8,128)(2,1)} %pad_maximum_fusion.2.d0), channel_id=1, source_target_pairs={{0,8},{8,0},{1,9},{9,1},{2,10},{10,2},{3,11},{11,3},{4,12},{12,4},... | collective-permute-start | bytes 589832 | tf_op jit(solution)/shard_map/ppermute | solution.py:388
  53.1 8.0 %shard_map.94 = (bf16[3,1024,128]{2,1,0:T(8,128)(2,1)S(1)}, bf16[3,1024,128]{2,1,0:T(8,128)(2,1)S(1)}, bf16[3,1024,128]{2,1,0:T(8,128)(2,1)S(1)}, bf16[4,256,768]{2,1,0:T(8,128)(2,1)S(1)}) custom-call(s32[3]{0:T(128)S(1)} %pad_add_fusion.pos, bf16[4,128,768]{2,1,0:T(8,128)(2,1)} %all-to-all-done.near, bf16[4,128,768]{2,1,0:T(8,128)(2,1)} %collective-permute-done.2.other, ...), custom_call_target="tpu_custom_call" | custom-call | tf_op jit(solution)/shard_map/pallas_call | solution.py:42
  65.1 3.1 %collective-permute-done.3.d4 = bf16[128,768]{1,0:T(8,128)(2,1)} collective-permute-done((bf16[128,768]{1,0:T(8,128)(2,1)}, bf16[128,768]{1,0:T(8,128)(2,1)}, u32[]{:S(2)}, u32[]{:S(2)}) %collective-permute-start.3) | collective-permute-done | bytes 196640 | tf_op jit(solution)/shard_map/ppermute | solution.py:388
  68.2 8.5 %collective-permute-start.4 = (bf16[4,128,768]{2,1,0:T(8,128)(2,1)}, bf16[4,128,768]{2,1,0:T(8,128)(2,1)S(1)}, u32[]{:S(2)}, u32[]{:S(2)}) collective-permute-start(bf16[4,128,768]{2,1,0:T(8,128)(2,1)} %all-to-all-done.1.near), channel_id=1, source_target_pairs={{0,1},{1,0},{2,3},{3,2},{4,5},{5,4},{6,7},{7,6},{8,9},{9,8},{10,11... | collective-permute-start | bytes 2359304 | tf_op jit(solution)/shard_map/ppermute | solution.py:388
  78.6 2.5 %collective-permute-start.5 = (bf16[256,768]{1,0:T(8,128)(2,1)S(1)}, bf16[256,768]{1,0:T(8,128)(2,1)S(1)}, u32[]{:S(2)}, u32[]{:S(2)}) collective-permute-start(bf16[256,768]{1,0:T(8,128)(2,1)S(1)} %constant_dynamic-update-slice_fusion), channel_id=1, source_target_pairs={{2,0},{4,2},{6,4},{0,6},{3,1},{5,3},{7,5},{1,7},{10,8},{12,10},{14... | collective-permute-start | bytes 1179656 | tf_op jit(solution)/shard_map/ppermute | solution.py:392
  81.1 2.6 %collective-permute-start.6 = (bf16[256,768]{1,0:T(8,128)(2,1)S(1)}, bf16[256,768]{1,0:T(8,128)(2,1)S(1)}, u32[]{:S(2)}, u32[]{:S(2)}) collective-permute-start(bf16[256,768]{1,0:T(8,128)(2,1)S(1)} %constant_dynamic-update-slice_fusion), channel_id=1, source_target_pairs={{4,0},{6,2},{0,4},{2,6},{5,1},{7,3},{1,5},{3,7},{12,8},{14,10},{8,... | collective-permute-start | bytes 1179656 | tf_op jit(solution)/shard_map/ppermute | solution.py:392
  83.6 3.9 %collective-permute-start.7 = (bf16[256,768]{1,0:T(8,128)(2,1)S(1)}, bf16[256,768]{1,0:T(8,128)(2,1)S(1)}, u32[]{:S(2)}, u32[]{:S(2)}) collective-permute-start(bf16[256,768]{1,0:T(8,128)(2,1)S(1)} %constant_dynamic-update-slice_fusion), channel_id=1, source_target_pairs={{6,0},{0,2},{2,4},{4,6},{7,1},{1,3},{3,5},{5,7},{14,8},{8,10},{10,... | collective-permute-start | bytes 1179656 | tf_op jit(solution)/shard_map/ppermute | solution.py:392
  93.1 8.9 %shard_map.95 = (bf16[3,2048,128]{2,1,0:T(8,128)(2,1)S(1)}, bf16[3,2048,128]{2,1,0:T(8,128)(2,1)S(1)}, bf16[3,2048,128]{2,1,0:T(8,128)(2,1)S(1)}, bf16[160,768]{1,0:T(8,128)(2,1)S(1)}) custom-call(s32[3]{0:T(128)S(1)} %pad_add_fusion.pos, bf16[4,128,768]{2,1,0:T(8,128)(2,1)} %all-to-all-done.1.near, bf16[4,128,768]{2,1,0:T(8,128)(2,1)S(1)} %collective-permute-done.4.other, ...), custom_call_target="tpu_custom_call" | custom-call | tf_op jit(solution)/shard_map/pallas_call | solution.py:42
  102.1 10.1 %shard_map.96 = (bf16[3,256,128]{2,1,0:T(8,128)(2,1)S(1)}, f32[8,512]{1,0:T(8,128)S(1)}) custom-call(bf16[3,2048,128]{2,1,0:T(8,128)(2,1)S(1)} %get-tuple-element.41.q, bf16[3,2048,128]{2,1,0:T(8,128)(2,1)S(1)} %get-tuple-element.42.k, bf16[3,2048,128]{2,1,0:T(8,128)(2,1)S(1)} %get-tuple-element.43.v, bf16[128,768]{1,0:T(8,128)(2,1)S(1)} %copy-done, ...), custom_call_target="tpu_custom_call" | custom-call | tf_op jit(solution)/shard_map/pallas_call | solution.py:42
  112.2 6.5 %all_to_all.25.stats = f32[4,8,512]{2,1,0:T(8,128)S(1)} all-to-all(f32[4,8,512]{2,1,0:T(8,128)S(1)} %broadcast_in_dim.17), channel_id=1, replica_groups=mesh['y'=4,'zm'=2,'zl'=4,'zh'=2,'x'=4,'core'=2] {'x'}, dimensions={0} | all-to-all | bytes 131072 | tf_op jit(solution)/shard_map/all_to_all | solution.py:397
  118.8 10.3 %shard_map.97 = (bf16[160,1152]{1,0:T(8,128)(2,1)S(1)}, bf16[160,1152]{1,0:T(8,128)(2,1)S(1)}) custom-call(s32[3]{0:T(128)S(1)} %pad_add_fusion.pos, bf16[3,2048,128]{2,1,0:T(8,128)(2,1)S(1)} %get-tuple-element.41.q, bf16[3,2048,128]{2,1,0:T(8,128)(2,1)S(1)} %get-tuple-element.42.k, bf16[3,2048,128]{2,1,0:T(8,128)(2,1)S(1)} %get-tuple-element.43.v, ...), custom_call_target="tpu_custom_call" | custom-call | tf_op jit(solution)/shard_map/pallas_call | solution.py:42
  129.1 4.1 %collective-permute-start.8 = (bf16[160,1152]{1,0:T(8,128)(2,1)S(1)}, bf16[160,1152]{1,0:T(8,128)(2,1)S(1)}, u32[]{:S(2)}, u32[]{:S(2)}) collective-permute-start(bf16[160,1152]{1,0:T(8,128)(2,1)S(1)} %get-tuple-element.52), channel_id=1, source_target_pairs={{0,1},{1,0},{2,3},{3,2},{4,5},{5,4},{6,7},{7,6},{8,9},{9,8},{10,11... | collective-permute-start | bytes 1105928 | tf_op jit(solution)/shard_map/ppermute | solution.py:388
  134.5 3.9 %shard_map.98 = (bf16[128,768]{1,0:T(8,128)(2,1)}, f32[2,16,128]{2,1,0:T(8,128)S(1)}) custom-call(s32[3]{0:T(128)S(1)} %pad_add_fusion.pos, bf16[160,1152]{1,0:T(8,128)(2,1)S(1)} %get-tuple-element.51.mine, bf16[160,1152]{1,0:T(8,128)(2,1)S(1)} %collective-permute-done.8.recv, bf16[768,1152]{1,0:T(8,128)(2,1)S(1)} %pad_maximum_fusion.w.w_own, ...), custom_call_target="tpu_custom_call" | custom-call | tf_op jit(solution)/shard_map/pallas_call | solution.py:42
  138.4 12.3 %all_to_all.26 = f32[32,16,128]{2,1,0:T(8,128)S(1)} all-to-all(f32[32,16,128]{2,1,0:T(8,128)S(1)} %bitcast.8), channel_id=1, replica_groups=mesh['y'=4,'zm'=2,'zl'=4,'zh'=2,'x'=4,'core'=2] {'y','x','core'}, dimensions={0} | all-to-all | bytes 524288 | tf_op jit(solution)/shard_map/all_to_all | solution.py:494
  150.7 23.1 %all_to_all.27 = bf16[16,16,128]{2,1,0:T(8,128)(2,1)S(1)} all-to-all(bf16[16,16,128]{2,1,0:T(8,128)(2,1)S(1)} %broadcast_in_dim.20), channel_id=1, replica_groups=mesh['y'=4,'zm'=2,'zl'=4,'zh'=2,'x'=4,'core'=2] {'zm','zl','zh'}, dimensions={0} | all-to-all | bytes 131072 | tf_op jit(solution)/shard_map/all_to_all | solution.py:397
  173.8 3.3 %all-gather = f32[32,128]{1,0:T(8,128)S(1)} all-gather(f32[16,128]{1,0:T(8,128)S(1)} %convert_reduce_fusion), channel_id=2, replica_groups=mesh['y'=4,'zm'=2,'zl'=4,'zh'=2,'x'=4,'core'=2] {'core'}, dimensions={0}, use_global_device_ids=true | all-gather | bytes 24576 | tf_op jit(solution)/shard_map/all_gather | solution.py:497
  177.1 1.9 %multiply_reduce_fusion = (f32[768]{0:T(1024)}, f32[5,768]{1,0:T(8,128)}) fusion(f32[5,768]{1,0:T(8,128)S(1)} %constant_dynamic-update-slice_fusion.2, f32[5,768]{1,0:T(8,128)} %param.9, f32[768]{0:T(1024)S(1)} %copy-done.16), kind=kLoop, calls=%fused_computation.15 | loop fusion | flops 10752 | bytes 52224 | tf_op jit(solution)/shard_map/reduce_sum | solution.py:500
  (68 shorter events, 21.8 us)
Async XLA Ops:
  0.6 26.5 %copy-start.13 = (bf16[768,768]{1,0:T(8,128)(2,1)S(1)}, bf16[768,768]{1,0:T(8,128)(2,1)}, u32[]{:S(2)}) copy-start(bf16[768,768]{1,0:T(8,128)(2,1)} %param.10) | copy-start | bytes 3538948
  0.6 31.3 %collective-permute-start = (bf16[128,768]{1,0:T(8,128)(2,1)}, bf16[128,768]{1,0:T(8,128)(2,1)}, u32[]{:S(2)}, u32[]{:S(2)}) collective-permute-start(bf16[128,768]{1,0:T(8,128)(2,1)} %bitcast.11), channel_id=1, source_target_pairs={{0,8},{8,0},{1,9},{9,1},{2,10},{10,2},{3,11},{11,3},{4,12},{12,4},... | collective-permute-start | bytes 589832 | tf_op jit(solution)/shard_map/ppermute | solution.py:388
  17.8 12.4 %collective-permute-start.1 = (bf16[128,384]{1,0:T(8,128)(2,1)}, bf16[128,384]{1,0:T(8,128)(2,1)}, u32[]{:S(2)}, u32[]{:S(2)}) collective-permute-start(bf16[128,384]{1,0:T(8,128)(2,1)} %broadcast_select_fusion.8), channel_id=1, source_target_pairs={{0,1},{1,0},{2,3},{3,2},{4,5},{5,4},{6,7},{7,6},{8,9},{9,8},{10,11... | collective-permute-start | bytes 294920 | tf_op jit(solution)/shard_map/ppermute | solution.py:388
  22.6 4.6 %copy-start.11 = (bf16[768,768]{1,0:T(8,128)(2,1)S(1)}, bf16[768,768]{1,0:T(8,128)(2,1)}, u32[]{:S(2)}) copy-start(bf16[768,768]{1,0:T(8,128)(2,1)} %param.12) | copy-start | bytes 3538948
  22.6 15.1 %all-to-all-start = ((bf16[4,128,768]{2,1,0:T(8,128)(2,1)}), bf16[4,128,768]{2,1,0:T(8,128)(2,1)}, u32[]{:S(2)}, u32[]{:S(2)}) async-start(bf16[4,128,768]{2,1,0:T(8,128)(2,1)} %broadcast_in_dim.15), calls=%async_computation | async-start | bytes 1572864 | tf_op jit(solution)/shard_map/all_to_all | solution.py:397
  27.1 1.3 copy-start.12
  28.8 1.4 copy-start.14
  37.7 14.7 %collective-permute-start.2 = (bf16[4,128,768]{2,1,0:T(8,128)(2,1)}, bf16[4,128,768]{2,1,0:T(8,128)(2,1)}, u32[]{:S(2)}, u32[]{:S(2)}) collective-permute-start(bf16[4,128,768]{2,1,0:T(8,128)(2,1)} %all-to-all-done.near), channel_id=1, source_target_pairs={{0,1},{1,0},{2,3},{3,2},{4,5},{5,4},{6,7},{7,6},{8,9},{9,8},{10,11... | collective-permute-start | bytes 2359304 | tf_op jit(solution)/shard_map/ppermute | solution.py:388
  42.4 25.8 %all-to-all-start.1 = ((bf16[4,128,768]{2,1,0:T(8,128)(2,1)}), bf16[4,128,768]{2,1,0:T(8,128)(2,1)}, u32[]{:S(2)}, u32[]{:S(2)}) async-start(bf16[4,128,768]{2,1,0:T(8,128)(2,1)} %broadcast_in_dim.16), calls=%async_computation.1 | async-start | bytes 1572864 | tf_op jit(solution)/shard_map/all_to_all | solution.py:397
  48.4 19.8 %collective-permute-start.3 = (bf16[128,768]{1,0:T(8,128)(2,1)}, bf16[128,768]{1,0:T(8,128)(2,1)}, u32[]{:S(2)}, u32[]{:S(2)}) collective-permute-start(bf16[128,768]{1,0:T(8,128)(2,1)} %pad_maximum_fusion.2.d0), channel_id=1, source_target_pairs={{0,8},{8,0},{1,9},{9,1},{2,10},{10,2},{3,11},{11,3},{4,12},{12,4},... | collective-permute-start | bytes 589832 | tf_op jit(solution)/shard_map/ppermute | solution.py:388
  61.2 1.2 copy-start.1
  62.4 0.9 copy-start.3
  63.2 0.9 copy-start.5
  64.1 0.9 copy-start.7
  68.2 19.4 %collective-permute-start.4 = (bf16[4,128,768]{2,1,0:T(8,128)(2,1)}, bf16[4,128,768]{2,1,0:T(8,128)(2,1)S(1)}, u32[]{:S(2)}, u32[]{:S(2)}) collective-permute-start(bf16[4,128,768]{2,1,0:T(8,128)(2,1)} %all-to-all-done.1.near), channel_id=1, source_target_pairs={{0,1},{1,0},{2,3},{3,2},{4,5},{5,4},{6,7},{7,6},{8,9},{9,8},{10,11... | collective-permute-start | bytes 2359304 | tf_op jit(solution)/shard_map/ppermute | solution.py:388
  78.6 33.6 %collective-permute-start.5 = (bf16[256,768]{1,0:T(8,128)(2,1)S(1)}, bf16[256,768]{1,0:T(8,128)(2,1)S(1)}, u32[]{:S(2)}, u32[]{:S(2)}) collective-permute-start(bf16[256,768]{1,0:T(8,128)(2,1)S(1)} %constant_dynamic-update-slice_fusion), channel_id=1, source_target_pairs={{2,0},{4,2},{6,4},{0,6},{3,1},{5,3},{7,5},{1,7},{10,8},{12,10},{14... | collective-permute-start | bytes 1179656 | tf_op jit(solution)/shard_map/ppermute | solution.py:392
  81.1 31.1 %collective-permute-start.6 = (bf16[256,768]{1,0:T(8,128)(2,1)S(1)}, bf16[256,768]{1,0:T(8,128)(2,1)S(1)}, u32[]{:S(2)}, u32[]{:S(2)}) collective-permute-start(bf16[256,768]{1,0:T(8,128)(2,1)S(1)} %constant_dynamic-update-slice_fusion), channel_id=1, source_target_pairs={{4,0},{6,2},{0,4},{2,6},{5,1},{7,3},{1,5},{3,7},{12,8},{14,10},{8,... | collective-permute-start | bytes 1179656 | tf_op jit(solution)/shard_map/ppermute | solution.py:392
  83.6 28.5 %collective-permute-start.7 = (bf16[256,768]{1,0:T(8,128)(2,1)S(1)}, bf16[256,768]{1,0:T(8,128)(2,1)S(1)}, u32[]{:S(2)}, u32[]{:S(2)}) collective-permute-start(bf16[256,768]{1,0:T(8,128)(2,1)S(1)} %constant_dynamic-update-slice_fusion), channel_id=1, source_target_pairs={{6,0},{0,2},{2,4},{4,6},{7,1},{1,3},{3,5},{5,7},{14,8},{8,10},{10,... | collective-permute-start | bytes 1179656 | tf_op jit(solution)/shard_map/ppermute | solution.py:392
  87.6 1.4 copy-start.2
  89.0 1.1 copy-start.4
  90.1 1.1 copy-start.6
  91.3 1.1 copy-start.8
  93.1 8.9 %copy-start = (bf16[128,768]{1,0:T(8,128)(2,1)S(1)}, bf16[128,768]{1,0:T(8,128)(2,1)}, u32[]{:S(2)}) copy-start(bf16[128,768]{1,0:T(8,128)(2,1)} %pad_maximum_fusion.2.d0) | copy-start | bytes 589828
  129.1 5.4 %collective-permute-start.8 = (bf16[160,1152]{1,0:T(8,128)(2,1)S(1)}, bf16[160,1152]{1,0:T(8,128)(2,1)S(1)}, u32[]{:S(2)}, u32[]{:S(2)}) collective-permute-start(bf16[160,1152]{1,0:T(8,128)(2,1)S(1)} %get-tuple-element.52), channel_id=1, source_target_pairs={{0,1},{1,0},{2,3},{3,2},{4,5},{5,4},{6,7},{7,6},{8,9},{9,8},{10,11... | collective-permute-start | bytes 1105928 | tf_op jit(solution)/shard_map/ppermute | solution.py:388
  (4 other events, 2.9 us)

commit v7 on v5

--- a/solution.py
+++ b/solution.py
@@ -74,16 +74,16 @@
 
 
 def hidden_body(
-    pos, near, other, w, taps, q, k, v, ext, xs, ns, hs
+    pos, near, far, e0, e1, w, taps, q, k, v, ext, xs, ns, hs
 ):
     core = pos[2]
     here = pl.multiple_of(core * BLOCK, BLOCK)
     there = pl.multiple_of((1 - core) * BLOCK, BLOCK)
     for c in range(CHUNKS):
         xa = lax.rem(pos[1] + c % 4, 4)
-        sl = slice((c // 4) * BLOCK, (c // 4 + 1) * BLOCK)
-        xs[c, pl.ds(here, BLOCK), :] = near[xa, sl, :]
-        xs[c, pl.ds(there, BLOCK), :] = other[xa, sl, :]
+        own, other = ((near, e0), (far, e1))[c // 4]
+        xs[c, pl.ds(here, BLOCK), :] = own[xa, 0:BLOCK, :]
+        xs[c, pl.ds(there, BLOCK), :] = other[xa, :, 0:C]
     prev, nxt, prev_ok, nxt_ok = neighbours(pos, jnp.int32(0), jnp.int32(0))
     first = core == 0
     ext[16:144, :] = near[pos[1], 0:BLOCK, :]
@@ -131,13 +131,19 @@
 KB = 512
 
 
-def forward_body(q, k, v, d0, d4, dq, stats, ds, ss, sm):
-    for g, d in enumerate((d0, d4)):
+def cotangents(core, own, other, at, h, dst, row):
+    here = pl.multiple_of(row + core * BLOCK, BLOCK)
+    there = pl.multiple_of(row + (1 - core) * BLOCK, BLOCK)
+    low = own[at, BLOCK:CHUNK, h * 128 : (h + 1) * 128]
+    high = own[at, BLOCK:CHUNK, HALF + h * 128 : HALF + (h + 1) * 128]
+    dst[h, pl.ds(here, BLOCK), :] = jnp.where(core == 0, low, high)
+    dst[h, pl.ds(there, BLOCK), :] = other[at, :, C + h * 128 : C + (h + 1) * 128]
+
+
+def forward_body(pos, q, k, v, near, far, e0, e1, dq, stats, ds, ss, sm):
+    for g, (own, other) in enumerate(((near, e0), (far, e1))):
         for h in range(OWN_HEADS):
-            ds[h, g * CHUNK : g * CHUNK + BLOCK, :] = d[0:BLOCK, h * 128 : (h + 1) * 128]
-            ds[h, g * CHUNK + BLOCK : (g + 1) * CHUNK, :] = d[
-                0:BLOCK, HALF + h * 128 : HALF + (h + 1) * 128
-            ]
+            cotangents(pos[2], own, other, pos[1], h, ds, g * CHUNK)
     sm[...] = jnp.zeros_like(sm)
     lane = lax.broadcasted_iota(jnp.int32, (CHUNK, 128), 1)
 
@@ -186,20 +192,17 @@
 
 
 def backward_body(
-    pos, q, k, v, dq, d0, d4, b1, b2, b3, stats, mine, give, ds, gs, kx, vx, qx, dx_, st
+    pos, q, k, v, dq, near, far, e0, e1, stats, mine, give, ds, gs, kx, vx, qx, dx_, st
 ):
     core = pos[2]
 
     def place(c):
         return lax.rem(pos[1] + c, 4)
 
-    blocks = ((d0, 0), (b1, 0), (b2, 0), (b3, 0), (d4, 0), (b1, BLOCK), (b2, BLOCK), (b3, BLOCK))
-    for c, (d, low) in enumerate(blocks):
+    for c in range(CHUNKS):
+        own, other = ((near, e0), (far, e1))[c // 4]
         for h in range(OWN_HEADS):
-            lo = c * CHUNK
-            rows = slice(low, low + BLOCK)
-            ds[h, lo : lo + BLOCK, :] = d[rows, h * 128 : (h + 1) * 128]
-            ds[h, lo + BLOCK : lo + CHUNK, :] = d[rows, HALF + h * 128 : HALF + (h + 1) * 128]
+            cotangents(core, own, other, place(jnp.int32(c)), h, ds, c * CHUNK)
     prev, nxt, _, _ = neighbours(pos, jnp.int32(0), jnp.int32(0))
     low = pl.multiple_of(prev * CHUNK + CHUNK - EDGE, EDGE)
     high = pl.multiple_of(nxt * CHUNK, EDGE)
@@ -338,51 +341,50 @@
         low, high = a[:, :HALF], a[:, HALF:]
         return jnp.where(first, low, high), jnp.where(first, high, low)
 
-    keep, give = halves(cot)
-    got = swap(give, "core")
-    cot_own = jnp.concatenate(
-        [jnp.where(first, keep, got), jnp.where(first, got, keep)], axis=1
-    )
-    sig_z = swap(sig, "zh")
+    both = jnp.concatenate([sig, cot], axis=0)
+    both_z = swap(both, "zh")
+    near = share(both, "x", 4)
+
+    def exchange(a):
+        rows, cots = a[:, :BLOCK], a[:, BLOCK:]
+        give = jnp.where(first, cots[:, :, HALF:], cots[:, :, :HALF])
+        return swap(jnp.concatenate([rows, give], axis=-1), "core")
+
     parts = [halves(w) for w in (w_query, w_key, w_value)]
     w_own = jnp.concatenate([p[0] for p in parts], axis=1)
     w_oth = jnp.concatenate([p[1] for p in parts], axis=1)
     coef = jnp.concatenate([conv_taps, gain, jnp.zeros((2, C), F32)], axis=0)
-    sig_z, cot_own, w_own, w_oth, coef = lax.optimization_barrier(
-        (sig_z, cot_own, w_own, w_oth, coef)
+    both_z, near, w_own, w_oth, coef = lax.optimization_barrier(
+        (both_z, near, w_own, w_oth, coef)
     )
-    cot_z = swap(cot_own, "zh")
-    near = share(jnp.concatenate([sig, sig_z], axis=0), "x", 4)
-    near, cot_z = lax.optimization_barrier((near, cot_z))
-    other = swap(near, "core")
-    both = jnp.concatenate([cot_own, cot_z], axis=0)
-    cots = [from_x(both, d) for d in (1, 2, 3)]
+    e0 = exchange(near)
+    far = share(both_z, "x", 4)
+    e1 = exchange(far)
 
     head_shape = jax.ShapeDtypeStruct((OWN_HEADS, BINS, HEAD_DIM), BF16)
     q, k, v, ext = call(
         hidden_body,
         (head_shape, head_shape, head_shape, jax.ShapeDtypeStruct((160, C), BF16)),
-        (pos, near, other, w_own, coef),
+        (pos, near, far, e0, e1, w_own, coef),
         (VM((CHUNKS, CHUNK, C), BF16), VM((288, C), F32), VM((CHUNK, C), BF16)),
     )
     part = jax.ShapeDtypeStruct((OWN_HEADS, CHUNK, HEAD_DIM), BF16)
     dq, stats = call(
         forward_body,
         (part, jax.ShapeDtypeStruct((8, 2 * CHUNK), F32)),
-        (q, k, v, cot_own, cot_z),
+        (pos, q, k, v, near, far, e0, e1),
         (
             VM((OWN_HEADS, 2 * CHUNK, HEAD_DIM), BF16),
             VM((CHUNK, BINS), F32),
             VM((2 * CHUNK, 128), F32),
         ),
     )
-    stats, cots = lax.optimization_barrier((stats, cots))
     stats_all = share(stats, "x", 4)
     grads = jax.ShapeDtypeStruct((WINDOW, 3 * HALF), BF16)
     mine, give = call(
         backward_body,
         (grads, grads),
-        (pos, q, k, v, dq, cot_own, cot_z, *cots, stats_all),
+        (pos, q, k, v, dq, near, far, e0, e1, stats_all),
         (
             VM((OWN_HEADS, BINS, HEAD_DIM), BF16),
             VM((WIDE, 3 * HALF), BF16),

time: 178 us -> 183 us (1.028)
  waiting for transfers between devices: 10.5 us -> 27.6 us
  starting transfers between devices: 49.3 us -> 37.9 us
  blocking collectives: 60.9 us -> 57.5 us
  other arithmetic: 7.41 us -> 9.39 us
    all_to_all x1 -> x2, waiting for transfers between devices: 2.07 us -> 21.2 us  [share(): return lax.all_to_all(wide, axes, 0, 0)]
    ppermute x3 -> x0, starting transfers between devices: 9.58 us -> none  [from_x(): return lax.ppermute(a, 'x', [((i + step) % 4, i) for i in range(4)])]
    ppermute x5 -> x4, starting transfers between devices: 35.2 us -> 28.4 us  [swap(): return lax.ppermute(a, axis, [(0, 1), (1, 0)])]
    all_to_all x1 -> x2, starting transfers between devices: 4.51 us -> 9.53 us  [share(): return lax.all_to_all(wide, axes, 0, 0)]
    all_to_all x2, blocking collectives: 43.1 us -> 39.6 us  [share(): return lax.all_to_all(wide, axes, 0, 0)]
    broadcast_in_dim x3 -> x4, local copies, waits for them, and re-layouts: 1.26 us -> 3.56 us  [share(): wide = jnp.broadcast_to(a[None], (size,) + a.shape)]
    ppermute x5 -> x4, waiting for transfers between devices: 8.45 us -> 6.43 us  [swap(): return lax.ppermute(a, axis, [(0, 1), (1, 0)])]
  transfers between devices with their start and end apart: 9 -> 6, of which waited for: 3 -> 5; matrix products, arithmetic and copies ran while one was open for 4% -> 5% of each run, Pallas kernels for 14% -> 0%
where the time goes in v7:
time: 183 us; the launch traced here: 180 us
  blocking collectives  57.5 us (31%)
  Pallas kernels  41 us (22%)
  starting transfers between devices  37.9 us (21%)
  waiting for transfers between devices  27.6 us (15%)
  other arithmetic  9.39 us (5%)
  local copies, waits for them, and re-layouts  5.65 us (3%)
    pallas_call x4, Pallas kernels, call(): pl.pallas_call(body, out_shape=out_shape, in_specs=specs, out_specs=outs,...  41 us
    all_to_all x2, blocking collectives, share(): return lax.all_to_all(wide, axes, 0, 0)  39.6 us
    ppermute x4, starting transfers between devices, swap(): return lax.ppermute(a, axis, [(0, 1), (1, 0)])  28.4 us
    all_to_all x2, waiting for transfers between devices, share(): return lax.all_to_all(wide, axes, 0, 0)  21.2 us
    all_to_all x1, blocking collectives, shards(): part = jnp.sum(lax.all_to_all(wide, ('y', 'x', 'core'), 0, 0), axis=0)  14.6 us
    all_to_all x2, starting transfers between devices, share(): return lax.all_to_all(wide, axes, 0, 0)  9.53 us
    ppermute x4, waiting for transfers between devices, swap(): return lax.ppermute(a, axis, [(0, 1), (1, 0)])  6.43 us
  transfers between devices with their start and end apart: 6, of which 5 were waited for; matrix products, arithmetic and copies ran while one was open for 5% of the time, Pallas kernels for 0%

profile of v7, /device:TPU:7, one launch (start us, length us, event | category | flops | bytes accessed | tf_op | source)
XLA Modules:
  0.0 179.9 jit_solution(8300756819967704252)
XLA Ops:
  1.7 15.4 %collective-permute-start = (bf16[256,768]{1,0:T(8,128)(2,1)S(1)}, bf16[256,768]{1,0:T(8,128)(2,1)}, u32[]{:S(2)}, u32[]{:S(2)}) collective-permute-start(bf16[256,768]{1,0:T(8,128)(2,1)S(1)} %pad_maximum_fusion.4), channel_id=1, source_target_pairs={{0,8},{8,0},{1,9},{9,1},{2,10},{10,2},{3,11},{11,3},{4,12},{12,4},... | collective-permute-start | bytes 1179656 | tf_op jit(solution)/shard_map/ppermute | solution.py:318
  17.1 1.3 broadcast_in_dim.14
  18.4 4.2 %all-to-all-start = ((bf16[4,256,768]{2,1,0:T(8,128)(2,1)}), bf16[4,256,768]{2,1,0:T(8,128)(2,1)S(1)}, u32[]{:S(2)}, u32[]{:S(2)}) async-start(bf16[4,256,768]{2,1,0:T(8,128)(2,1)} %broadcast_in_dim.14), calls=%async_computation | async-start | bytes 3145728 | tf_op jit(solution)/shard_map/all_to_all | solution.py:327
  22.6 1.5 broadcast_select_fusion.2
  24.9 1.4 pad_maximum_fusion.1.w_oth
  26.3 1.4 pad_maximum_fusion.w.w_own
  27.7 2.6 %collective-permute-done = bf16[256,768]{1,0:T(8,128)(2,1)} collective-permute-done((bf16[256,768]{1,0:T(8,128)(2,1)S(1)}, bf16[256,768]{1,0:T(8,128)(2,1)}, u32[]{:S(2)}, u32[]{:S(2)}) %collective-permute-start) | collective-permute-done | bytes 393248 | tf_op jit(solution)/shard_map/ppermute | solution.py:318
  30.3 10.0 %all-to-all-done.near = bf16[4,256,768]{2,1,0:T(8,128)(2,1)S(1)} async-done(((bf16[4,256,768]{2,1,0:T(8,128)(2,1)}), bf16[4,256,768]{2,1,0:T(8,128)(2,1)S(1)}, u32[]{:S(2)}, u32[]{:S(2)}) %all-to-all-start) | async-done | bytes 1572896 | tf_op jit(solution)/shard_map/all_to_all | solution.py:327
  40.3 2.3 %broadcast_in_dim.16 = bf16[4,256,768]{2,1,0:T(8,128)(2,1)} broadcast(bf16[256,768]{1,0:T(8,128)(2,1)} %collective-permute-done), dimensions={1,2} | broadcast | bytes 1966080 | tf_op jit(solution)/shard_map/broadcast_in_dim | solution.py:326
  42.6 5.3 %all-to-all-start.1 = ((bf16[4,256,768]{2,1,0:T(8,128)(2,1)}), bf16[4,256,768]{2,1,0:T(8,128)(2,1)S(1)}, u32[]{:S(2)}, u32[]{:S(2)}) async-start(bf16[4,256,768]{2,1,0:T(8,128)(2,1)} %broadcast_in_dim.16), calls=%async_computation.1 | async-start | bytes 3145728 | tf_op jit(solution)/shard_map/all_to_all | solution.py:327
  49.2 4.3 %collective-permute-start.1 = (bf16[4,128,1152]{2,1,0:T(8,128)(2,1)}, bf16[4,128,1152]{2,1,0:T(8,128)(2,1)}, u32[]{:S(2)}, u32[]{:S(2)}) collective-permute-start(bf16[4,128,1152]{2,1,0:T(8,128)(2,1)} %pad_maximum_fusion.2), channel_id=1, source_target_pairs={{0,1},{1,0},{2,3},{3,2},{4,5},{5,4},{6,7},{7,6},{8,9},{9,8},{10,11... | collective-permute-start | bytes 3538952 | tf_op jit(solution)/shard_map/ppermute | solution.py:318
  53.5 11.2 %all-to-all-done.1.far = bf16[4,256,768]{2,1,0:T(8,128)(2,1)S(1)} async-done(((bf16[4,256,768]{2,1,0:T(8,128)(2,1)}), bf16[4,256,768]{2,1,0:T(8,128)(2,1)S(1)}, u32[]{:S(2)}, u32[]{:S(2)}) %all-to-all-start.1) | async-done | bytes 1572896 | tf_op jit(solution)/shard_map/all_to_all | solution.py:327
  66.0 5.0 %collective-permute-start.2 = (bf16[4,128,1152]{2,1,0:T(8,128)(2,1)}, bf16[4,128,1152]{2,1,0:T(8,128)(2,1)}, u32[]{:S(2)}, u32[]{:S(2)}) collective-permute-start(bf16[4,128,1152]{2,1,0:T(8,128)(2,1)} %pad_maximum_fusion.3), channel_id=1, source_target_pairs={{0,1},{1,0},{2,3},{3,2},{4,5},{5,4},{6,7},{7,6},{8,9},{9,8},{10,11... | collective-permute-start | bytes 3538952 | tf_op jit(solution)/shard_map/ppermute | solution.py:318
  71.1 2.7 %collective-permute-done.2.e1 = bf16[4,128,1152]{2,1,0:T(8,128)(2,1)} collective-permute-done((bf16[4,128,1152]{2,1,0:T(8,128)(2,1)}, bf16[4,128,1152]{2,1,0:T(8,128)(2,1)}, u32[]{:S(2)}, u32[]{:S(2)}) %collective-permute-start.2) | collective-permute-done | bytes 1179680 | tf_op jit(solution)/shard_map/ppermute | solution.py:318
  73.8 1.5 copy-done
  75.3 15.0 %shard_map.94 = (bf16[3,2048,128]{2,1,0:T(8,128)(2,1)S(1)}, bf16[3,2048,128]{2,1,0:T(8,128)(2,1)S(1)}, bf16[3,2048,128]{2,1,0:T(8,128)(2,1)S(1)}, bf16[160,768]{1,0:T(8,128)(2,1)S(1)}) custom-call(s32[3]{0:T(128)S(1)} %pad_add_fusion.pos, bf16[4,256,768]{2,1,0:T(8,128)(2,1)S(1)} %all-to-all-done.near, bf16[4,256,768]{2,1,0:T(8,128)(2,1)S(1)} %all-to-all-done.1.far, ...), custom_call_target="tpu_custom_call" | custom-call | tf_op jit(solution)/shard_map/pallas_call | solution.py:40
  90.3 10.8 %shard_map.95 = (bf16[3,256,128]{2,1,0:T(8,128)(2,1)S(1)}, f32[8,512]{1,0:T(8,128)S(1)}) custom-call(s32[3]{0:T(128)S(1)} %pad_add_fusion.pos, bf16[3,2048,128]{2,1,0:T(8,128)(2,1)S(1)} %get-tuple-element.22.q, bf16[3,2048,128]{2,1,0:T(8,128)(2,1)S(1)} %get-tuple-element.23.k, bf16[3,2048,128]{2,1,0:T(8,128)(2,1)S(1)} %get-tuple-element.24.v, ...), custom_call_target="tpu_custom_call" | custom-call | tf_op jit(solution)/shard_map/pallas_call | solution.py:40
  101.1 6.8 %all_to_all.25.stats = f32[4,8,512]{2,1,0:T(8,128)S(1)} all-to-all(f32[4,8,512]{2,1,0:T(8,128)S(1)} %broadcast_in_dim.17), channel_id=1, replica_groups=mesh['y'=4,'zm'=2,'zl'=4,'zh'=2,'x'=4,'core'=2] {'x'}, dimensions={0} | all-to-all | bytes 131072 | tf_op jit(solution)/shard_map/all_to_all | solution.py:327
  108.0 11.3 %shard_map.96 = (bf16[160,1152]{1,0:T(8,128)(2,1)S(1)}, bf16[160,1152]{1,0:T(8,128)(2,1)S(1)}) custom-call(s32[3]{0:T(128)S(1)} %pad_add_fusion.pos, bf16[3,2048,128]{2,1,0:T(8,128)(2,1)S(1)} %get-tuple-element.22.q, bf16[3,2048,128]{2,1,0:T(8,128)(2,1)S(1)} %get-tuple-element.23.k, bf16[3,2048,128]{2,1,0:T(8,128)(2,1)S(1)} %get-tuple-element.24.v, ...), custom_call_target="tpu_custom_call" | custom-call | tf_op jit(solution)/shard_map/pallas_call | solution.py:40
  119.3 3.6 %collective-permute-start.3 = (bf16[160,1152]{1,0:T(8,128)(2,1)S(1)}, bf16[160,1152]{1,0:T(8,128)(2,1)S(1)}, u32[]{:S(2)}, u32[]{:S(2)}) collective-permute-start(bf16[160,1152]{1,0:T(8,128)(2,1)S(1)} %get-tuple-element.28), channel_id=1, source_target_pairs={{0,1},{1,0},{2,3},{3,2},{4,5},{5,4},{6,7},{7,6},{8,9},{9,8},{10,11... | collective-permute-start | bytes 1105928 | tf_op jit(solution)/shard_map/ppermute | solution.py:318
  124.0 3.9 %shard_map.97 = (bf16[128,768]{1,0:T(8,128)(2,1)}, f32[2,16,128]{2,1,0:T(8,128)S(1)}) custom-call(s32[3]{0:T(128)S(1)} %pad_add_fusion.pos, bf16[160,1152]{1,0:T(8,128)(2,1)S(1)} %get-tuple-element.27.mine, bf16[160,1152]{1,0:T(8,128)(2,1)S(1)} %collective-permute-done.3.recv, bf16[768,1152]{1,0:T(8,128)(2,1)S(1)} %copy-done.1, ...), custom_call_target="tpu_custom_call" | custom-call | tf_op jit(solution)/shard_map/pallas_call | solution.py:40
  127.9 14.6 %all_to_all.26 = f32[32,16,128]{2,1,0:T(8,128)S(1)} all-to-all(f32[32,16,128]{2,1,0:T(8,128)S(1)} %bitcast.8), channel_id=1, replica_groups=mesh['y'=4,'zm'=2,'zl'=4,'zh'=2,'x'=4,'core'=2] {'y','x','core'}, dimensions={0} | all-to-all | bytes 524288 | tf_op jit(solution)/shard_map/all_to_all | solution.py:406
  142.6 32.8 %all_to_all.27 = bf16[16,16,128]{2,1,0:T(8,128)(2,1)S(1)} all-to-all(bf16[16,16,128]{2,1,0:T(8,128)(2,1)S(1)} %broadcast_in_dim.20), channel_id=1, replica_groups=mesh['y'=4,'zm'=2,'zl'=4,'zh'=2,'x'=4,'core'=2] {'zm','zl','zh'}, dimensions={0} | all-to-all | bytes 131072 | tf_op jit(solution)/shard_map/all_to_all | solution.py:327
  175.4 3.3 %all-gather = f32[32,128]{1,0:T(8,128)S(1)} all-gather(f32[16,128]{1,0:T(8,128)S(1)} %convert_reduce_fusion), channel_id=2, replica_groups=mesh['y'=4,'zm'=2,'zl'=4,'zh'=2,'x'=4,'core'=2] {'core'}, dimensions={0}, use_global_device_ids=true | all-gather | bytes 24576 | tf_op jit(solution)/shard_map/all_gather | solution.py:409
  (39 shorter events, 6.9 us)
Async XLA Ops:
  1.7 28.6 %collective-permute-start = (bf16[256,768]{1,0:T(8,128)(2,1)S(1)}, bf16[256,768]{1,0:T(8,128)(2,1)}, u32[]{:S(2)}, u32[]{:S(2)}) collective-permute-start(bf16[256,768]{1,0:T(8,128)(2,1)S(1)} %pad_maximum_fusion.4), channel_id=1, source_target_pairs={{0,8},{8,0},{1,9},{9,1},{2,10},{10,2},{3,11},{11,3},{4,12},{12,4},... | collective-permute-start | bytes 1179656 | tf_op jit(solution)/shard_map/ppermute | solution.py:318
  18.4 21.9 %all-to-all-start = ((bf16[4,256,768]{2,1,0:T(8,128)(2,1)}), bf16[4,256,768]{2,1,0:T(8,128)(2,1)S(1)}, u32[]{:S(2)}, u32[]{:S(2)}) async-start(bf16[4,256,768]{2,1,0:T(8,128)(2,1)} %broadcast_in_dim.14), calls=%async_computation | async-start | bytes 3145728 | tf_op jit(solution)/shard_map/all_to_all | solution.py:327
  22.6 1.5 copy-start.6
  22.6 1.6 copy-start.3
  22.6 2.0 %copy-start.4 = (bf16[768,768]{1,0:T(8,128)(2,1)S(1)}, bf16[768,768]{1,0:T(8,128)(2,1)}, u32[]{:S(2)}) copy-start(bf16[768,768]{1,0:T(8,128)(2,1)} %param.11) | copy-start | bytes 3538948
  24.9 1.4 copy-start.5
  42.6 22.1 %all-to-all-start.1 = ((bf16[4,256,768]{2,1,0:T(8,128)(2,1)}), bf16[4,256,768]{2,1,0:T(8,128)(2,1)S(1)}, u32[]{:S(2)}, u32[]{:S(2)}) async-start(bf16[4,256,768]{2,1,0:T(8,128)(2,1)} %broadcast_in_dim.16), calls=%async_computation.1 | async-start | bytes 3145728 | tf_op jit(solution)/shard_map/all_to_all | solution.py:327
  49.2 21.9 %collective-permute-start.1 = (bf16[4,128,1152]{2,1,0:T(8,128)(2,1)}, bf16[4,128,1152]{2,1,0:T(8,128)(2,1)}, u32[]{:S(2)}, u32[]{:S(2)}) collective-permute-start(bf16[4,128,1152]{2,1,0:T(8,128)(2,1)} %pad_maximum_fusion.2), channel_id=1, source_target_pairs={{0,1},{1,0},{2,3},{3,2},{4,5},{5,4},{6,7},{7,6},{8,9},{9,8},{10,11... | collective-permute-start | bytes 3538952 | tf_op jit(solution)/shard_map/ppermute | solution.py:318
  66.0 7.8 %collective-permute-start.2 = (bf16[4,128,1152]{2,1,0:T(8,128)(2,1)}, bf16[4,128,1152]{2,1,0:T(8,128)(2,1)}, u32[]{:S(2)}, u32[]{:S(2)}) collective-permute-start(bf16[4,128,1152]{2,1,0:T(8,128)(2,1)} %pad_maximum_fusion.3), channel_id=1, source_target_pairs={{0,1},{1,0},{2,3},{3,2},{4,5},{5,4},{6,7},{7,6},{8,9},{9,8},{10,11... | collective-permute-start | bytes 3538952 | tf_op jit(solution)/shard_map/ppermute | solution.py:318
  73.8 1.5 copy-start
  108.0 16.0 %copy-start.1 = (bf16[768,1152]{1,0:T(8,128)(2,1)S(1)}, bf16[768,1152]{1,0:T(8,128)(2,1)}, u32[]{:S(2)}) copy-start(bf16[768,1152]{1,0:T(8,128)(2,1)} %pad_maximum_fusion.w.w_own) | copy-start | bytes 5308420
  108.0 16.0 %copy-start.2 = (bf16[768,1152]{1,0:T(8,128)(2,1)S(1)}, bf16[768,1152]{1,0:T(8,128)(2,1)}, u32[]{:S(2)}) copy-start(bf16[768,1152]{1,0:T(8,128)(2,1)} %pad_maximum_fusion.1.w_oth) | copy-start | bytes 5308420
  119.3 4.7 %collective-permute-start.3 = (bf16[160,1152]{1,0:T(8,128)(2,1)S(1)}, bf16[160,1152]{1,0:T(8,128)(2,1)S(1)}, u32[]{:S(2)}, u32[]{:S(2)}) collective-permute-start(bf16[160,1152]{1,0:T(8,128)(2,1)S(1)} %get-tuple-element.28), channel_id=1, source_target_pairs={{0,1},{1,0},{2,3},{3,2},{4,5},{5,4},{6,7},{7,6},{8,9},{9,8},{10,11... | collective-permute-start | bytes 1105928 | tf_op jit(solution)/shard_map/ppermute | solution.py:318

commit v8 on v5

--- a/solution.py
+++ b/solution.py
@@ -15,6 +15,7 @@
 EPSILON = 1e-06
 GELU_ROOT = math.sqrt(2.0 / math.pi)
 SCALE = 1.0 / math.sqrt(HEAD_DIM)
+LOG2E = math.log2(math.e)
 BLOCK = 128
 CHUNK = 256
 CHUNKS = 8
@@ -74,7 +75,7 @@
 
 
 def hidden_body(
-    pos, near, other, w, taps, q, k, v, ext, xs, ns, hs
+    pos, near, other, w, taps, q, k, v, ext, xs, ns, hs, ns2, hs2
 ):
     core = pos[2]
     here = pl.multiple_of(core * BLOCK, BLOCK)
@@ -98,7 +99,7 @@
         ext[0:16, :] = xs[0, 112:128, :]
         ext[144:160, :] = (xs[nxt, 0:16, :].astype(F32) * nxt_ok).astype(BF16)
 
-    def chunk(c, _):
+    def prepare(c, ns, hs):
         dz = lax.div(c, 4)
         dx = lax.rem(c, 4)
         prev, nxt, prev_ok, nxt_ok = neighbours(pos, dz, dx)
@@ -113,19 +114,42 @@
                 u = tap[0] * ns[14 + r : 78 + r, j : j + 128]
                 for t in range(1, 5):
                     u = u + tap[t] * ns[14 + r + t : 78 + r + t, j : j + 128]
-                inner = GELU_ROOT * (u + 0.044715 * u * u * u)
-                act = 0.5 * u * (1.0 + jnp.tanh(inner))
+                inner = u * (GELU_ROOT + (GELU_ROOT * 0.044715) * (u * u))
+                half = 0.5 * u
                 x = xs[c, r : r + 64, j : j + 128].astype(F32)
-                hs[r : r + 64, j : j + 128] = (x + act).astype(BF16)
+                hs[r : r + 64, j : j + 128] = (x + (half + half * jnp.tanh(inner))).astype(BF16)
+
+    def project(c, hs):
         y = nn(hs[...], w[...]).astype(BF16)
         at = pl.multiple_of(c * CHUNK, CHUNK)
         for h in range(OWN_HEADS):
             q[h, pl.ds(at, CHUNK), :] = y[:, h * 128 : (h + 1) * 128]
             k[h, pl.ds(at, CHUNK), :] = y[:, HALF + h * 128 : HALF + (h + 1) * 128]
             v[h, pl.ds(at, CHUNK), :] = y[:, 2 * HALF + h * 128 : 2 * HALF + (h + 1) * 128]
+
+    prepare(jnp.int32(0), ns, hs)
+
+    def pair(i, _):
+        c = 2 * i
+        project(c, hs)
+        prepare(c + 1, ns2, hs2)
+        project(c + 1, hs2)
+        prepare(c + 2, ns, hs)
         return 0
 
-    lax.fori_loop(0, CHUNKS, chunk, 0)
+    lax.fori_loop(0, CHUNKS // 2 - 1, pair, 0)
+    project(jnp.int32(CHUNKS - 2), hs)
+    prepare(jnp.int32(CHUNKS - 1), ns2, hs2)
+    project(jnp.int32(CHUNKS - 1), hs2)
+
+
+HID_SCRATCH = (
+    VM((CHUNKS, CHUNK, C), BF16),
+    VM((288, C), F32),
+    VM((CHUNK, C), BF16),
+    VM((288, C), F32),
+    VM((CHUNK, C), BF16),
+)
 
 
 KB = 512
@@ -147,17 +171,17 @@
             top = None
             for b in range(0, BINS, KB):
                 s = nt(qh, k[h, b : b + KB, :])
-                ss[:, b : b + KB] = s
+                ss[g, :, b : b + KB] = s
                 m = jnp.max(s, axis=1, keepdims=True)
                 top = m if top is None else jnp.maximum(top, m)
             total = jnp.zeros((CHUNK, 1), F32)
             out = jnp.zeros((CHUNK, HEAD_DIM), F32)
             for b in range(0, BINS, KB):
-                p = jnp.exp((ss[:, b : b + KB] - top) * SCALE)
+                p = jnp.exp2((ss[g, :, b : b + KB] - top) * (SCALE * LOG2E))
                 total = total + jnp.sum(p, axis=1, keepdims=True)
                 out = out + nn(p.astype(BF16), v[h, b : b + KB, :])
                 if g == 0:
-                    ss[:, b : b + KB] = p
+                    ss[g, :, b : b + KB] = p
             inverse = 1.0 / total
             attended = (out * inverse).astype(BF16).astype(F32)
             do = ds[h, g * CHUNK : (g + 1) * CHUNK, :]
@@ -171,14 +195,17 @@
                 acc = jnp.zeros((CHUNK, HEAD_DIM), F32)
                 for b in range(0, BINS, KB):
                     dp = nt(do, v[h, b : b + KB, :])
-                    dsc = (ss[:, b : b + KB] * inverse * (dp - delta)).astype(BF16)
+                    dsc = (ss[g, :, b : b + KB] * (dp - delta)).astype(BF16)
                     acc = acc + nn(dsc, k[h, b : b + KB, :])
-                dq[h, :, :] = (acc * SCALE).astype(BF16)
+                dq[h, :, :] = (acc * (inverse * SCALE)).astype(BF16)
         return 0
 
-    lax.fori_loop(0, OWN_HEADS, head, 0)
+    for h in range(OWN_HEADS):
+        head(h, 0)
     stats[...] = jnp.transpose(sm[...])[0:8, :]
 
+
+FWD_SCRATCH = (VM((OWN_HEADS, 2 * CHUNK, HEAD_DIM), BF16), VM((2, CHUNK, BINS), F32), VM((2 * CHUNK, 128), F32))
 
 EDGE = 16
 WIDE = CHUNK + 2 * EDGE
@@ -218,29 +245,29 @@
     high_stats = jnp.transpose(jnp.tile(high_rows, (16, 1)))
     st[0:EDGE, :] = low_stats[128 - EDGE : 128, :]
     st[EDGE : 2 * EDGE, :] = high_stats[0:EDGE, :]
-    for h in range(OWN_HEADS):
-        kh = kx[h]
-        vh = vx[h]
-
-        def step(dx, carry):
-            acc_k, acc_v = carry
+    def step(dx, carry):
+        row = place(dx)
+        res = []
+        for h in range(OWN_HEADS):
+            acc_k, acc_v = carry[2 * h], carry[2 * h + 1]
             for dz in range(2):
-                c = dz * 4 + dx
-                at = pl.multiple_of(c * CHUNK, CHUNK)
+                at = pl.multiple_of((dz * 4 + dx) * CHUNK, CHUNK)
                 qc = q[h, pl.ds(at, CHUNK), :]
                 dc = ds[h, pl.ds(at, CHUNK), :]
-                row = place(c)
                 lanes = slice(dz * CHUNK, (dz + 1) * CHUNK)
                 log_total = stats[row, h : h + 1, lanes]
                 delta = stats[row, h + OWN_HEADS : h + OWN_HEADS + 1, lanes]
-                p = jnp.exp(nt(kh, qc) * SCALE - log_total)
+                p = jnp.exp2(nt(kx[h], qc) * (SCALE * LOG2E) - log_total * LOG2E)
                 acc_v = acc_v + nn(p.astype(BF16), dc)
-                dsc = (p * (nt(vh, dc) - delta)).astype(BF16)
+                dsc = (p * (nt(vx[h], dc) - delta)).astype(BF16)
                 acc_k = acc_k + nn(dsc, qc)
-            return acc_k, acc_v
-
-        zero = jnp.zeros((WIDE, HEAD_DIM), F32)
-        acc_k, acc_v = lax.fori_loop(0, 4, step, (zero, zero))
+            res += [acc_k, acc_v]
+        return tuple(res)
+
+    zero = jnp.zeros((WIDE, HEAD_DIM), F32)
+    sums = lax.fori_loop(0, 4, step, (zero,) * 6)
+    for h in range(OWN_HEADS):
+        acc_k, acc_v = sums[2 * h], sums[2 * h + 1]
         p = jnp.exp(nt(qx[h], k[h]) * SCALE - st[:, h : h + 1])
         dsc = (p * (nt(dx_[h], v[h]) - st[:, h + OWN_HEADS : h + OWN_HEADS + 1])).astype(BF16)
         dqx = (nn(dsc, k[h]) * SCALE).astype(BF16)
@@ -363,18 +390,14 @@
         hidden_body,
         (head_shape, head_shape, head_shape, jax.ShapeDtypeStruct((160, C), BF16)),
         (pos, near, other, w_own, coef),
-        (VM((CHUNKS, CHUNK, C), BF16), VM((288, C), F32), VM((CHUNK, C), BF16)),
+        HID_SCRATCH,
     )
     part = jax.ShapeDtypeStruct((OWN_HEADS, CHUNK, HEAD_DIM), BF16)
     dq, stats = call(
         forward_body,
         (part, jax.ShapeDtypeStruct((8, 2 * CHUNK), F32)),
         (q, k, v, cot_own, cot_z),
-        (
-            VM((OWN_HEADS, 2 * CHUNK, HEAD_DIM), BF16),
-            VM((CHUNK, BINS), F32),
-            VM((2 * CHUNK, 128), F32),
-        ),
+        FWD_SCRATCH,
     )
     stats, cots = lax.optimization_barrier((stats, cots))
     stats_all = share(stats, "x", 4)

time: 178 us -> 173 us (0.972)
  Pallas kernels: 39.8 us -> 35.3 us
    pallas_call x4, Pallas kernels: 39.8 us -> 35.3 us  [call(): pl.pallas_call(body, out_shape=out_shape, in_specs=specs, out_specs=outs,...]
  transfers between devices with their start and end apart: 9 -> 9, of which waited for: 3 -> 3; matrix products, arithmetic and copies ran while one was open for 4% -> 5% of each run, Pallas kernels for 14% -> 13%
where the time goes in v8:
time: 173 us; the launch traced here: 170 us
  blocking collectives  60.9 us (35%)
  starting transfers between devices  49.1 us (28%)
  Pallas kernels  35.3 us (20%)
  waiting for transfers between devices  10.7 us (6%)
  other arithmetic  7.41 us (4%)
  local copies, waits for them, and re-layouts  5.97 us (3%)
    all_to_all x2, blocking collectives, share(): return lax.all_to_all(wide, axes, 0, 0)  43 us
    pallas_call x4, Pallas kernels, call(): pl.pallas_call(body, out_shape=out_shape, in_specs=specs, out_specs=outs,...  35.3 us
    ppermute x5, starting transfers between devices, swap(): return lax.ppermute(a, axis, [(0, 1), (1, 0)])  35 us
    all_to_all x1, blocking collectives, shards(): part = jnp.sum(lax.all_to_all(wide, ('y', 'x', 'core'), 0, 0), axis=0)  14.6 us
    ppermute x3, starting transfers between devices, from_x(): return lax.ppermute(a, 'x', [((i + step) % 4, i) for i in range(4)])  9.58 us
    ppermute x5, waiting for transfers between devices, swap(): return lax.ppermute(a, axis, [(0, 1), (1, 0)])  8.63 us
    all_to_all x1, starting transfers between devices, share(): return lax.all_to_all(wide, axes, 0, 0)  4.51 us
  transfers between devices with their start and end apart: 9, of which 3 were waited for; matrix products, arithmetic and copies ran while one was open for 5% of the time, Pallas kernels for 13%

profile of v8, /device:TPU:7, one launch (start us, length us, event | category | flops | bytes accessed | tf_op | source)
XLA Modules:
  0.0 170.4 jit_solution(1255860784035923014)
XLA Ops:
  0.7 15.6 %collective-permute-start = (bf16[128,768]{1,0:T(8,128)(2,1)}, bf16[128,768]{1,0:T(8,128)(2,1)}, u32[]{:S(2)}, u32[]{:S(2)}) collective-permute-start(bf16[128,768]{1,0:T(8,128)(2,1)} %bitcast.11), channel_id=1, source_target_pairs={{0,8},{8,0},{1,9},{9,1},{2,10},{10,2},{3,11},{11,3},{4,12},{12,4},... | collective-permute-start | bytes 589832 | tf_op jit(solution)/shard_map/ppermute | solution.py:342
  17.3 2.9 %collective-permute-start.1 = (bf16[128,384]{1,0:T(8,128)(2,1)S(1)}, bf16[128,384]{1,0:T(8,128)(2,1)S(1)}, u32[]{:S(2)}, u32[]{:S(2)}) collective-permute-start(bf16[128,384]{1,0:T(8,128)(2,1)S(1)} %broadcast_select_fusion.8), channel_id=1, source_target_pairs={{0,1},{1,0},{2,3},{3,2},{4,5},{5,4},{6,7},{7,6},{8,9},{9,8},{10,11... | collective-permute-start | bytes 294920 | tf_op jit(solution)/shard_map/ppermute | solution.py:342
  20.2 1.4 broadcast_select_fusion.2
  26.4 4.5 %all-to-all-start = ((bf16[4,256,768]{2,1,0:T(8,128)(2,1)}), bf16[4,256,768]{2,1,0:T(8,128)(2,1)}, u32[]{:S(2)}, u32[]{:S(2)}) async-start(bf16[4,256,768]{2,1,0:T(8,128)(2,1)} %broadcast_in_dim.13), calls=%async_computation | async-start | bytes 3145728 | tf_op jit(solution)/shard_map/all_to_all | solution.py:351
  31.0 9.8 %collective-permute-start.2 = (bf16[128,768]{1,0:T(8,128)(2,1)}, bf16[128,768]{1,0:T(8,128)(2,1)}, u32[]{:S(2)}, u32[]{:S(2)}) collective-permute-start(bf16[128,768]{1,0:T(8,128)(2,1)} %pad_maximum_fusion.3.d0), channel_id=1, source_target_pairs={{0,8},{8,0},{1,9},{9,1},{2,10},{10,2},{3,11},{11,3},{4,12},{12,4},... | collective-permute-start | bytes 589832 | tf_op jit(solution)/shard_map/ppermute | solution.py:342
  40.7 7.3 %collective-permute-done.2.d4 = bf16[128,768]{1,0:T(8,128)(2,1)} collective-permute-done((bf16[128,768]{1,0:T(8,128)(2,1)}, bf16[128,768]{1,0:T(8,128)(2,1)}, u32[]{:S(2)}, u32[]{:S(2)}) %collective-permute-start.2) | collective-permute-done | bytes 196640 | tf_op jit(solution)/shard_map/ppermute | solution.py:342
  48.1 2.1 %all-to-all-done.near = bf16[4,256,768]{2,1,0:T(8,128)(2,1)} async-done(((bf16[4,256,768]{2,1,0:T(8,128)(2,1)}), bf16[4,256,768]{2,1,0:T(8,128)(2,1)}, u32[]{:S(2)}, u32[]{:S(2)}) %all-to-all-start) | async-done | bytes 1572896 | tf_op jit(solution)/shard_map/all_to_all | solution.py:351
  50.1 2.7 %collective-permute-start.3 = (bf16[4,256,768]{2,1,0:T(8,128)(2,1)}, bf16[4,256,768]{2,1,0:T(8,128)(2,1)}, u32[]{:S(2)}, u32[]{:S(2)}) collective-permute-start(bf16[4,256,768]{2,1,0:T(8,128)(2,1)} %all-to-all-done.near), channel_id=1, source_target_pairs={{0,1},{1,0},{2,3},{3,2},{4,5},{5,4},{6,7},{7,6},{8,9},{9,8},{10,11... | collective-permute-start | bytes 4718600 | tf_op jit(solution)/shard_map/ppermute | solution.py:342
  52.8 1.6 constant_dynamic-update-slice_fusion.1
  54.5 1.6 constant_dynamic-update-slice_fusion
  56.1 1.9 %collective-permute-start.4 = (bf16[256,768]{1,0:T(8,128)(2,1)}, bf16[256,768]{1,0:T(8,128)(2,1)}, u32[]{:S(2)}, u32[]{:S(2)}) collective-permute-start(bf16[256,768]{1,0:T(8,128)(2,1)} %constant_dynamic-update-slice_fusion), channel_id=1, source_target_pairs={{2,0},{4,2},{6,4},{0,6},{3,1},{5,3},{7,5},{1,7},{10,8},{12,10},{14... | collective-permute-start | bytes 1179656 | tf_op jit(solution)/shard_map/ppermute | solution.py:346
  58.0 4.9 %collective-permute-start.5 = (bf16[256,768]{1,0:T(8,128)(2,1)}, bf16[256,768]{1,0:T(8,128)(2,1)}, u32[]{:S(2)}, u32[]{:S(2)}) collective-permute-start(bf16[256,768]{1,0:T(8,128)(2,1)} %constant_dynamic-update-slice_fusion), channel_id=1, source_target_pairs={{4,0},{6,2},{0,4},{2,6},{5,1},{7,3},{1,5},{3,7},{12,8},{14,10},{8,... | collective-permute-start | bytes 1179656 | tf_op jit(solution)/shard_map/ppermute | solution.py:346
  62.9 2.8 %collective-permute-start.6 = (bf16[256,768]{1,0:T(8,128)(2,1)}, bf16[256,768]{1,0:T(8,128)(2,1)}, u32[]{:S(2)}, u32[]{:S(2)}) collective-permute-start(bf16[256,768]{1,0:T(8,128)(2,1)} %constant_dynamic-update-slice_fusion), channel_id=1, source_target_pairs={{6,0},{0,2},{2,4},{4,6},{7,1},{1,3},{3,5},{5,7},{14,8},{8,10},{10,... | collective-permute-start | bytes 1179656 | tf_op jit(solution)/shard_map/ppermute | solution.py:346
  66.6 14.2 %shard_map.94 = (bf16[3,2048,128]{2,1,0:T(8,128)(2,1)S(1)}, bf16[3,2048,128]{2,1,0:T(8,128)(2,1)S(1)}, bf16[3,2048,128]{2,1,0:T(8,128)(2,1)S(1)}, bf16[160,768]{1,0:T(8,128)(2,1)S(1)}) custom-call(s32[3]{0:T(128)S(1)} %pad_add_fusion.pos, bf16[4,256,768]{2,1,0:T(8,128)(2,1)} %all-to-all-done.near, bf16[4,256,768]{2,1,0:T(8,128)(2,1)} %collective-permute-done.3.other, ...), custom_call_target="tpu_custom_call" | custom-call | tf_op jit(solution)/shard_map/pallas_call | solution.py:41
  80.8 8.8 %shard_map.95 = (bf16[3,256,128]{2,1,0:T(8,128)(2,1)S(1)}, f32[8,512]{1,0:T(8,128)S(1)}) custom-call(bf16[3,2048,128]{2,1,0:T(8,128)(2,1)S(1)} %get-tuple-element.29.q, bf16[3,2048,128]{2,1,0:T(8,128)(2,1)S(1)} %get-tuple-element.30.k, bf16[3,2048,128]{2,1,0:T(8,128)(2,1)S(1)} %get-tuple-element.31.v, bf16[128,768]{1,0:T(8,128)(2,1)S(1)} %copy-done, ...), custom_call_target="tpu_custom_call" | custom-call | tf_op jit(solution)/shard_map/pallas_call | solution.py:41
  89.6 6.8 %all_to_all.20.stats = f32[4,8,512]{2,1,0:T(8,128)S(1)} all-to-all(f32[4,8,512]{2,1,0:T(8,128)S(1)} %broadcast_in_dim.14), channel_id=1, replica_groups=mesh['y'=4,'zm'=2,'zl'=4,'zh'=2,'x'=4,'core'=2] {'x'}, dimensions={0} | all-to-all | bytes 131072 | tf_op jit(solution)/shard_map/all_to_all | solution.py:351
  96.4 8.5 %shard_map.96 = (bf16[160,1152]{1,0:T(8,128)(2,1)S(1)}, bf16[160,1152]{1,0:T(8,128)(2,1)S(1)}) custom-call(s32[3]{0:T(128)S(1)} %pad_add_fusion.pos, bf16[3,2048,128]{2,1,0:T(8,128)(2,1)S(1)} %get-tuple-element.29.q, bf16[3,2048,128]{2,1,0:T(8,128)(2,1)S(1)} %get-tuple-element.30.k, bf16[3,2048,128]{2,1,0:T(8,128)(2,1)S(1)} %get-tuple-element.31.v, ...), custom_call_target="tpu_custom_call" | custom-call | tf_op jit(solution)/shard_map/pallas_call | solution.py:41
  104.9 4.1 %collective-permute-start.7 = (bf16[160,1152]{1,0:T(8,128)(2,1)S(1)}, bf16[160,1152]{1,0:T(8,128)(2,1)S(1)}, u32[]{:S(2)}, u32[]{:S(2)}) collective-permute-start(bf16[160,1152]{1,0:T(8,128)(2,1)S(1)} %get-tuple-element.40), channel_id=1, source_target_pairs={{0,1},{1,0},{2,3},{3,2},{4,5},{5,4},{6,7},{7,6},{8,9},{9,8},{10,11... | collective-permute-start | bytes 1105928 | tf_op jit(solution)/shard_map/ppermute | solution.py:342
  109.0 1.3 collective-permute-done.7.recv
  110.3 3.9 %shard_map.97 = (bf16[128,768]{1,0:T(8,128)(2,1)}, f32[2,16,128]{2,1,0:T(8,128)S(1)}) custom-call(s32[3]{0:T(128)S(1)} %pad_add_fusion.pos, bf16[160,1152]{1,0:T(8,128)(2,1)S(1)} %get-tuple-element.39.mine, bf16[160,1152]{1,0:T(8,128)(2,1)S(1)} %collective-permute-done.7.recv, bf16[768,1152]{1,0:T(8,128)(2,1)S(1)} %pad_maximum_fusion.w.w_own, ...), custom_call_target="tpu_custom_call" | custom-call | tf_op jit(solution)/shard_map/pallas_call | solution.py:41
  114.2 14.6 %all_to_all.21 = f32[32,16,128]{2,1,0:T(8,128)S(1)} all-to-all(f32[32,16,128]{2,1,0:T(8,128)S(1)} %bitcast.8), channel_id=1, replica_groups=mesh['y'=4,'zm'=2,'zl'=4,'zh'=2,'x'=4,'core'=2] {'y','x','core'}, dimensions={0} | all-to-all | bytes 524288 | tf_op jit(solution)/shard_map/all_to_all | solution.py:427
  128.8 36.2 %all_to_all.22 = bf16[16,16,128]{2,1,0:T(8,128)(2,1)S(1)} all-to-all(bf16[16,16,128]{2,1,0:T(8,128)(2,1)S(1)} %broadcast_in_dim.17), channel_id=1, replica_groups=mesh['y'=4,'zm'=2,'zl'=4,'zh'=2,'x'=4,'core'=2] {'zm','zl','zh'}, dimensions={0} | all-to-all | bytes 131072 | tf_op jit(solution)/shard_map/all_to_all | solution.py:351
  165.1 3.3 %all-gather = f32[32,128]{1,0:T(8,128)S(1)} all-gather(f32[16,128]{1,0:T(8,128)S(1)} %convert_reduce_fusion), channel_id=2, replica_groups=mesh['y'=4,'zm'=2,'zl'=4,'zh'=2,'x'=4,'core'=2] {'core'}, dimensions={0}, use_global_device_ids=true | all-gather | bytes 24576 | tf_op jit(solution)/shard_map/all_gather | solution.py:430
  168.4 1.9 %multiply_reduce_fusion = (f32[768]{0:T(1024)}, f32[5,768]{1,0:T(8,128)}) fusion(f32[5,768]{1,0:T(8,128)S(1)} %constant_dynamic-update-slice_fusion.2, f32[5,768]{1,0:T(8,128)} %param.9, f32[768]{0:T(1024)S(1)} %copy-done.7), kind=kLoop, calls=%fused_computation.16 | loop fusion | flops 10752 | bytes 52224 | tf_op jit(solution)/shard_map/reduce_sum | solution.py:433
  (45 shorter events, 6.9 us)
Async XLA Ops:
  0.6 20.9 %copy-start.7 = (f32[768]{0:T(1024)S(1)}, f32[768]{0:T(1024)}, u32[]{:S(2)}) copy-start(f32[768]{0:T(1024)} %param.8) | copy-start | bytes 9220
  0.6 20.9 %copy-start.2 = (bf16[768,768]{1,0:T(8,128)(2,1)S(1)}, bf16[768,768]{1,0:T(8,128)(2,1)}, u32[]{:S(2)}) copy-start(bf16[768,768]{1,0:T(8,128)(2,1)} %param.12) | copy-start | bytes 3538948
  0.7 23.6 %collective-permute-start = (bf16[128,768]{1,0:T(8,128)(2,1)}, bf16[128,768]{1,0:T(8,128)(2,1)}, u32[]{:S(2)}, u32[]{:S(2)}) collective-permute-start(bf16[128,768]{1,0:T(8,128)(2,1)} %bitcast.11), channel_id=1, source_target_pairs={{0,8},{8,0},{1,9},{9,1},{2,10},{10,2},{3,11},{11,3},{4,12},{12,4},... | collective-permute-start | bytes 589832 | tf_op jit(solution)/shard_map/ppermute | solution.py:342
  16.2 5.3 %copy-start.3 = (bf16[768,768]{1,0:T(8,128)(2,1)S(1)}, bf16[768,768]{1,0:T(8,128)(2,1)}, u32[]{:S(2)}) copy-start(bf16[768,768]{1,0:T(8,128)(2,1)} %param.11) | copy-start | bytes 3538948
  17.3 6.2 %collective-permute-start.1 = (bf16[128,384]{1,0:T(8,128)(2,1)S(1)}, bf16[128,384]{1,0:T(8,128)(2,1)S(1)}, u32[]{:S(2)}, u32[]{:S(2)}) collective-permute-start(bf16[128,384]{1,0:T(8,128)(2,1)S(1)} %broadcast_select_fusion.8), channel_id=1, source_target_pairs={{0,1},{1,0},{2,3},{3,2},{4,5},{5,4},{6,7},{7,6},{8,9},{9,8},{10,11... | collective-permute-start | bytes 294920 | tf_op jit(solution)/shard_map/ppermute | solution.py:342
  22.1 0.7 copy-start.6
  22.1 1.4 copy-start.4
  22.1 2.1 %copy-start.5 = (bf16[1,128,768]{2,1,0:T(8,128)(2,1)S(1)}, bf16[1,128,768]{2,1,0:T(8,128)(2,1)}, u32[]{:S(2)}) copy-start(bf16[1,128,768]{2,1,0:T(8,128)(2,1)} %param.7) | copy-start | bytes 589828
  26.4 23.7 %all-to-all-start = ((bf16[4,256,768]{2,1,0:T(8,128)(2,1)}), bf16[4,256,768]{2,1,0:T(8,128)(2,1)}, u32[]{:S(2)}, u32[]{:S(2)}) async-start(bf16[4,256,768]{2,1,0:T(8,128)(2,1)} %broadcast_in_dim.13), calls=%async_computation | async-start | bytes 3145728 | tf_op jit(solution)/shard_map/all_to_all | solution.py:351
  31.0 17.1 %collective-permute-start.2 = (bf16[128,768]{1,0:T(8,128)(2,1)}, bf16[128,768]{1,0:T(8,128)(2,1)}, u32[]{:S(2)}, u32[]{:S(2)}) collective-permute-start(bf16[128,768]{1,0:T(8,128)(2,1)} %pad_maximum_fusion.3.d0), channel_id=1, source_target_pairs={{0,8},{8,0},{1,9},{9,1},{2,10},{10,2},{3,11},{11,3},{4,12},{12,4},... | collective-permute-start | bytes 589832 | tf_op jit(solution)/shard_map/ppermute | solution.py:342
  50.1 15.6 %collective-permute-start.3 = (bf16[4,256,768]{2,1,0:T(8,128)(2,1)}, bf16[4,256,768]{2,1,0:T(8,128)(2,1)}, u32[]{:S(2)}, u32[]{:S(2)}) collective-permute-start(bf16[4,256,768]{2,1,0:T(8,128)(2,1)} %all-to-all-done.near), channel_id=1, source_target_pairs={{0,1},{1,0},{2,3},{3,2},{4,5},{5,4},{6,7},{7,6},{8,9},{9,8},{10,11... | collective-permute-start | bytes 4718600 | tf_op jit(solution)/shard_map/ppermute | solution.py:342
  56.1 33.5 %collective-permute-start.4 = (bf16[256,768]{1,0:T(8,128)(2,1)}, bf16[256,768]{1,0:T(8,128)(2,1)}, u32[]{:S(2)}, u32[]{:S(2)}) collective-permute-start(bf16[256,768]{1,0:T(8,128)(2,1)} %constant_dynamic-update-slice_fusion), channel_id=1, source_target_pairs={{2,0},{4,2},{6,4},{0,6},{3,1},{5,3},{7,5},{1,7},{10,8},{12,10},{14... | collective-permute-start | bytes 1179656 | tf_op jit(solution)/shard_map/ppermute | solution.py:346
  58.0 31.6 %collective-permute-start.5 = (bf16[256,768]{1,0:T(8,128)(2,1)}, bf16[256,768]{1,0:T(8,128)(2,1)}, u32[]{:S(2)}, u32[]{:S(2)}) collective-permute-start(bf16[256,768]{1,0:T(8,128)(2,1)} %constant_dynamic-update-slice_fusion), channel_id=1, source_target_pairs={{4,0},{6,2},{0,4},{2,6},{5,1},{7,3},{1,5},{3,7},{12,8},{14,10},{8,... | collective-permute-start | bytes 1179656 | tf_op jit(solution)/shard_map/ppermute | solution.py:346
  62.9 26.7 %collective-permute-start.6 = (bf16[256,768]{1,0:T(8,128)(2,1)}, bf16[256,768]{1,0:T(8,128)(2,1)}, u32[]{:S(2)}, u32[]{:S(2)}) collective-permute-start(bf16[256,768]{1,0:T(8,128)(2,1)} %constant_dynamic-update-slice_fusion), channel_id=1, source_target_pairs={{6,0},{0,2},{2,4},{4,6},{7,1},{1,3},{3,5},{5,7},{14,8},{8,10},{10,... | collective-permute-start | bytes 1179656 | tf_op jit(solution)/shard_map/ppermute | solution.py:346
  65.8 15.0 %copy-start = (bf16[128,768]{1,0:T(8,128)(2,1)S(1)}, bf16[128,768]{1,0:T(8,128)(2,1)}, u32[]{:S(2)}) copy-start(bf16[128,768]{1,0:T(8,128)(2,1)} %pad_maximum_fusion.3.d0) | copy-start | bytes 589828
  65.8 0.8 copy-start.1
  104.9 5.4 %collective-permute-start.7 = (bf16[160,1152]{1,0:T(8,128)(2,1)S(1)}, bf16[160,1152]{1,0:T(8,128)(2,1)S(1)}, u32[]{:S(2)}, u32[]{:S(2)}) collective-permute-start(bf16[160,1152]{1,0:T(8,128)(2,1)S(1)} %get-tuple-element.40), channel_id=1, source_target_pairs={{0,1},{1,0},{2,3},{3,2},{4,5},{5,4},{6,7},{7,6},{8,9},{9,8},{10,11... | collective-permute-start | bytes 1105928 | tf_op jit(solution)/shard_map/ppermute | solution.py:342

commit v9 on v8

--- a/solution.py
+++ b/solution.py
@@ -213,18 +213,17 @@
 
 
 def backward_body(
-    pos, q, k, v, dq, d0, d4, b1, b2, b3, stats, mine, give, ds, gs, kx, vx, qx, dx_, st
+    pos, q, k, v, dq, d0, d4, d1, d2, d3, d5, d6, d7, stats, mine, give, ds, gs, kx, vx, qx, dx_, st
 ):
     core = pos[2]
 
     def place(c):
         return lax.rem(pos[1] + c, 4)
 
-    blocks = ((d0, 0), (b1, 0), (b2, 0), (b3, 0), (d4, 0), (b1, BLOCK), (b2, BLOCK), (b3, BLOCK))
-    for c, (d, low) in enumerate(blocks):
+    for c, d in enumerate((d0, d1, d2, d3, d4, d5, d6, d7)):
         for h in range(OWN_HEADS):
             lo = c * CHUNK
-            rows = slice(low, low + BLOCK)
+            rows = slice(0, BLOCK)
             ds[h, lo : lo + BLOCK, :] = d[rows, h * 128 : (h + 1) * 128]
             ds[h, lo + BLOCK : lo + CHUNK, :] = d[rows, HALF + h * 128 : HALF + (h + 1) * 128]
     prev, nxt, _, _ = neighbours(pos, jnp.int32(0), jnp.int32(0))
@@ -375,15 +374,15 @@
     w_own = jnp.concatenate([p[0] for p in parts], axis=1)
     w_oth = jnp.concatenate([p[1] for p in parts], axis=1)
     coef = jnp.concatenate([conv_taps, gain, jnp.zeros((2, C), F32)], axis=0)
-    sig_z, cot_own, w_own, w_oth, coef = lax.optimization_barrier(
-        (sig_z, cot_own, w_own, w_oth, coef)
+    cots_near = [from_x(cot_own, d) for d in (1, 2, 3)]
+    sig_z, cot_own, w_own, w_oth, coef, cots_near = lax.optimization_barrier(
+        (sig_z, cot_own, w_own, w_oth, coef, cots_near)
     )
     cot_z = swap(cot_own, "zh")
     near = share(jnp.concatenate([sig, sig_z], axis=0), "x", 4)
     near, cot_z = lax.optimization_barrier((near, cot_z))
     other = swap(near, "core")
-    both = jnp.concatenate([cot_own, cot_z], axis=0)
-    cots = [from_x(both, d) for d in (1, 2, 3)]
+    cots = cots_near + [from_x(cot_z, d) for d in (1, 2, 3)]
 
     head_shape = jax.ShapeDtypeStruct((OWN_HEADS, BINS, HEAD_DIM), BF16)
     q, k, v, ext = call(

time: 173 us -> 177 us (1.023)
  blocking collectives: 60.9 us -> 41 us
  starting transfers between devices: 49.1 us -> 62.7 us
  waiting for transfers between devices: 10.7 us -> 23.7 us
    all_to_all x2, blocking collectives: 43 us -> 23.1 us  [share(): return lax.all_to_all(wide, axes, 0, 0)]
    ppermute x5, waiting for transfers between devices: 8.63 us -> 19 us  [swap(): return lax.ppermute(a, axis, [(0, 1), (1, 0)])]
    ppermute x3 -> x6, starting transfers between devices: 9.58 us -> 17.9 us  [from_x(): return lax.ppermute(a, 'x', [((i + step) % 4, i) for i in range(4)])]
    ppermute x3 -> x6, waiting for transfers between devices: 0.02 us -> 4.73 us  [from_x(): return lax.ppermute(a, 'x', [((i + step) % 4, i) for i in range(4)])]
    all_to_all x1, starting transfers between devices: 4.51 us -> 7.6 us  [share(): return lax.all_to_all(wide, axes, 0, 0)]
    ppermute x5, starting transfers between devices: 35 us -> 37.2 us  [swap(): return lax.ppermute(a, axis, [(0, 1), (1, 0)])]
    all_to_all x1, waiting for transfers between devices: 2.07 us -> 0.01 us  [share(): return lax.all_to_all(wide, axes, 0, 0)]
  transfers between devices with their start and end apart: 9 -> 12, of which waited for: 3 -> 4; matrix products, arithmetic and copies ran while one was open for 5% -> 2% of each run, Pallas kernels for 13% -> 13%
where the time goes in v9:
time: 177 us; the launch traced here: 174 us
  starting transfers between devices  62.7 us (35%)
  blocking collectives  41 us (23%)
  Pallas kernels  35.3 us (20%)
  waiting for transfers between devices  23.7 us (13%)
  other arithmetic  5.83 us (3%)
  local copies, waits for them, and re-layouts  4.89 us (3%)
    ppermute x5, starting transfers between devices, swap(): return lax.ppermute(a, axis, [(0, 1), (1, 0)])  37.2 us
    pallas_call x4, Pallas kernels, call(): pl.pallas_call(body, out_shape=out_shape, in_specs=specs, out_specs=outs,...  35.3 us
    all_to_all x2, blocking collectives, share(): return lax.all_to_all(wide, axes, 0, 0)  23.1 us
    ppermute x5, waiting for transfers between devices, swap(): return lax.ppermute(a, axis, [(0, 1), (1, 0)])  19 us
    ppermute x6, starting transfers between devices, from_x(): return lax.ppermute(a, 'x', [((i + step) % 4, i) for i in range(4)])  17.9 us
    all_to_all x1, blocking collectives, shards(): part = jnp.sum(lax.all_to_all(wide, ('y', 'x', 'core'), 0, 0), axis=0)  14.6 us
    all_to_all x1, starting transfers between devices, share(): return lax.all_to_all(wide, axes, 0, 0)  7.6 us
    ppermute x6, waiting for transfers between devices, from_x(): return lax.ppermute(a, 'x', [((i + step) % 4, i) for i in range(4)])  4.73 us
  transfers between devices with their start and end apart: 12, of which 4 were waited for; matrix products, arithmetic and copies ran while one was open for 2% of the time, Pallas kernels for 13%

profile of v9, /device:TPU:7, one launch (start us, length us, event | category | flops | bytes accessed | tf_op | source)
XLA Modules:
  0.0 174.4 jit_solution(16743972057936985986)
XLA Ops:
  1.8 2.6 %collective-permute-start.1 = (bf16[128,384]{1,0:T(8,128)(2,1)S(1)}, bf16[128,384]{1,0:T(8,128)(2,1)S(1)}, u32[]{:S(2)}, u32[]{:S(2)}) collective-permute-start(bf16[128,384]{1,0:T(8,128)(2,1)S(1)} %broadcast_select_fusion.8), channel_id=1, source_target_pairs={{0,1},{1,0},{2,3},{3,2},{4,5},{5,4},{6,7},{7,6},{8,9},{9,8},{10,11... | collective-permute-start | bytes 294920 | tf_op jit(solution)/shard_map/ppermute | solution.py:341
  4.4 15.4 %collective-permute-start = (bf16[128,768]{1,0:T(8,128)(2,1)}, bf16[128,768]{1,0:T(8,128)(2,1)S(1)}, u32[]{:S(2)}, u32[]{:S(2)}) collective-permute-start(bf16[128,768]{1,0:T(8,128)(2,1)} %bitcast.11), channel_id=1, source_target_pairs={{0,8},{8,0},{1,9},{9,1},{2,10},{10,2},{3,11},{11,3},{4,12},{12,4},... | collective-permute-start | bytes 589832 | tf_op jit(solution)/shard_map/ppermute | solution.py:341
  19.8 1.4 broadcast_select_fusion.2
  22.6 2.5 %collective-permute-start.2 = (bf16[128,768]{1,0:T(8,128)(2,1)S(1)}, bf16[128,768]{1,0:T(8,128)(2,1)S(1)}, u32[]{:S(2)}, u32[]{:S(2)}) collective-permute-start(bf16[128,768]{1,0:T(8,128)(2,1)S(1)} %pad_maximum_fusion.3.d0), channel_id=1, source_target_pairs={{2,0},{4,2},{6,4},{0,6},{3,1},{5,3},{7,5},{1,7},{10,8},{12,10},{14... | collective-permute-start | bytes 589832 | tf_op jit(solution)/shard_map/ppermute | solution.py:345
  25.1 2.7 %collective-permute-start.3 = (bf16[128,768]{1,0:T(8,128)(2,1)S(1)}, bf16[128,768]{1,0:T(8,128)(2,1)S(1)}, u32[]{:S(2)}, u32[]{:S(2)}) collective-permute-start(bf16[128,768]{1,0:T(8,128)(2,1)S(1)} %pad_maximum_fusion.3.d0), channel_id=1, source_target_pairs={{4,0},{6,2},{0,4},{2,6},{5,1},{7,3},{1,5},{3,7},{12,8},{14,10},{8,... | collective-permute-start | bytes 589832 | tf_op jit(solution)/shard_map/ppermute | solution.py:345
  27.8 3.7 %collective-permute-start.4 = (bf16[128,768]{1,0:T(8,128)(2,1)S(1)}, bf16[128,768]{1,0:T(8,128)(2,1)S(1)}, u32[]{:S(2)}, u32[]{:S(2)}) collective-permute-start(bf16[128,768]{1,0:T(8,128)(2,1)S(1)} %pad_maximum_fusion.3.d0), channel_id=1, source_target_pairs={{6,0},{0,2},{2,4},{4,6},{7,1},{1,3},{3,5},{5,7},{14,8},{8,10},{10,... | collective-permute-start | bytes 589832 | tf_op jit(solution)/shard_map/ppermute | solution.py:345
  32.3 3.9 %collective-permute-done.2.d1 = bf16[128,768]{1,0:T(8,128)(2,1)S(1)} collective-permute-done((bf16[128,768]{1,0:T(8,128)(2,1)S(1)}, bf16[128,768]{1,0:T(8,128)(2,1)S(1)}, u32[]{:S(2)}, u32[]{:S(2)}) %collective-permute-start.2) | collective-permute-done | bytes 196640 | tf_op jit(solution)/shard_map/ppermute | solution.py:345
  40.3 7.6 %all-to-all-start = ((bf16[4,256,768]{2,1,0:T(8,128)(2,1)}), bf16[4,256,768]{2,1,0:T(8,128)(2,1)}, u32[]{:S(2)}, u32[]{:S(2)}) async-start(bf16[4,256,768]{2,1,0:T(8,128)(2,1)} %broadcast_in_dim.13), calls=%async_computation | async-start | bytes 3145728 | tf_op jit(solution)/shard_map/all_to_all | solution.py:350
  47.9 2.0 %collective-permute-start.5 = (bf16[128,768]{1,0:T(8,128)(2,1)}, bf16[128,768]{1,0:T(8,128)(2,1)}, u32[]{:S(2)}, u32[]{:S(2)}) collective-permute-start(bf16[128,768]{1,0:T(8,128)(2,1)} %copy-done), channel_id=1, source_target_pairs={{0,8},{8,0},{1,9},{9,1},{2,10},{10,2},{3,11},{11,3},{4,12},{12,4},... | collective-permute-start | bytes 589832 | tf_op jit(solution)/shard_map/ppermute | solution.py:341
  49.8 17.7 %collective-permute-done.5.d4 = bf16[128,768]{1,0:T(8,128)(2,1)} collective-permute-done((bf16[128,768]{1,0:T(8,128)(2,1)}, bf16[128,768]{1,0:T(8,128)(2,1)}, u32[]{:S(2)}, u32[]{:S(2)}) %collective-permute-start.5) | collective-permute-done | bytes 196640 | tf_op jit(solution)/shard_map/ppermute | solution.py:341
  67.5 13.2 %collective-permute-start.6 = (bf16[4,256,768]{2,1,0:T(8,128)(2,1)}, bf16[4,256,768]{2,1,0:T(8,128)(2,1)}, u32[]{:S(2)}, u32[]{:S(2)}) collective-permute-start(bf16[4,256,768]{2,1,0:T(8,128)(2,1)} %all-to-all-done.near), channel_id=1, source_target_pairs={{0,1},{1,0},{2,3},{3,2},{4,5},{5,4},{6,7},{7,6},{8,9},{9,8},{10,11... | collective-permute-start | bytes 4718600 | tf_op jit(solution)/shard_map/ppermute | solution.py:341
  80.7 2.5 %collective-permute-start.7 = (bf16[128,768]{1,0:T(8,128)(2,1)}, bf16[128,768]{1,0:T(8,128)(2,1)}, u32[]{:S(2)}, u32[]{:S(2)}) collective-permute-start(bf16[128,768]{1,0:T(8,128)(2,1)} %collective-permute-done.5.d4), channel_id=1, source_target_pairs={{2,0},{4,2},{6,4},{0,6},{3,1},{5,3},{7,5},{1,7},{10,8},{12,10},{14... | collective-permute-start | bytes 589832 | tf_op jit(solution)/shard_map/ppermute | solution.py:345
  83.2 2.6 %collective-permute-start.8 = (bf16[128,768]{1,0:T(8,128)(2,1)}, bf16[128,768]{1,0:T(8,128)(2,1)}, u32[]{:S(2)}, u32[]{:S(2)}) collective-permute-start(bf16[128,768]{1,0:T(8,128)(2,1)} %collective-permute-done.5.d4), channel_id=1, source_target_pairs={{4,0},{6,2},{0,4},{2,6},{5,1},{7,3},{1,5},{3,7},{12,8},{14,10},{8,... | collective-permute-start | bytes 589832 | tf_op jit(solution)/shard_map/ppermute | solution.py:345
  85.8 3.9 %collective-permute-start.9 = (bf16[128,768]{1,0:T(8,128)(2,1)}, bf16[128,768]{1,0:T(8,128)(2,1)}, u32[]{:S(2)}, u32[]{:S(2)}) collective-permute-start(bf16[128,768]{1,0:T(8,128)(2,1)} %collective-permute-done.5.d4), channel_id=1, source_target_pairs={{6,0},{0,2},{2,4},{4,6},{7,1},{1,3},{3,5},{5,7},{14,8},{8,10},{10,... | collective-permute-start | bytes 589832 | tf_op jit(solution)/shard_map/ppermute | solution.py:345
  90.6 14.2 %shard_map.94 = (bf16[3,2048,128]{2,1,0:T(8,128)(2,1)S(1)}, bf16[3,2048,128]{2,1,0:T(8,128)(2,1)S(1)}, bf16[3,2048,128]{2,1,0:T(8,128)(2,1)S(1)}, bf16[160,768]{1,0:T(8,128)(2,1)S(1)}) custom-call(s32[3]{0:T(128)S(1)} %pad_add_fusion.pos, bf16[4,256,768]{2,1,0:T(8,128)(2,1)} %all-to-all-done.near, bf16[4,256,768]{2,1,0:T(8,128)(2,1)} %collective-permute-done.6.other, ...), custom_call_target="tpu_custom_call" | custom-call | tf_op jit(solution)/shard_map/pallas_call | solution.py:41
  104.8 8.8 %shard_map.95 = (bf16[3,256,128]{2,1,0:T(8,128)(2,1)S(1)}, f32[8,512]{1,0:T(8,128)S(1)}) custom-call(bf16[3,2048,128]{2,1,0:T(8,128)(2,1)S(1)} %get-tuple-element.35.q, bf16[3,2048,128]{2,1,0:T(8,128)(2,1)S(1)} %get-tuple-element.36.k, bf16[3,2048,128]{2,1,0:T(8,128)(2,1)S(1)} %get-tuple-element.37.v, bf16[128,768]{1,0:T(8,128)(2,1)S(1)} %copy-done.1, ...), custom_call_target="tpu_custom_call" | custom-call | tf_op jit(solution)/shard_map/pallas_call | solution.py:41
  113.7 6.5 %all_to_all.20.stats = f32[4,8,512]{2,1,0:T(8,128)S(1)} all-to-all(f32[4,8,512]{2,1,0:T(8,128)S(1)} %broadcast_in_dim.14), channel_id=1, replica_groups=mesh['y'=4,'zm'=2,'zl'=4,'zh'=2,'x'=4,'core'=2] {'x'}, dimensions={0} | all-to-all | bytes 131072 | tf_op jit(solution)/shard_map/all_to_all | solution.py:350
  120.2 8.4 %shard_map.96 = (bf16[160,1152]{1,0:T(8,128)(2,1)S(1)}, bf16[160,1152]{1,0:T(8,128)(2,1)S(1)}) custom-call(s32[3]{0:T(128)S(1)} %pad_add_fusion.pos, bf16[3,2048,128]{2,1,0:T(8,128)(2,1)S(1)} %get-tuple-element.35.q, bf16[3,2048,128]{2,1,0:T(8,128)(2,1)S(1)} %get-tuple-element.36.k, bf16[3,2048,128]{2,1,0:T(8,128)(2,1)S(1)} %get-tuple-element.37.v, ...), custom_call_target="tpu_custom_call" | custom-call | tf_op jit(solution)/shard_map/pallas_call | solution.py:41
  128.6 4.1 %collective-permute-start.10 = (bf16[160,1152]{1,0:T(8,128)(2,1)S(1)}, bf16[160,1152]{1,0:T(8,128)(2,1)S(1)}, u32[]{:S(2)}, u32[]{:S(2)}) collective-permute-start(bf16[160,1152]{1,0:T(8,128)(2,1)S(1)} %get-tuple-element.52), channel_id=1, source_target_pairs={{0,1},{1,0},{2,3},{3,2},{4,5},{5,4},{6,7},{7,6},{8,9},{9,8},{10,11... | collective-permute-start | bytes 1105928 | tf_op jit(solution)/shard_map/ppermute | solution.py:341
  134.0 3.9 %shard_map.97 = (bf16[128,768]{1,0:T(8,128)(2,1)}, f32[2,16,128]{2,1,0:T(8,128)S(1)}) custom-call(s32[3]{0:T(128)S(1)} %pad_add_fusion.pos, bf16[160,1152]{1,0:T(8,128)(2,1)S(1)} %get-tuple-element.51.mine, bf16[160,1152]{1,0:T(8,128)(2,1)S(1)} %collective-permute-done.10.recv, bf16[768,1152]{1,0:T(8,128)(2,1)S(1)} %pad_maximum_fusion.w.w_own, ...), custom_call_target="tpu_custom_call" | custom-call | tf_op jit(solution)/shard_map/pallas_call | solution.py:41
  137.9 14.6 %all_to_all.21 = f32[32,16,128]{2,1,0:T(8,128)S(1)} all-to-all(f32[32,16,128]{2,1,0:T(8,128)S(1)} %bitcast.8), channel_id=1, replica_groups=mesh['y'=4,'zm'=2,'zl'=4,'zh'=2,'x'=4,'core'=2] {'y','x','core'}, dimensions={0} | all-to-all | bytes 524288 | tf_op jit(solution)/shard_map/all_to_all | solution.py:426
  152.6 16.5 %all_to_all.22 = bf16[16,16,128]{2,1,0:T(8,128)(2,1)S(1)} all-to-all(bf16[16,16,128]{2,1,0:T(8,128)(2,1)S(1)} %broadcast_in_dim.17), channel_id=1, replica_groups=mesh['y'=4,'zm'=2,'zl'=4,'zh'=2,'x'=4,'core'=2] {'zm','zl','zh'}, dimensions={0} | all-to-all | bytes 131072 | tf_op jit(solution)/shard_map/all_to_all | solution.py:350
  169.1 3.3 %all-gather = f32[32,128]{1,0:T(8,128)S(1)} all-gather(f32[16,128]{1,0:T(8,128)S(1)} %convert_reduce_fusion), channel_id=2, replica_groups=mesh['y'=4,'zm'=2,'zl'=4,'zh'=2,'x'=4,'core'=2] {'core'}, dimensions={0}, use_global_device_ids=true | all-gather | bytes 24576 | tf_op jit(solution)/shard_map/all_gather | solution.py:429
  172.5 1.9 %multiply_reduce_fusion = (f32[768]{0:T(1024)}, f32[5,768]{1,0:T(8,128)}) fusion(f32[5,768]{1,0:T(8,128)S(1)} %constant_dynamic-update-slice_fusion, f32[5,768]{1,0:T(8,128)} %param.9, f32[768]{0:T(1024)S(1)} %copy-done.14), kind=kLoop, calls=%fused_computation.16 | loop fusion | flops 10752 | bytes 52224 | tf_op jit(solution)/shard_map/reduce_sum | solution.py:432
  (63 shorter events, 9.6 us)
Async XLA Ops:
  0.6 20.5 %copy-start.9 = (bf16[768,768]{1,0:T(8,128)(2,1)S(1)}, bf16[768,768]{1,0:T(8,128)(2,1)}, u32[]{:S(2)}) copy-start(bf16[768,768]{1,0:T(8,128)(2,1)} %param.12) | copy-start | bytes 3538948
  0.6 20.5 %copy-start.10 = (bf16[768,768]{1,0:T(8,128)(2,1)S(1)}, bf16[768,768]{1,0:T(8,128)(2,1)}, u32[]{:S(2)}) copy-start(bf16[768,768]{1,0:T(8,128)(2,1)} %param.11) | copy-start | bytes 3538948
  1.8 20.6 %collective-permute-start.1 = (bf16[128,384]{1,0:T(8,128)(2,1)S(1)}, bf16[128,384]{1,0:T(8,128)(2,1)S(1)}, u32[]{:S(2)}, u32[]{:S(2)}) collective-permute-start(bf16[128,384]{1,0:T(8,128)(2,1)S(1)} %broadcast_select_fusion.8), channel_id=1, source_target_pairs={{0,1},{1,0},{2,3},{3,2},{4,5},{5,4},{6,7},{7,6},{8,9},{9,8},{10,11... | collective-permute-start | bytes 294920 | tf_op jit(solution)/shard_map/ppermute | solution.py:341
  4.4 27.9 %collective-permute-start = (bf16[128,768]{1,0:T(8,128)(2,1)}, bf16[128,768]{1,0:T(8,128)(2,1)S(1)}, u32[]{:S(2)}, u32[]{:S(2)}) collective-permute-start(bf16[128,768]{1,0:T(8,128)(2,1)} %bitcast.11), channel_id=1, source_target_pairs={{0,8},{8,0},{1,9},{9,1},{2,10},{10,2},{3,11},{11,3},{4,12},{12,4},... | collective-permute-start | bytes 589832 | tf_op jit(solution)/shard_map/ppermute | solution.py:341
  21.6 0.7 copy-start.14
  21.6 0.9 copy-start.11
  21.6 9.9 %copy-start.13 = (f32[5,768]{1,0:T(8,128)S(1)}, f32[5,768]{1,0:T(8,128)}, u32[]{:S(2)}) copy-start(f32[5,768]{1,0:T(8,128)} %param.9) | copy-start | bytes 46084
  21.6 17.4 %copy-start.12 = (bf16[1,128,768]{2,1,0:T(8,128)(2,1)S(1)}, bf16[1,128,768]{2,1,0:T(8,128)(2,1)}, u32[]{:S(2)}) copy-start(bf16[1,128,768]{2,1,0:T(8,128)(2,1)} %param.7) | copy-start | bytes 589828
  22.6 5.2 %copy-start = (bf16[128,768]{1,0:T(8,128)(2,1)}, bf16[128,768]{1,0:T(8,128)(2,1)S(1)}, u32[]{:S(2)}) copy-start(bf16[128,768]{1,0:T(8,128)(2,1)S(1)} %pad_maximum_fusion.3.d0) | copy-start | bytes 589828
  22.6 13.5 %collective-permute-start.2 = (bf16[128,768]{1,0:T(8,128)(2,1)S(1)}, bf16[128,768]{1,0:T(8,128)(2,1)S(1)}, u32[]{:S(2)}, u32[]{:S(2)}) collective-permute-start(bf16[128,768]{1,0:T(8,128)(2,1)S(1)} %pad_maximum_fusion.3.d0), channel_id=1, source_target_pairs={{2,0},{4,2},{6,4},{0,6},{3,1},{5,3},{7,5},{1,7},{10,8},{12,10},{14... | collective-permute-start | bytes 589832 | tf_op jit(solution)/shard_map/ppermute | solution.py:345
  25.1 11.7 %collective-permute-start.3 = (bf16[128,768]{1,0:T(8,128)(2,1)S(1)}, bf16[128,768]{1,0:T(8,128)(2,1)S(1)}, u32[]{:S(2)}, u32[]{:S(2)}) collective-permute-start(bf16[128,768]{1,0:T(8,128)(2,1)S(1)} %pad_maximum_fusion.3.d0), channel_id=1, source_target_pairs={{4,0},{6,2},{0,4},{2,6},{5,1},{7,3},{1,5},{3,7},{12,8},{14,10},{8,... | collective-permute-start | bytes 589832 | tf_op jit(solution)/shard_map/ppermute | solution.py:345
  27.8 10.5 %collective-permute-start.4 = (bf16[128,768]{1,0:T(8,128)(2,1)S(1)}, bf16[128,768]{1,0:T(8,128)(2,1)S(1)}, u32[]{:S(2)}, u32[]{:S(2)}) collective-permute-start(bf16[128,768]{1,0:T(8,128)(2,1)S(1)} %pad_maximum_fusion.3.d0), channel_id=1, source_target_pairs={{6,0},{0,2},{2,4},{4,6},{7,1},{1,3},{3,5},{5,7},{14,8},{8,10},{10,... | collective-permute-start | bytes 589832 | tf_op jit(solution)/shard_map/ppermute | solution.py:345
  40.3 27.3 %all-to-all-start = ((bf16[4,256,768]{2,1,0:T(8,128)(2,1)}), bf16[4,256,768]{2,1,0:T(8,128)(2,1)}, u32[]{:S(2)}, u32[]{:S(2)}) async-start(bf16[4,256,768]{2,1,0:T(8,128)(2,1)} %broadcast_in_dim.13), calls=%async_computation | async-start | bytes 3145728 | tf_op jit(solution)/shard_map/all_to_all | solution.py:350
  47.9 19.7 %collective-permute-start.5 = (bf16[128,768]{1,0:T(8,128)(2,1)}, bf16[128,768]{1,0:T(8,128)(2,1)}, u32[]{:S(2)}, u32[]{:S(2)}) collective-permute-start(bf16[128,768]{1,0:T(8,128)(2,1)} %copy-done), channel_id=1, source_target_pairs={{0,8},{8,0},{1,9},{9,1},{2,10},{10,2},{3,11},{11,3},{4,12},{12,4},... | collective-permute-start | bytes 589832 | tf_op jit(solution)/shard_map/ppermute | solution.py:341
  67.5 22.2 %collective-permute-start.6 = (bf16[4,256,768]{2,1,0:T(8,128)(2,1)}, bf16[4,256,768]{2,1,0:T(8,128)(2,1)}, u32[]{:S(2)}, u32[]{:S(2)}) collective-permute-start(bf16[4,256,768]{2,1,0:T(8,128)(2,1)} %all-to-all-done.near), channel_id=1, source_target_pairs={{0,1},{1,0},{2,3},{3,2},{4,5},{5,4},{6,7},{7,6},{8,9},{9,8},{10,11... | collective-permute-start | bytes 4718600 | tf_op jit(solution)/shard_map/ppermute | solution.py:341
  80.7 32.9 %collective-permute-start.7 = (bf16[128,768]{1,0:T(8,128)(2,1)}, bf16[128,768]{1,0:T(8,128)(2,1)}, u32[]{:S(2)}, u32[]{:S(2)}) collective-permute-start(bf16[128,768]{1,0:T(8,128)(2,1)} %collective-permute-done.5.d4), channel_id=1, source_target_pairs={{2,0},{4,2},{6,4},{0,6},{3,1},{5,3},{7,5},{1,7},{10,8},{12,10},{14... | collective-permute-start | bytes 589832 | tf_op jit(solution)/shard_map/ppermute | solution.py:345
  83.2 30.5 %collective-permute-start.8 = (bf16[128,768]{1,0:T(8,128)(2,1)}, bf16[128,768]{1,0:T(8,128)(2,1)}, u32[]{:S(2)}, u32[]{:S(2)}) collective-permute-start(bf16[128,768]{1,0:T(8,128)(2,1)} %collective-permute-done.5.d4), channel_id=1, source_target_pairs={{4,0},{6,2},{0,4},{2,6},{5,1},{7,3},{1,5},{3,7},{12,8},{14,10},{8,... | collective-permute-start | bytes 589832 | tf_op jit(solution)/shard_map/ppermute | solution.py:345
  85.8 27.9 %collective-permute-start.9 = (bf16[128,768]{1,0:T(8,128)(2,1)}, bf16[128,768]{1,0:T(8,128)(2,1)}, u32[]{:S(2)}, u32[]{:S(2)}) collective-permute-start(bf16[128,768]{1,0:T(8,128)(2,1)} %collective-permute-done.5.d4), channel_id=1, source_target_pairs={{6,0},{0,2},{2,4},{4,6},{7,1},{1,3},{3,5},{5,7},{14,8},{8,10},{10,... | collective-permute-start | bytes 589832 | tf_op jit(solution)/shard_map/ppermute | solution.py:345
  89.8 15.0 %copy-start.1 = (bf16[128,768]{1,0:T(8,128)(2,1)S(1)}, bf16[128,768]{1,0:T(8,128)(2,1)}, u32[]{:S(2)}) copy-start(bf16[128,768]{1,0:T(8,128)(2,1)} %copy-done) | copy-start | bytes 589828
  89.8 0.8 copy-start.2
  104.8 15.4 %copy-start.4 = (bf16[128,768]{1,0:T(8,128)(2,1)S(1)}, bf16[128,768]{1,0:T(8,128)(2,1)}, u32[]{:S(2)}) copy-start(bf16[128,768]{1,0:T(8,128)(2,1)} %copy-done.3) | copy-start | bytes 589828
  104.8 15.4 %copy-start.6 = (bf16[128,768]{1,0:T(8,128)(2,1)S(1)}, bf16[128,768]{1,0:T(8,128)(2,1)}, u32[]{:S(2)}) copy-start(bf16[128,768]{1,0:T(8,128)(2,1)} %copy-done.5) | copy-start | bytes 589828
  104.8 15.4 %copy-start.8 = (bf16[128,768]{1,0:T(8,128)(2,1)S(1)}, bf16[128,768]{1,0:T(8,128)(2,1)}, u32[]{:S(2)}) copy-start(bf16[128,768]{1,0:T(8,128)(2,1)} %copy-done.7) | copy-start | bytes 589828
  128.6 5.4 %collective-permute-start.10 = (bf16[160,1152]{1,0:T(8,128)(2,1)S(1)}, bf16[160,1152]{1,0:T(8,128)(2,1)S(1)}, u32[]{:S(2)}, u32[]{:S(2)}) collective-permute-start(bf16[160,1152]{1,0:T(8,128)(2,1)S(1)} %get-tuple-element.52), channel_id=1, source_target_pairs={{0,1},{1,0},{2,3},{3,2},{4,5},{5,4},{6,7},{7,6},{8,9},{9,8},{10,11... | collective-permute-start | bytes 1105928 | tf_op jit(solution)/shard_map/ppermute | solution.py:341
  (3 other events, 2.0 us)
